TPU v7x, 512 devices: a whole 4x4x16 slice. The times are simulated.
512 devices in a mesh: dp: 64 (over x, y, z_lo), tensor: 8 (over z_hi, core).
Axes of the slice: x: 4, y: 4, z: 16 (z_hi: 4, z_lo: 4; z = z_hi * 4 + z_lo), core: 2. Of those that a mesh axis runs over, the one named last changes fastest.
Arguments:
- normed: bfloat16 [4096, 1280], P('dp'), may hold values from -6 to 6
- residual_in: bfloat16 [4096, 1280], P('dp'), may hold values from -6 to 6
- w_up: bfloat16 [1280, 5120], P('dp', 'tensor'), may hold values from -0.15625 to 0.15625
- w_down: bfloat16 [5120, 1280], P('tensor', 'dp'), may hold values from -0.15625 to 0.15625
- final_gain: float32 [1280], replicated, may hold values from 0.1 to 1.9
- head_cols: bfloat16 [1280, 16], replicated, may hold values from -4 to 4
- sub_inputs: int32 [8192], P('tensor'), may hold values from 0 to 1279
- sub_hidden: int32 [8192], P('tensor'), may hold values from 0 to 5119, as said below
- panels: bfloat16 [2, 256, 8192], P(None, 'dp', 'tensor'), may hold values from -0.1001 to 0.1001, as said below
- inverses: bfloat16 [2, 256, 256], replicated, may hold values from -0.1001 to 2, as said below
Outputs:
- whitened: bfloat16 [4096, 16, 8192], P('dp', None, 'tensor')
Inputs may be any that keep to these rules, and one draw needn't show every extreme that they name: `sub_hidden`: window rows t * 1024 to (t + 1) * 1024 - 1 name hidden units t * 640 to (t + 1) * 640 - 1. `panels`: entry [q, c, r] is zero for r < (q + 1) * 256. `inverses`: each block is lower triangular with a positive diagonal.
All inputs are finite; a program needn't handle non-finite values.
Results may differ from a plain program's by a relative error of at most 0.0069.
Values may be sent and summed in bfloat16 or wider, within the bound.
No kernel may reach another device: no remote copies, remote signals or barrier semaphores. Data moves between devices by JAX's collectives and lax.ppermute only.
A program may use at most 64 MiB of HBM per device.

v0:
```python
import jax
import jax.numpy as jnp
from jax import lax
from jax.sharding import PartitionSpec as P


def from_root(shard, axis, root):
    mine = lax.axis_index(axis) == root
    return lax.psum(jnp.where(mine, shard, jnp.zeros_like(shard)), axis)


def gelu_parts(values):
    normal_cdf = 0.5 * (1.0 + jax.scipy.special.erf(values * 0.7071067811865476))
    slope = normal_cdf + values * jnp.exp(-0.5 * values * values) * 0.3989422804014327
    return (values * normal_cdf, slope)


def logit_adjoint(block_result, final_gain, head_cols):
    mean_x = jnp.mean(block_result, axis=1, keepdims=True)
    centred_rows = block_result - mean_x
    inverse_deviation = lax.rsqrt(
        jnp.mean(centred_rows * centred_rows, axis=1, keepdims=True) + 1e-06
    )
    normalized_input = centred_rows * inverse_deviation
    head_scaled_rows = final_gain[:, None] * head_cols.astype(jnp.float32)
    head_average = jnp.mean(head_scaled_rows, axis=0)
    project_rows = (
        jnp.dot(normalized_input, head_scaled_rows, precision=lax.Precision.HIGHEST)
        / block_result.shape[1]
    )
    return inverse_deviation[:, :, None] * (
        head_scaled_rows.T[None, :, :]
        - head_average[None, :, None]
        - normalized_input[:, None, :] * project_rows[:, :, None]
    )


def apply_inverse(block, inverse):
    return lax.dot_general(
        block, inverse, (((1,), (1,)), ((), ())), preferred_element_type=jnp.float32
    )


def solve_panel(block, inverse):
    solved = apply_inverse(block, inverse).astype(jnp.bfloat16)
    return from_root(solved, "tensor", 0)


def body(
    normed,
    residual_in,
    w_up,
    w_down,
    final_gain,
    head_cols,
    sub_inputs,
    sub_hidden,
    panels,
    inverses,
):
    images = normed.shape[0]
    width = normed.shape[1]
    hidden_dev = w_up.shape[1]
    logits = head_cols.shape[1]
    panel = inverses.shape[1]
    rows_dev = sub_inputs.shape[0]
    tensor_rank = lax.axis_index("tensor")
    up_pre = jnp.dot(
        normed, lax.all_gather(w_up, "dp", axis=0, tiled=True), preferred_element_type=jnp.float32
    )
    activ, slope = gelu_parts(up_pre)
    hidden = activ.astype(jnp.bfloat16)
    down_full = lax.all_gather(w_down, "dp", axis=1, tiled=True)
    partial_out = jnp.dot(hidden, down_full, preferred_element_type=jnp.float32)
    block_result = residual_in.astype(jnp.float32) + lax.psum(partial_out, "tensor")
    adjoint = logit_adjoint(block_result, final_gain, head_cols).astype(jnp.bfloat16)
    back = lax.dot_general(
        adjoint.reshape(images * logits, width),
        down_full,
        (((1,), (1,)), ((), ())),
        preferred_element_type=jnp.float32,
    )
    delta = back.reshape(images, logits, hidden_dev) * slope[:, None, :]
    local_hidden = sub_hidden - tensor_rank * hidden_dev
    picked = jnp.take(normed, sub_inputs, axis=1).astype(jnp.float32)
    jac = (picked[:, None, :] * jnp.take(delta, local_hidden, axis=2)).astype(jnp.bfloat16)
    jac = jac.reshape(images * logits, rows_dev)
    first = solve_panel(jac[:, :panel], inverses[0])
    solved = first
    carry = jnp.dot(
        solved,
        lax.all_gather(panels[0], "dp", axis=0, tiled=True),
        preferred_element_type=jnp.float32,
    )
    second_in = (
        jac[:, panel : 2 * panel].astype(jnp.float32) - carry[:, panel : 2 * panel]
    ).astype(jnp.bfloat16)
    second = solve_panel(second_in, inverses[1])
    solved = second
    update = carry + jnp.dot(
        solved,
        lax.all_gather(panels[1], "dp", axis=0, tiled=True),
        preferred_element_type=jnp.float32,
    )
    below = (jac.astype(jnp.float32) - update).astype(jnp.bfloat16)
    solved_rows = jnp.concatenate([first, second, below[:, 2 * panel :]], axis=1)
    result = jnp.where(tensor_rank == 0, solved_rows, below)
    return result.reshape(images, logits, rows_dev)


def solution(mesh):
    in_specs = (
        P("dp", None),
        P("dp", None),
        P("dp", "tensor"),
        P("tensor", "dp"),
        P(),
        P(),
        P("tensor"),
        P("tensor"),
        P(None, "dp", "tensor"),
        P(),
    )
    out_specs = P("dp", None, "tensor")
    return jax.shard_map(body, mesh=mesh, in_specs=in_specs, out_specs=out_specs, check_vma=False)
```

profile of v0, /device:TPU:32, one launch (start us, length us, event | category | flops | bytes accessed | tf_op | source)
XLA Modules:
  0.0 1264.1 jit_solution(2242103107041094399)
XLA Ops:
  8.1 1.1 copy.24
  9.9 3.2 gather_fusion
  15.7 351.4 %all-gather.7.cloned.1.call-done = bf16[64,20,640]{2,1,0:T(8,128)(2,1)} async-done(((bf16[1,20,640]{2,1,0:T(8,128)(2,1)}), bf16[64,20,640]{2,1,0:T(8,128)(2,1)}) %all-gather.7.cloned.1.call-update) | async-done | bytes 1638416 | tf_op jit(solution)/shard_map/all_gather | solution.py:69
  367.2 2.4 reshape.98
  370.1 351.7 %all-gather.9.cloned.1.call-done = bf16[64,20,640]{2,1,0:T(8,128)(2,1)} async-done(((bf16[1,20,640]{2,1,0:T(8,128)(2,1)}), bf16[64,20,640]{2,1,0:T(8,128)(2,1)}) %all-gather.9.cloned.1.call-update) | async-done | bytes 1638416 | tf_op jit(solution)/shard_map/all_gather | solution.py:73
  721.8 3.7 reshape.100
  725.5 2.8 fusion.28
  728.6 1.3 reshape.101
  729.9 94.9 %all-reduce.4.cloned.1.call-done = f32[64,1280]{1,0:T(8,128)} async-done(((f32[64,1280]{1,0:T(8,128)}), f32[64,1280]{1,0:T(8,128)}) %all-reduce.4.cloned.1.call-update) | async-done | bytes 327696 | tf_op jit(solution)/shard_map/psum | solution.py:75
  824.9 1.1 fusion.27
  826.0 1.2 multiply_reduce_fusion
  828.7 3.8 fusion.7
  832.5 5.4 copy.27
  837.9 12.2 gather_fusion.1
  850.0 7.6 copy.28
  857.7 2.9 fusion.1
  860.6 1.1 fusion.8
  861.9 190.7 %all-gather = bf16[1,256,1024]{2,0,1:T(2,128)(2,1)S(1)} all-gather(bf16[1,4,1024]{2,0,1:T(2,128)(2,1)S(1)} %copy.33), channel_id=2, replica_groups=mesh['dp'=64,'tensor'=8] {'dp'}, dimensions={1}, use_global_device_ids=true | all-gather | bytes 532480 | tf_op jit(solution)/shard_map/all_gather | solution.py:92
  1052.6 1.8 fusion.16
  1054.4 1.9 copy-done
  1056.3 1.2 fusion.9
  1057.5 194.6 %all-gather.1 = bf16[1,256,1024]{2,0,1:T(2,128)(2,1)S(1)} all-gather(bf16[1,4,1024]{2,0,1:T(2,128)(2,1)S(1)} %copy.34), channel_id=3, replica_groups=mesh['dp'=64,'tensor'=8] {'dp'}, dimensions={1}, use_global_device_ids=true | all-gather | bytes 532480 | tf_op jit(solution)/shard_map/all_gather | solution.py:102
  1252.1 3.2 subtract_convert_fusion
  1255.5 2.1 maximum_select_fusion
  (52 shorter events, 7.2 us)
Async XLA Ops:
  6.5 8.4 copy-start.6
  6.5 360.6 %all-gather.7.cloned.1.call-start = ((), (), s32[]{:S(2)}) async-start(), calls=%async_computation.3 | async-start | bytes 1996800 | tf_op jit(solution)/shard_map/all_gather | solution.py:69
  7.3 714.5 %all-gather.9.cloned.1.call-start = ((), (), s32[]{:S(2)}) async-start(), calls=%async_computation.4 | async-start | bytes 1996800 | tf_op jit(solution)/shard_map/all_gather | solution.py:73
  8.0 816.9 %all-reduce.4.cloned.1.call-start = ((), (), s32[]{:S(2)}) async-start(), calls=%async_computation | async-start | bytes 655360 | tf_op jit(solution)/shard_map/psum | solution.py:75
  9.9 359.7 %copy-start.5 = (bf16[64,1280]{1,0:T(8,128)(2,1)S(1)}, bf16[64,1280]{1,0:T(8,128)(2,1)}, u32[]{:S(2)}) copy-start(bf16[64,1280]{1,0:T(8,128)(2,1)} %param.10) | copy-start | bytes 491524
  370.0 358.3 %copy-start.10 = (s32[1024]{0:T(1024)S(1)}, s32[1024]{0:T(1024)}, u32[]{:S(2)}) copy-start(s32[1024]{0:T(1024)} %param.17) | copy-start | bytes 12292
  721.8 6.8 copy-start.1
  728.2 96.6 %copy-start.4 = (bf16[64,1280]{1,0:T(8,128)(2,1)S(1)}, bf16[64,1280]{1,0:T(8,128)(2,1)}, u32[]{:S(2)}) copy-start(bf16[64,1280]{1,0:T(8,128)(2,1)} %param.11) | copy-start | bytes 491524
  728.3 324.3 %all-reduce.6.cloned.1.call-start = ((), (), s32[]{:S(2)}) async-start(), calls=%async_computation.1 | async-start | bytes 1048576 | tf_op jit(solution)/shard_map/psum | solution.py:9
  728.6 99.7 %copy-start.7 = (f32[1280]{0:T(1024)S(1)}, f32[1280]{0:T(1024)}, u32[]{:S(2)}) copy-start(f32[1280]{0:T(1024)} %param.14) | copy-start | bytes 15364
  857.7 2.9 copy-start.8
  857.7 4.1 copy-start.9
  861.8 390.4 %all-reduce.8.cloned.1.call-start = ((), (), s32[]{:S(2)}) async-start(), calls=%async_computation.2 | async-start | bytes 1048576 | tf_op jit(solution)/shard_map/psum | solution.py:9
  1054.4 1.9 copy-start
  1252.1 3.3 copy-start.2
  1252.1 3.3 copy-start.3
Sparse Core Ops, SparseCore 0:
  9.4 357.6 all-gather.6
  369.2 352.4 all-gather.8
  728.4 96.4 all-reduce.3
  861.9 97.4 all-reduce.5
  1057.6 98.0 all-reduce.7
where the time goes:
time: 1260 us
  waiting for transfers between devices  800 us (63%)
  blocking collectives  385 us (31%)
  local copies, waits for them, and re-layouts  39.4 us (3%)
  matrix products  14.6 us (1%)
  between operations  13.4 us (1%)
    all_gather x1, waiting for transfers between devices, body(): down_full = lax.all_gather(w_down, 'dp', axis=1, tiled=True)  352 us
    all_gather x1, waiting for transfers between devices, body(): lax.all_gather(w_up, 'dp', axis=0, tiled=True)  351 us
    all_gather x1, blocking collectives, body(): lax.all_gather(panels[1], 'dp', axis=0, tiled=True)  195 us
    all_gather x1, blocking collectives, body(): lax.all_gather(panels[0], 'dp', axis=0, tiled=True)  191 us
    psum x1, waiting for transfers between devices, body(): lax.psum(partial_out, 'tensor')  94.9 us
  transfers between devices with their start and end apart: 5, of which 3 were waited for; matrix products, arithmetic and copies ran while one was open for 1% of the time, Pallas kernels for 0%

commit v1 on v0

v1 whole, which is shorter than its diff:
```python
import jax
import jax.numpy as jnp
from jax import lax
from jax.experimental import pallas as pl
from jax.experimental.pallas import tpu as pltpu
from jax.sharding import Mesh, PartitionSpec as P

DP = ("x", "y", "zl")
TENSOR = ("zh", "c")
F32 = jnp.float32
BF16 = jnp.bfloat16
STEP = 16


def gelu_parts(values):
    normal_cdf = 0.5 * (1.0 + jax.scipy.special.erf(values * 0.7071067811865476))
    slope = normal_cdf + values * jnp.exp(-0.5 * values * values) * 0.3989422804014327
    return (values * normal_cdf, slope)


def swap_core(values):
    return lax.ppermute(values, "c", [(0, 1), (1, 0)])


def gather_by_sends(shard, axis, count):
    spread = jnp.broadcast_to(shard[None], (count,) + shard.shape)
    return lax.all_to_all(spread, axis, 0, 0)


def ring_gather(shard, axis, count):
    ahead = [shard] + [
        lax.ppermute(shard, axis, [(i, (i - k) % count) for i in range(count)]) for k in range(1, count)
    ]
    twice = jnp.concatenate([part[None] for part in ahead + ahead[:-1]], axis=0)
    start = (count - lax.axis_index(axis)) % count
    return lax.dynamic_slice_in_dim(twice, start, count, 0)


def split2(values):
    high = lax.reduce_precision(values, 8, 7)
    return high.astype(BF16), (values - high).astype(BF16)


def dot32(lhs, rhs):
    return jnp.dot(lhs, rhs, preferred_element_type=F32)


def dot_t(lhs, rhs):
    return lax.dot_general(lhs, rhs, (((1,), (1,)), ((), ())), preferred_element_type=F32)


def dot_split(values, rhs):
    rows = values.shape[0]
    both = dot32(jnp.concatenate(split2(values), axis=0), rhs)
    return both[:rows] + both[rows:]


def one_hot(index, depth):
    return (lax.broadcasted_iota(jnp.int32, (depth, index.shape[0]), 0) == index[None, :]).astype(BF16)


def middle_kernel(
    flag_ref, mine_ref, theirs_ref, normed_ref, picked_ref, head_ref, down_ref, extra_ref, inv_ref, share_ref, own_ref, mix_ref, up0, down0
):
    images, width = normed_ref.shape
    rows_dev = down_ref.shape[1]
    half = mix_ref.shape[1]
    logits = head_ref.shape[0] // 4
    places, sub = extra_ref.shape[0], extra_ref.shape[1]
    parts = width // (places * sub)
    at = 2 * rows_dev
    for place in range(places):
        for b in range(parts):
            row = (place * parts + b) * sub
            up0[row : row + sub, :] = extra_ref[place, :, at + b * half : at + (b + 1) * half]
            low = at + (parts + b) * half
            down0[row : row + sub, :] = extra_ref[place, :, low : low + half]
    _, slope0 = gelu_parts(dot32(normed_ref[...], up0[...]))
    mix_ref[:images, :] = slope0 * picked_ref[...]

    first_core = flag_ref[1] == 0
    mine, theirs = mine_ref[...], theirs_ref[...]
    block = jnp.concatenate([jnp.where(first_core, mine, theirs), jnp.where(first_core, theirs, mine)], axis=0)
    centred = block - jnp.mean(block, axis=1, keepdims=True)
    inv_std = lax.rsqrt(jnp.mean(centred * centred, axis=1, keepdims=True) + 1e-06)
    xhat = centred * inv_std
    inv_ref[...] = inv_std
    high = xhat.astype(BF16)
    low = (xhat - high.astype(F32)).astype(BF16)
    head = head_ref[...]
    both = jnp.concatenate([high, low], axis=0)
    share = dot_t(both, head[2 * logits :])
    share = share[:images] + share[images:]
    share_ref[...] = (share[:, :logits] + share[:, logits:]) / width
    lhs = jnp.concatenate([both, head[: 2 * logits]], axis=0)
    for rhs, out, base in ((down_ref, own_ref, 0), (down0, mix_ref, images)):
        product = dot32(lhs, rhs[...])
        out[base : base + images, :] = product[:images] + product[images : 2 * images]
        tail = product[2 * images :]
        out[base + images : base + images + logits, :] = tail[:logits] + tail[logits:]


def last_kernel(flag_ref, gain_ref, inv_ref, share_ref, own_ref, mine_ref, theirs_ref, inverse_ref, extra_ref, out_ref):
    images = gain_ref.shape[0]
    logits = share_ref.shape[1]
    rows_dev = gain_ref.shape[1]
    panel = inverse_ref.shape[1]
    first_image = pl.multiple_of(pl.program_id(0) * STEP, STEP)
    here = pl.ds(first_image, STEP)
    inv_std = inv_ref[here, :]
    diagonal = lax.broadcasted_iota(jnp.int32, (1, logits, logits), 1) == lax.broadcasted_iota(
        jnp.int32, (1, logits, logits), 2
    )
    share = jnp.sum(jnp.where(diagonal, share_ref[here, :][:, None, :], 0.0), axis=2, keepdims=True)

    def jacobian(gain, along, head):
        scale = gain * inv_std
        values = scale[:, None, :] * (head[None] - share * along[:, None, :])
        return values.reshape(STEP * logits, values.shape[2])

    def solved_side(side):
        is_mine = flag_ref[1] == side
        gain, along, head = (
            jnp.where(is_mine, mine_ref[rows, :], theirs_ref[rows, :])
            for rows in (here, pl.ds(images + first_image, STEP), slice(2 * images, 2 * images + logits))
        )
        return jacobian(gain, along, head)

    def inverted(values, inverse):
        high = values.astype(BF16)
        low = (values - high.astype(F32)).astype(BF16)
        return (dot_t(high, inverse) + dot_t(low, inverse)).astype(BF16)

    first = inverted(solved_side(0), inverse_ref[0])
    at = extra_ref.shape[2] - panel
    panel_01 = extra_ref[:, :, at:].reshape(panel, panel)
    second = inverted(solved_side(1) - dot32(first, panel_01), inverse_ref[1])
    own = jacobian(gain_ref[here, :], own_ref[here, :], own_ref[images : images + logits, :])
    panel_0 = extra_ref[:, :, :rows_dev].reshape(panel, rows_dev)
    panel_1 = extra_ref[:, :, rows_dev : 2 * rows_dev].reshape(panel, rows_dev)
    below = (own - (dot32(first, panel_0) + dot32(second, panel_1))).astype(BF16)
    out_ref[...] = below.reshape(out_ref.shape)

    @pl.when(flag_ref[0] == 1)
    def _():
        out_ref[:, :, :panel] = first.reshape(STEP, logits, panel)
        out_ref[:, :, panel : 2 * panel] = second.reshape(STEP, logits, panel)


def body(normed, residual_in, w_up, w_down, final_gain, head_cols, sub_inputs, sub_hidden, panels, inverses):
    images, width = normed.shape
    own, hidden_dev = w_up.shape
    logits = head_cols.shape[1]
    panel = inverses.shape[1]
    panel_dev = panels.shape[1]
    rows_dev = sub_inputs.shape[0]
    z_hi, core = lax.axis_index("zh"), lax.axis_index("c")
    rank = z_hi * 2 + core
    local_hidden = sub_hidden - rank * hidden_dev
    half = panel

    both = jnp.concatenate([w_up, w_down.T], axis=0)
    line = gather_by_sends(both, "zl", 4)
    line = jnp.concatenate(
        [line[:, :own].reshape(4 * own, hidden_dev), line[:, own:].reshape(4 * own, hidden_dev)], axis=0
    )
    plane = gather_by_sends(line, ("x", "y"), 16)
    up_full = plane[:, : 4 * own].reshape(width, hidden_dev)
    down_t = plane[:, 4 * own :].reshape(width, hidden_dev)

    later, hidden_first, inputs_first, panels_later, _ = lax.optimization_barrier(
        (both, local_hidden[: 2 * panel], sub_inputs[: 2 * panel], panels, line)
    )
    chosen = dot32(later, one_hot(hidden_first, hidden_dev)).astype(BF16)
    coded = jnp.stack([inputs_first // 128, inputs_first % 128]).astype(BF16)
    block01 = panels_later[0][:, panel : 2 * panel]
    sides = [
        jnp.concatenate([chosen[:, s * half : (s + 1) * half], block01, coded[:, s * half : (s + 1) * half]], axis=0)
        for s in range(2)
    ]
    payload = jnp.where(core == 0, sides[0], lax.ppermute(sides[1], "c", [(0, 1)]))
    sent = [lax.ppermute(payload, "zh", [(0, k)]) for k in (1, 2, 3)]
    payload = jnp.where(z_hi == 0, payload, sent[0] + sent[1] + sent[2])

    narrow = jnp.concatenate(
        [panels_later.reshape(2 * panel_dev * (rows_dev // half), half), payload[: 2 * own + panel_dev]], axis=0
    )
    narrow = ring_gather(narrow, "zl", 4)
    count = 2 * panel_dev * (rows_dev // half)
    line_panels = narrow[:, :count].reshape(4, 2, panel_dev, rows_dev)
    narrow = narrow[:, count:]
    chosen_up = narrow[:, :own].reshape(5, 16, half)
    chosen_down = narrow[:, own : 2 * own].reshape(5, 16, half)
    extra = jnp.concatenate(
        [line_panels[:, q].reshape(16, rows_dev) for q in range(2)]
        + [chosen_up[b] for b in range(5)]
        + [chosen_down[b] for b in range(5)]
        + [narrow[:, 2 * own :].reshape(16, half)],
        axis=1,
    )

    up_pre = dot32(normed, up_full)
    activ, slope = gelu_parts(up_pre)
    partial_out = dot_t(activ.astype(BF16), down_t)
    kept = lax.dynamic_slice_in_dim(partial_out, core * (images // 2), images // 2, 0)
    given = lax.dynamic_slice_in_dim(partial_out, (1 - core) * (images // 2), images // 2, 0)
    pair = kept + swap_core(given)
    peers = [lax.ppermute(pair, "zh", [(i, (i + k) % 4) for i in range(4)]) for k in (2, 1, 3)]

    spread = jnp.broadcast_to(extra[None], (16,) + extra.shape)
    spread, _ = lax.optimization_barrier((spread, plane[:, :1, :128]))
    extra = lax.all_to_all(spread, ("x", "y"), 0, 0)

    pick_own = one_hot(local_hidden, hidden_dev)
    down_own = dot32(down_t, pick_own).astype(BF16)
    gain_own = dot_split(slope, pick_own) * dot32(normed, one_hot(sub_inputs, width))
    index = payload[2 * own + panel_dev :].astype(jnp.int32)
    picked = dot32(normed, one_hot(index[0] * 128 + index[1], width))
    head = final_gain[:, None] * head_cols.astype(F32)
    centred_head = head - jnp.mean(head, axis=0)
    head_parts = jnp.concatenate(split2(centred_head.T) + split2(head.T), axis=0)

    mine = lax.dynamic_slice_in_dim(residual_in, core * (images // 2), images // 2, 0)
    block = mine.astype(F32) + ((pair + peers[0]) + (peers[1] + peers[2]))
    block_pair = swap_core(block)
    flag = jnp.stack([jnp.where(rank == 0, 1, 0), core]).astype(jnp.int32)

    vmem = pl.BlockSpec(memory_space=pltpu.VMEM)
    inv_std, share, own_products, mix = pl.pallas_call(
        middle_kernel,
        out_shape=(
            jax.ShapeDtypeStruct((images, 1), F32),
            jax.ShapeDtypeStruct((images, logits), F32),
            jax.ShapeDtypeStruct((images + logits, rows_dev), F32),
            jax.ShapeDtypeStruct((2 * images + logits, half), F32),
        ),
        in_specs=[pl.BlockSpec(memory_space=pltpu.SMEM)] + [vmem] * 7,
        out_specs=(vmem,) * 4,
        scratch_shapes=[pltpu.VMEM((width, half), BF16), pltpu.VMEM((width, half), BF16)],
        name="middle",
    )(flag, block, block_pair, normed, picked, head_parts, down_own, extra)
    mix_pair = swap_core(mix)
    return pl.pallas_call(
        last_kernel,
        grid=(images // STEP,),
        out_shape=jax.ShapeDtypeStruct((images, logits, rows_dev), BF16),
        in_specs=[pl.BlockSpec(memory_space=pltpu.SMEM)] + [vmem] * 8,
        out_specs=pl.BlockSpec((STEP, logits, rows_dev), lambda i: (i, 0, 0)),
        name="last",
    )(flag, gain_own, inv_std, share, own_products, mix, mix_pair, inverses, extra)


def solution(mesh):
    fine = Mesh(mesh.devices.reshape(4, 4, 4, 4, 2), ("x", "y", "zl", "zh", "c"))
    in_specs = (
        P(DP, None),
        P(DP, None),
        P(DP, TENSOR),
        P(TENSOR, DP),
        P(),
        P(),
        P(TENSOR),
        P(TENSOR),
        P(None, DP, TENSOR),
        P(),
    )
    out_specs = P(DP, None, TENSOR)

    return jax.shard_map(body, mesh=fine, in_specs=in_specs, out_specs=out_specs, check_vma=False)
```

time: 1260 us -> 166 us (0.13)
  the two profiles are of different devices: /device:TPU:32 before, /device:TPU:99 now
where the time goes in v1:
time: 166 us; the launch traced here: 165 us
  starting transfers between devices  68 us (41%)
  waiting for transfers between devices  58.3 us (35%)
  local copies, waits for them, and re-layouts  13.5 us (8%)
  Pallas kernels  11.8 us (7%)
  matrix products  8.44 us (5%)
  other arithmetic  4.68 us (3%)
    all_to_all x2, waiting for transfers between devices, gather_by_sends(): return lax.all_to_all(spread, axis, 0, 0)  28.3 us
    ppermute x3, waiting for transfers between devices, body(): lax.ppermute(pair, 'zh', [(i, (i + k) % 4) for i in range(4)])  25.8 us
    ppermute x3, starting transfers between devices, body(): sent = [lax.ppermute(payload, 'zh', [(0, k)]) for k in (1, 2, 3)]  14.5 us
    ppermute x3, starting transfers between devices, body(): lax.ppermute(pair, 'zh', [(i, (i + k) % 4) for i in range(4)])  11.8 us
    all_to_all x2, starting transfers between devices, gather_by_sends(): return lax.all_to_all(spread, axis, 0, 0)  11.4 us
    all_to_all x1, starting transfers between devices, body(): extra = lax.all_to_all(spread, ('x', 'y'), 0, 0)  11.4 us
    ppermute x3, starting transfers between devices, ring_gather(): lax.ppermute(shard, axis, [(i, (i - k) % count) for i in range(count)])  9.18 us
    ppermute x3, starting transfers between devices, swap_core(): return lax.ppermute(values, 'c', [(0, 1), (1, 0)])  8.38 us
  transfers between devices with their start and end apart: 16, of which 7 were waited for; matrix products, arithmetic and copies ran while one was open for 12% of the time, Pallas kernels for 0%

profile of v1, /device:TPU:99, one launch (start us, length us, event | category | flops | bytes accessed | tf_op | source)
XLA Modules:
  0.0 165.4 jit_solution(1609971029030636954)
XLA Ops:
  1.5 4.5 %all-to-all-start = ((bf16[4,40,640]{2,1,0:T(8,128)(2,1)}), bf16[4,40,640]{2,1,0:T(8,128)(2,1)S(1)}, u32[]{:S(2)}, u32[]{:S(2)}) async-start(bf16[4,40,640]{2,1,0:T(8,128)(2,1)} %broadcast_in_dim.14), calls=%async_computation | async-start | bytes 409600 | tf_op jit(solution)/shard_map/all_to_all | solution.py:27
  9.2 2.1 %all-to-all-done = bf16[4,40,640]{2,1,0:T(8,128)(2,1)S(1)} async-done(((bf16[4,40,640]{2,1,0:T(8,128)(2,1)}), bf16[4,40,640]{2,1,0:T(8,128)(2,1)S(1)}, u32[]{:S(2)}, u32[]{:S(2)}) %all-to-all-start) | async-done | bytes 204832 | tf_op jit(solution)/shard_map/all_to_all | solution.py:27
  15.2 10.2 %collective-permute-start.8 = (bf16[46,256]{1,0:T(8,128)(2,1)S(1)}, bf16[46,256]{1,0:T(8,128)(2,1)S(1)}, u32[]{:S(2)}, u32[]{:S(2)}) collective-permute-start(bf16[46,256]{1,0:T(8,128)(2,1)S(1)} %fusion.27), channel_id=1, source_target_pairs={{0,6},{1,7},{8,14},{9,15},{16,22},{17,23},{24,30},{25,31},{32,38},... | collective-permute-start | bytes 70664 | tf_op jit(solution)/shard_map/ppermute | solution.py:182
  26.6 3.0 %collective-permute-start.7 = (bf16[46,256]{1,0:T(8,128)(2,1)S(1)}, bf16[46,256]{1,0:T(8,128)(2,1)S(1)}, u32[]{:S(2)}, u32[]{:S(2)}) collective-permute-start(bf16[46,256]{1,0:T(8,128)(2,1)S(1)} %fusion.27), channel_id=1, source_target_pairs={{0,4},{1,5},{8,12},{9,13},{16,20},{17,21},{24,28},{25,29},{32,36},... | collective-permute-start | bytes 70664 | tf_op jit(solution)/shard_map/ppermute | solution.py:182
  30.3 2.0 %broadcast_in_dim.15 = bf16[16,160,640]{2,1,0:T(8,128)(2,1)} broadcast(bf16[160,640]{1,0:T(8,128)(2,1)S(1)} %constant_dynamic-update-slice_fusion), dimensions={1,2} | broadcast | bytes 3481600 | tf_op jit(solution)/shard_map/broadcast_in_dim | solution.py:26
  32.3 6.9 %all-to-all-start.1 = ((bf16[16,160,640]{2,1,0:T(8,128)(2,1)}), bf16[16,160,640]{2,1,0:T(8,128)(2,1)S(1)}, u32[]{:S(2)}, u32[]{:S(2)}) async-start(bf16[16,160,640]{2,1,0:T(8,128)(2,1)} %broadcast_in_dim.15), calls=%async_computation.1 | async-start | bytes 6553600 | tf_op jit(solution)/shard_map/all_to_all | solution.py:27
  39.2 1.9 %collective-permute-start.9 = (bf16[76,256]{1,0:T(8,128)(2,1)S(1)}, bf16[76,256]{1,0:T(8,128)(2,1)S(1)}, u32[]{:S(2)}, u32[]{:S(2)}) collective-permute-start(bf16[76,256]{1,0:T(8,128)(2,1)S(1)} %pad_maximum_fusion.2), channel_id=1, source_target_pairs={{0,24},{8,0},{16,8},{24,16},{1,25},{9,1},{17,9},{25,17},{2,26},{10... | collective-permute-start | bytes 116744 | tf_op jit(solution)/shard_map/ppermute | solution.py:32
  41.2 4.3 %collective-permute-start.10 = (bf16[76,256]{1,0:T(8,128)(2,1)S(1)}, bf16[76,256]{1,0:T(8,128)(2,1)S(1)}, u32[]{:S(2)}, u32[]{:S(2)}) collective-permute-start(bf16[76,256]{1,0:T(8,128)(2,1)S(1)} %pad_maximum_fusion.2), channel_id=1, source_target_pairs={{0,16},{8,24},{16,0},{24,8},{1,17},{9,25},{17,1},{25,9},{2,18},{10... | collective-permute-start | bytes 116744 | tf_op jit(solution)/shard_map/ppermute | solution.py:32
  45.5 3.0 %collective-permute-start.11 = (bf16[76,256]{1,0:T(8,128)(2,1)S(1)}, bf16[76,256]{1,0:T(8,128)(2,1)S(1)}, u32[]{:S(2)}, u32[]{:S(2)}) collective-permute-start(bf16[76,256]{1,0:T(8,128)(2,1)S(1)} %pad_maximum_fusion.2), channel_id=1, source_target_pairs={{0,8},{8,16},{16,24},{24,0},{1,9},{9,17},{17,25},{25,1},{2,10},{10... | collective-permute-start | bytes 116744 | tf_op jit(solution)/shard_map/ppermute | solution.py:32
  48.5 2.0 %collective-permute-done.11 = bf16[76,256]{1,0:T(8,128)(2,1)S(1)} collective-permute-done((bf16[76,256]{1,0:T(8,128)(2,1)S(1)}, bf16[76,256]{1,0:T(8,128)(2,1)S(1)}, u32[]{:S(2)}, u32[]{:S(2)}) %collective-permute-start.11) | collective-permute-done | bytes 38944 | tf_op jit(solution)/shard_map/ppermute | solution.py:32
  54.8 26.2 %all-to-all-done.1 = bf16[16,160,640]{2,1,0:T(8,128)(2,1)S(1)} async-done(((bf16[16,160,640]{2,1,0:T(8,128)(2,1)}), bf16[16,160,640]{2,1,0:T(8,128)(2,1)S(1)}, u32[]{:S(2)}, u32[]{:S(2)}) %all-to-all-start.1) | async-done | bytes 3276832 | tf_op jit(solution)/shard_map/all_to_all | solution.py:27
  82.7 11.4 %all-to-all-start.2 = ((bf16[16,16,4864]{2,1,0:T(8,128)(2,1)}), bf16[16,16,4864]{2,1,0:T(8,128)(2,1)S(1)}, u32[]{:S(2)}, u32[]{:S(2)}) async-start(bf16[16,16,4864]{2,1,0:T(8,128)(2,1)} %broadcast_in_dim.20), calls=%async_computation.2 | async-start | bytes 4980736 | tf_op jit(solution)/shard_map/all_to_all | solution.py:212
  94.1 2.3 %fusion.34 = (bf16[16,80,640]{2,1,0:T(8,128)(2,1)S(1)}, bf16[16,80,640]{2,1,0:T(8,128)(2,1)S(1)}) fusion(bf16[16,160,640]{2,1,0:T(8,128)(2,1)} %copy-done.1), kind=kLoop, calls=%fused_computation.113 | loop fusion | bytes 6553600 | tf_op jit(solution)/shard_map/slice | solution.py:169
  97.5 4.1 %collective-permute-start = (f32[32,1280]{1,0:T(8,128)S(1)}, f32[32,1280]{1,0:T(8,128)S(1)}, u32[]{:S(2)}, u32[]{:S(2)}) collective-permute-start(f32[32,1280]{1,0:T(8,128)S(1)} %constant_dynamic-slice_fusion.4), channel_id=1, source_target_pairs={{0,1},{1,0},{2,3},{3,2},{4,5},{5,4},{6,7},{7,6},{8,9},{9,8},{10,11... | collective-permute-start | bytes 491528 | tf_op jit(solution)/shard_map/ppermute | solution.py:22
  102.6 2.1 %collective-permute-start.2 = (f32[32,1280]{1,0:T(8,128)S(1)}, f32[32,1280]{1,0:T(8,128)S(1)}, u32[]{:S(2)}, u32[]{:S(2)}) collective-permute-start(f32[32,1280]{1,0:T(8,128)S(1)} %dynamic-slice_add_fusion), channel_id=1, source_target_pairs={{0,2},{2,4},{4,6},{6,0},{1,3},{3,5},{5,7},{7,1},{8,10},{10,12},{12... | collective-permute-start | bytes 491528 | tf_op jit(solution)/shard_map/ppermute | solution.py:208
  104.6 7.3 %collective-permute-start.3 = (f32[32,1280]{1,0:T(8,128)S(1)}, f32[32,1280]{1,0:T(8,128)S(1)}, u32[]{:S(2)}, u32[]{:S(2)}) collective-permute-start(f32[32,1280]{1,0:T(8,128)S(1)} %dynamic-slice_add_fusion), channel_id=1, source_target_pairs={{0,6},{2,0},{4,2},{6,4},{1,7},{3,1},{5,3},{7,5},{8,14},{10,8},{12,... | collective-permute-start | bytes 491528 | tf_op jit(solution)/shard_map/ppermute | solution.py:208
  111.9 2.5 %collective-permute-start.1 = (f32[32,1280]{1,0:T(8,128)S(1)}, f32[32,1280]{1,0:T(8,128)S(1)}, u32[]{:S(2)}, u32[]{:S(2)}) collective-permute-start(f32[32,1280]{1,0:T(8,128)S(1)} %dynamic-slice_add_fusion), channel_id=1, source_target_pairs={{0,4},{2,6},{4,0},{6,2},{1,5},{3,7},{5,1},{7,3},{8,12},{10,14},{12... | collective-permute-start | bytes 491528 | tf_op jit(solution)/shard_map/ppermute | solution.py:208
  114.4 3.7 %convolution_convert_fusion.down_ref = bf16[1280,1024]{1,0:T(8,128)(2,1)} fusion(bf16[1280,640]{1,0:T(8,128)(2,1)S(1)} %bitcast.82, s32[1024]{0:T(1024)S(1)} %broadcast_subtract_fusion), kind=kOutput, calls=%fused_computation.2 | convolution fusion | flops 1679687680 | bytes 4263936 | tf_op jit(solution)/shard_map/dot_general | solution.py:45
  118.2 4.1 %collective-permute-done.2 = f32[32,1280]{1,0:T(8,128)S(1)} collective-permute-done((f32[32,1280]{1,0:T(8,128)S(1)}, f32[32,1280]{1,0:T(8,128)S(1)}, u32[]{:S(2)}, u32[]{:S(2)}) %collective-permute-start.2) | collective-permute-done | bytes 163872 | tf_op jit(solution)/shard_map/ppermute | solution.py:208
  122.3 21.7 %collective-permute-done.1 = f32[32,1280]{1,0:T(8,128)S(1)} collective-permute-done((f32[32,1280]{1,0:T(8,128)S(1)}, f32[32,1280]{1,0:T(8,128)S(1)}, u32[]{:S(2)}, u32[]{:S(2)}) %collective-permute-start.1) | collective-permute-done | bytes 163872 | tf_op jit(solution)/shard_map/ppermute | solution.py:208
  144.1 2.4 %collective-permute-start.4 = (f32[32,1280]{1,0:T(8,128)S(1)}, f32[32,1280]{1,0:T(8,128)S(1)}, u32[]{:S(2)}, u32[]{:S(2)}) collective-permute-start(f32[32,1280]{1,0:T(8,128)S(1)} %add_add_fusion.mine_ref), channel_id=1, source_target_pairs={{0,1},{1,0},{2,3},{3,2},{4,5},{5,4},{6,7},{7,6},{8,9},{9,8},{10,11... | collective-permute-start | bytes 491528 | tf_op jit(solution)/shard_map/ppermute | solution.py:22
  149.3 4.5 %middle.1 = (f32[64,1]{1,0:T(8,128)}, f32[64,16]{1,0:T(8,128)}, f32[80,1024]{1,0:T(8,128)}, f32[144,256]{1,0:T(8,128)}) custom-call(s32[2]{0:T(128)} %pad_add_fusion.flag_ref, f32[32,1280]{1,0:T(8,128)} %copy-done.4, f32[32,1280]{1,0:T(8,128)} %copy-done.5, bf16[64,1280]{1,0:T(8,128)(2,1)} %normed_ref.1, f32[64,256]{1,0:T(8,128)} %fusion.9.picked_ref, ...), custom_call_target="tpu_custom_call" | custom-call | tf_op jit(solution)/shard_map/middle/pallas_call | solution.py:229
  153.8 1.9 %collective-permute-start.12 = (f32[144,256]{1,0:T(8,128)}, f32[144,256]{1,0:T(8,128)S(1)}, u32[]{:S(2)}, u32[]{:S(2)}) collective-permute-start(f32[144,256]{1,0:T(8,128)} %get-tuple-element.20.mine_ref), channel_id=1, source_target_pairs={{0,1},{1,0},{2,3},{3,2},{4,5},{5,4},{6,7},{7,6},{8,9},{9,8},{10,11... | collective-permute-start | bytes 442376 | tf_op jit(solution)/shard_map/ppermute | solution.py:22
  158.1 7.3 %last.1 = bf16[64,16,1024]{2,1,0:T(8,128)(2,1)} custom-call(s32[2]{0:T(128)} %pad_add_fusion.flag_ref, f32[64,1024]{1,0:T(8,128)} %fusion.8.gain_ref, f32[64,1]{1,0:T(8,128)} %get-tuple-element.17.inv_ref, f32[64,16]{1,0:T(8,128)} %get-tuple-element.18.share_ref, f32[80,1024]{1,0:T(8,128)} %get-tuple-element.19.own_ref, ...), custom_call_target="tpu_custom_call" | custom-call | tf_op jit(solution)/shard_map/last/pallas_call | solution.py:243
  (105 shorter events, 23.4 us)
Async XLA Ops:
  0.0 11.5 %slice-start = ((s32[1024]{0:T(1024)}), s32[512]{0:T(512)S(1)}, s32[]{:S(2)}) async-start(s32[1024]{0:T(1024)} %param.16), calls=%async_computation.3 | async-start | bytes 4096 | tf_op jit(solution)/shard_map/slice | solution.py:172
  0.0 11.5 %copy-start.9 = (bf16[2,4,1024]{2,1,0:T(4,128)(2,1)S(1)}, bf16[2,4,1024]{2,1,0:T(4,128)(2,1)}, u32[]{:S(2)}) copy-start(bf16[2,4,1024]{2,1,0:T(4,128)(2,1)} %param.18) | copy-start | bytes 49156
  1.5 9.8 %all-to-all-start = ((bf16[4,40,640]{2,1,0:T(8,128)(2,1)}), bf16[4,40,640]{2,1,0:T(8,128)(2,1)S(1)}, u32[]{:S(2)}, u32[]{:S(2)}) async-start(bf16[4,40,640]{2,1,0:T(8,128)(2,1)} %broadcast_in_dim.14), calls=%async_computation | async-start | bytes 409600 | tf_op jit(solution)/shard_map/all_to_all | solution.py:27
  11.9 3.2 %collective-permute-start.5 = (bf16[46,256]{1,0:T(8,128)(2,1)S(1)}, bf16[46,256]{1,0:T(8,128)(2,1)S(1)}, u32[]{:S(2)}, u32[]{:S(2)}) collective-permute-start(bf16[46,256]{1,0:T(8,128)(2,1)S(1)} %fusion.28), channel_id=1, source_target_pairs={{0,1},{2,3},{4,5},{6,7},{8,9},{10,11},{12,13},{14,15},{16,17},{18,... | collective-permute-start | bytes 70664 | tf_op jit(solution)/shard_map/ppermute | solution.py:181
  15.2 24.0 %collective-permute-start.8 = (bf16[46,256]{1,0:T(8,128)(2,1)S(1)}, bf16[46,256]{1,0:T(8,128)(2,1)S(1)}, u32[]{:S(2)}, u32[]{:S(2)}) collective-permute-start(bf16[46,256]{1,0:T(8,128)(2,1)S(1)} %fusion.27), channel_id=1, source_target_pairs={{0,6},{1,7},{8,14},{9,15},{16,22},{17,23},{24,30},{25,31},{32,38},... | collective-permute-start | bytes 70664 | tf_op jit(solution)/shard_map/ppermute | solution.py:182
  25.3 13.8 %collective-permute-start.6 = (bf16[46,256]{1,0:T(8,128)(2,1)S(1)}, bf16[46,256]{1,0:T(8,128)(2,1)S(1)}, u32[]{:S(2)}, u32[]{:S(2)}) collective-permute-start(bf16[46,256]{1,0:T(8,128)(2,1)S(1)} %fusion.27), channel_id=1, source_target_pairs={{0,2},{1,3},{8,10},{9,11},{16,18},{17,19},{24,26},{25,27},{32,34},... | collective-permute-start | bytes 70664 | tf_op jit(solution)/shard_map/ppermute | solution.py:182
  26.6 12.5 %collective-permute-start.7 = (bf16[46,256]{1,0:T(8,128)(2,1)S(1)}, bf16[46,256]{1,0:T(8,128)(2,1)S(1)}, u32[]{:S(2)}, u32[]{:S(2)}) collective-permute-start(bf16[46,256]{1,0:T(8,128)(2,1)S(1)} %fusion.27), channel_id=1, source_target_pairs={{0,4},{1,5},{8,12},{9,13},{16,20},{17,21},{24,28},{25,29},{32,36},... | collective-permute-start | bytes 70664 | tf_op jit(solution)/shard_map/ppermute | solution.py:182
  32.3 48.8 %all-to-all-start.1 = ((bf16[16,160,640]{2,1,0:T(8,128)(2,1)}), bf16[16,160,640]{2,1,0:T(8,128)(2,1)S(1)}, u32[]{:S(2)}, u32[]{:S(2)}) async-start(bf16[16,160,640]{2,1,0:T(8,128)(2,1)} %broadcast_in_dim.15), calls=%async_computation.1 | async-start | bytes 6553600 | tf_op jit(solution)/shard_map/all_to_all | solution.py:27
  39.2 9.2 %collective-permute-start.9 = (bf16[76,256]{1,0:T(8,128)(2,1)S(1)}, bf16[76,256]{1,0:T(8,128)(2,1)S(1)}, u32[]{:S(2)}, u32[]{:S(2)}) collective-permute-start(bf16[76,256]{1,0:T(8,128)(2,1)S(1)} %pad_maximum_fusion.2), channel_id=1, source_target_pairs={{0,24},{8,0},{16,8},{24,16},{1,25},{9,1},{17,9},{25,17},{2,26},{10... | collective-permute-start | bytes 116744 | tf_op jit(solution)/shard_map/ppermute | solution.py:32
  41.2 7.3 %collective-permute-start.10 = (bf16[76,256]{1,0:T(8,128)(2,1)S(1)}, bf16[76,256]{1,0:T(8,128)(2,1)S(1)}, u32[]{:S(2)}, u32[]{:S(2)}) collective-permute-start(bf16[76,256]{1,0:T(8,128)(2,1)S(1)} %pad_maximum_fusion.2), channel_id=1, source_target_pairs={{0,16},{8,24},{16,0},{24,8},{1,17},{9,25},{17,1},{25,9},{2,18},{10... | collective-permute-start | bytes 116744 | tf_op jit(solution)/shard_map/ppermute | solution.py:32
  45.5 5.0 %collective-permute-start.11 = (bf16[76,256]{1,0:T(8,128)(2,1)S(1)}, bf16[76,256]{1,0:T(8,128)(2,1)S(1)}, u32[]{:S(2)}, u32[]{:S(2)}) collective-permute-start(bf16[76,256]{1,0:T(8,128)(2,1)S(1)} %pad_maximum_fusion.2), channel_id=1, source_target_pairs={{0,8},{8,16},{16,24},{24,0},{1,9},{9,17},{17,25},{25,1},{2,10},{10... | collective-permute-start | bytes 116744 | tf_op jit(solution)/shard_map/ppermute | solution.py:32
  81.0 1.7 %copy-start.1 = (bf16[16,160,640]{2,1,0:T(8,128)(2,1)}, bf16[16,160,640]{2,1,0:T(8,128)(2,1)S(1)}, u32[]{:S(2)}) copy-start(bf16[16,160,640]{2,1,0:T(8,128)(2,1)S(1)} %all-to-all-done.1) | copy-start | bytes 9830404
  82.7 64.4 %all-to-all-start.2 = ((bf16[16,16,4864]{2,1,0:T(8,128)(2,1)}), bf16[16,16,4864]{2,1,0:T(8,128)(2,1)S(1)}, u32[]{:S(2)}, u32[]{:S(2)}) async-start(bf16[16,16,4864]{2,1,0:T(8,128)(2,1)} %broadcast_in_dim.20), calls=%async_computation.2 | async-start | bytes 4980736 | tf_op jit(solution)/shard_map/all_to_all | solution.py:212
  94.1 2.3 %copy-start.2 = (bf16[64,1280]{1,0:T(8,128)(2,1)S(1)}, bf16[64,1280]{1,0:T(8,128)(2,1)}, u32[]{:S(2)}) copy-start(bf16[64,1280]{1,0:T(8,128)(2,1)} %normed_ref.1) | copy-start | bytes 491524
  97.5 5.1 %collective-permute-start = (f32[32,1280]{1,0:T(8,128)S(1)}, f32[32,1280]{1,0:T(8,128)S(1)}, u32[]{:S(2)}, u32[]{:S(2)}) collective-permute-start(f32[32,1280]{1,0:T(8,128)S(1)} %constant_dynamic-slice_fusion.4), channel_id=1, source_target_pairs={{0,1},{1,0},{2,3},{3,2},{4,5},{5,4},{6,7},{7,6},{8,9},{9,8},{10,11... | collective-permute-start | bytes 491528 | tf_op jit(solution)/shard_map/ppermute | solution.py:22
  102.6 41.4 %copy-start.8 = (bf16[64,1280]{1,0:T(8,128)(2,1)S(1)}, bf16[64,1280]{1,0:T(8,128)(2,1)}, u32[]{:S(2)}) copy-start(bf16[64,1280]{1,0:T(8,128)(2,1)} %param.11) | copy-start | bytes 491524
  102.6 19.7 %collective-permute-start.2 = (f32[32,1280]{1,0:T(8,128)S(1)}, f32[32,1280]{1,0:T(8,128)S(1)}, u32[]{:S(2)}, u32[]{:S(2)}) collective-permute-start(f32[32,1280]{1,0:T(8,128)S(1)} %dynamic-slice_add_fusion), channel_id=1, source_target_pairs={{0,2},{2,4},{4,6},{6,0},{1,3},{3,5},{5,7},{7,1},{8,10},{10,12},{12... | collective-permute-start | bytes 491528 | tf_op jit(solution)/shard_map/ppermute | solution.py:208
  104.6 17.7 %collective-permute-start.3 = (f32[32,1280]{1,0:T(8,128)S(1)}, f32[32,1280]{1,0:T(8,128)S(1)}, u32[]{:S(2)}, u32[]{:S(2)}) collective-permute-start(f32[32,1280]{1,0:T(8,128)S(1)} %dynamic-slice_add_fusion), channel_id=1, source_target_pairs={{0,6},{2,0},{4,2},{6,4},{1,7},{3,1},{5,3},{7,5},{8,14},{10,8},{12,... | collective-permute-start | bytes 491528 | tf_op jit(solution)/shard_map/ppermute | solution.py:208
  111.9 32.1 %collective-permute-start.1 = (f32[32,1280]{1,0:T(8,128)S(1)}, f32[32,1280]{1,0:T(8,128)S(1)}, u32[]{:S(2)}, u32[]{:S(2)}) collective-permute-start(f32[32,1280]{1,0:T(8,128)S(1)} %dynamic-slice_add_fusion), channel_id=1, source_target_pairs={{0,4},{2,6},{4,0},{6,2},{1,5},{3,7},{5,1},{7,3},{8,12},{10,14},{12... | collective-permute-start | bytes 491528 | tf_op jit(solution)/shard_map/ppermute | solution.py:208
  144.0 3.4 %copy-start.4 = (f32[32,1280]{1,0:T(8,128)}, f32[32,1280]{1,0:T(8,128)S(1)}, u32[]{:S(2)}) copy-start(f32[32,1280]{1,0:T(8,128)S(1)} %add_add_fusion.mine_ref) | copy-start | bytes 491524
  144.1 3.4 %collective-permute-start.4 = (f32[32,1280]{1,0:T(8,128)S(1)}, f32[32,1280]{1,0:T(8,128)S(1)}, u32[]{:S(2)}, u32[]{:S(2)}) collective-permute-start(f32[32,1280]{1,0:T(8,128)S(1)} %add_add_fusion.mine_ref), channel_id=1, source_target_pairs={{0,1},{1,0},{2,3},{3,2},{4,5},{5,4},{6,7},{7,6},{8,9},{9,8},{10,11... | collective-permute-start | bytes 491528 | tf_op jit(solution)/shard_map/ppermute | solution.py:22
  147.1 8.6 %copy-start.3 = (bf16[64,1280]{1,0:T(8,128)(2,1)S(1)}, bf16[64,1280]{1,0:T(8,128)(2,1)}, u32[]{:S(2)}) copy-start(bf16[64,1280]{1,0:T(8,128)(2,1)} %normed_ref.1) | copy-start | bytes 491524
  147.1 8.6 %copy-start.10 = (s32[1024]{0:T(1024)S(1)}, s32[1024]{0:T(1024)}, u32[]{:S(2)}) copy-start(s32[1024]{0:T(1024)} %param.16) | copy-start | bytes 12292
  153.8 3.6 %collective-permute-start.12 = (f32[144,256]{1,0:T(8,128)}, f32[144,256]{1,0:T(8,128)S(1)}, u32[]{:S(2)}, u32[]{:S(2)}) collective-permute-start(f32[144,256]{1,0:T(8,128)} %get-tuple-element.20.mine_ref), channel_id=1, source_target_pairs={{0,1},{1,0},{2,3},{3,2},{4,5},{5,4},{6,7},{7,6},{8,9},{9,8},{10,11... | collective-permute-start | bytes 442376 | tf_op jit(solution)/shard_map/ppermute | solution.py:22
  (4 other events, 3.5 us)

commit v2 on v1

v2 whole, which is shorter than its diff:
```python
import jax
import jax.numpy as jnp
import numpy as np
from jax import lax
from jax.experimental import pallas as pl
from jax.experimental.pallas import tpu as pltpu
from jax.sharding import Mesh, PartitionSpec as P

DP = ("x", "y", "zl")
TENSOR = ("zh", "c")
F32 = jnp.float32
BF16 = jnp.bfloat16
STEP = 16
LIMIT = pltpu.CompilerParams(vmem_limit_bytes=16 * 1024 * 1024)


def gelu_parts(values):
    normal_cdf = 0.5 * (1.0 + jax.scipy.special.erf(values * 0.7071067811865476))
    slope = normal_cdf + values * jnp.exp(-0.5 * values * values) * 0.3989422804014327
    return (values * normal_cdf, slope)


def swap_core(values):
    return lax.ppermute(values, "c", [(0, 1), (1, 0)])


def gather_by_sends(shard, axis, count):
    spread = jnp.broadcast_to(shard[None], (count,) + shard.shape)
    return lax.all_to_all(spread, axis, 0, 0)


def ring_pieces(shard, axis, count):
    return [shard] + [
        lax.ppermute(shard, axis, [(i, (i - k) % count) for i in range(count)]) for k in range(1, count)
    ]


def weights_kernel(code_ref, line_ref, out_ref):
    pieces, rows, _ = line_ref.shape
    total = None
    for k in range(pieces):
        lane = lax.broadcasted_iota(jnp.int32, (code_ref.shape[0], rows), 1) + k * rows
        part = dot32((lane == code_ref[...]).astype(BF16), line_ref[k])
        total = part if total is None else total + part
    line = total.astype(BF16)
    for place in range(out_ref.shape[0]):
        out_ref[place] = line


def extra_kernel(flag_ref, device_ref, row_ref, p0, p1, p2, p3, out_ref):
    places, sub, _ = out_ref.shape
    rows, half = p0.shape
    code = jnp.bitwise_and(device_ref[...] - flag_ref[2], 3) * rows + row_ref[...]
    total = None
    for k, piece in enumerate((p0, p1, p2, p3)):
        lane = lax.broadcasted_iota(jnp.int32, (code.shape[0], rows), 1) + k * rows
        part = dot32((lane == code).astype(BF16), piece[...])
        total = part if total is None else total + part
    line = total.astype(BF16)
    for place in range(places):
        for b in range(line.shape[0] // sub):
            out_ref[place, :, b * half : (b + 1) * half] = line[b * sub : (b + 1) * sub, :]


def forward_kernel(flag_ref, normed_ref, plane_ref, pick_ref, picked_ref, kept_ref, given_ref, slope_ref, part):
    _, rows, hidden_dev = plane_ref.shape
    images, width = normed_ref.shape
    half_images = kept_ref.shape[0]
    half = pick_ref.shape[1] // 2
    up_pre = dot32(normed_ref[...], plane_ref[:, : rows // 2, :].reshape(width, hidden_dev))
    activ, slope = gelu_parts(up_pre)
    slope_ref[...] = slope
    down_t = plane_ref[:, rows // 2 :, :].reshape(width, hidden_dev)
    part[...] = dot_t(activ.astype(BF16), down_t)
    core = flag_ref[1]
    high = slope.astype(BF16)
    low = (slope - high.astype(F32)).astype(BF16)
    gain = dot32(jnp.concatenate([high, low], axis=0), pick_ref[...])
    gain = jnp.where(core == 0, (gain[:images] + gain[images:]) * picked_ref[...], 0.0)
    for out, side, at in ((kept_ref, core, 0), (given_ref, 1 - core, half)):
        out[:, :width] = part[pl.ds(pl.multiple_of(side * half_images, half_images), half_images), :]
        out[:, width : width + half] = gain[:half_images, at : at + half]
        out[:, width + half :] = gain[half_images:, at : at + half]


def split2(values):
    high = lax.reduce_precision(values, 8, 7)
    return high.astype(BF16), (values - high).astype(BF16)


def dot32(lhs, rhs):
    return jnp.dot(lhs, rhs, preferred_element_type=F32)


def dot_t(lhs, rhs):
    return lax.dot_general(lhs, rhs, (((1,), (1,)), ((), ())), preferred_element_type=F32)


def dot_split(values, rhs):
    rows = values.shape[0]
    both = dot32(jnp.concatenate(split2(values), axis=0), rhs)
    return both[:rows] + both[rows:]


def one_hot(index, depth):
    return (lax.broadcasted_iota(jnp.int32, (depth, index.shape[0]), 0) == index[None, :]).astype(BF16)


def solved_kernel(extra_ref, down_ref):
    width, half = down_ref.shape
    places, sub, lanes = extra_ref.shape
    parts = width // (places * sub)
    at = lanes - (parts + 1) * half
    for place in range(places):
        for b in range(parts):
            row = (place * parts + b) * sub
            down_ref[row : row + sub, :] = extra_ref[place, :, at + b * half : at + (b + 1) * half]


def middle_kernel(
    flag_ref, mine_ref, theirs_ref, head_ref, down_ref, down0_ref, down1_ref, inv_ref, share_ref, own_ref, mix_ref
):
    half_images = mine_ref.shape[0]
    width = head_ref.shape[1]
    images = 2 * half_images
    half = down0_ref.shape[1]
    logits = head_ref.shape[0] // 4
    first_core = flag_ref[1] == 0
    mine, theirs = mine_ref[:, :width], theirs_ref[:, :width]
    for side, source in ((flag_ref[1], mine_ref), (1 - flag_ref[1], theirs_ref)):
        mix_ref[side, :half_images, :] = source[:, width : width + half]
        mix_ref[side, half_images:images, :] = source[:, width + half :]
    block = jnp.concatenate([jnp.where(first_core, mine, theirs), jnp.where(first_core, theirs, mine)], axis=0)
    centred = block - jnp.mean(block, axis=1, keepdims=True)
    inv_std = lax.rsqrt(jnp.mean(centred * centred, axis=1, keepdims=True) + 1e-06)
    xhat = centred * inv_std
    inv_ref[...] = inv_std
    high = xhat.astype(BF16)
    low = (xhat - high.astype(F32)).astype(BF16)
    head = head_ref[...]
    both = jnp.concatenate([high, low], axis=0)
    share = dot_t(both, head[2 * logits :])
    share = share[:images] + share[images:]
    share_ref[...] = (share[:, :logits] + share[:, logits:]) / width
    lhs = jnp.concatenate([both, head[: 2 * logits]], axis=0)

    def write(rhs_ref, put):
        product = dot32(lhs, rhs_ref[...])
        tail = product[2 * images :]
        put(slice(0, images), product[:images] + product[images : 2 * images])
        put(slice(images, images + logits), tail[:logits] + tail[logits:])

    def put_own(rows, values):
        own_ref[rows, :] = values

    def put_mine(rows, values):
        mix_ref[flag_ref[1], images + rows.start : images + rows.stop, :] = values

    def put_theirs(rows, values):
        mix_ref[1 - flag_ref[1], images + rows.start : images + rows.stop, :] = values

    write(down_ref, put_own)
    write(down0_ref, put_mine)
    write(down1_ref, put_theirs)


def last_kernel(flag_ref, gain_ref, inv_ref, share_ref, own_ref, mix_ref, inverse_ref, extra_ref, out_ref):
    images = gain_ref.shape[0]
    logits = share_ref.shape[1]
    panel = inverse_ref.shape[1]
    first_image = pl.multiple_of(pl.program_id(0) * STEP, STEP)
    here = pl.ds(first_image, STEP)
    inv_std = inv_ref[here, :]
    diagonal = lax.broadcasted_iota(jnp.int32, (1, logits, logits), 1) == lax.broadcasted_iota(
        jnp.int32, (1, logits, logits), 2
    )
    share = jnp.sum(jnp.where(diagonal, share_ref[here, :][:, None, :], 0.0), axis=2, keepdims=True)

    def jacobian(gain, along, head):
        scale = gain * inv_std
        values = scale[:, None, :] * (head[None] - share * along[:, None, :])
        return values.reshape(STEP * logits, values.shape[2])

    def solved_side(side):
        along = mix_ref[side, pl.ds(images + first_image, STEP), :]
        return jacobian(mix_ref[side, here, :], along, mix_ref[side, 2 * images : 2 * images + logits, :])

    def inverted(values, inverse):
        high = values.astype(BF16)
        low = (values - high.astype(F32)).astype(BF16)
        return (dot_t(high, inverse) + dot_t(low, inverse)).astype(BF16)

    first = inverted(solved_side(0), inverse_ref[0])
    rows_dev = gain_ref.shape[1]
    panel_01 = extra_ref[:, :, extra_ref.shape[2] - panel :].reshape(panel, panel)
    second = inverted(solved_side(1) - dot32(first, panel_01), inverse_ref[1])
    own = jacobian(gain_ref[here, :], own_ref[here, :], own_ref[images : images + logits, :])
    panel_0 = extra_ref[:, :, :rows_dev].reshape(panel, rows_dev)
    panel_1 = extra_ref[:, :, rows_dev : 2 * rows_dev].reshape(panel, rows_dev)
    below = (own - (dot32(first, panel_0) + dot32(second, panel_1))).astype(BF16)
    out_ref[...] = below.reshape(out_ref.shape)

    @pl.when(flag_ref[0] == 1)
    def _():
        out_ref[:, :, :panel] = first.reshape(STEP, logits, panel)
        out_ref[:, :, panel : 2 * panel] = second.reshape(STEP, logits, panel)


def body(normed, residual_in, w_up, w_down, final_gain, head_cols, sub_inputs, sub_hidden, panels, inverses):
    images, width = normed.shape
    own, hidden_dev = w_up.shape
    logits = head_cols.shape[1]
    panel = inverses.shape[1]
    panel_dev = panels.shape[1]
    rows_dev = sub_inputs.shape[0]
    z_hi, core = lax.axis_index("zh"), lax.axis_index("c")
    rank = z_hi * 2 + core
    local_hidden = sub_hidden - rank * hidden_dev
    half = panel
    vmem = pl.BlockSpec(memory_space=pltpu.VMEM)
    smem = pl.BlockSpec(memory_space=pltpu.SMEM)
    flag = jnp.stack([jnp.where(rank == 0, 1, 0), core, lax.axis_index("zl")]).astype(jnp.int32)

    both = jnp.concatenate([w_up, w_down.T], axis=0)
    line = gather_by_sends(both, "zl", 4)
    row = np.arange(8 * own)
    code = row % (4 * own) // own * (2 * own) + row // (4 * own) * own + row % own
    line = pl.pallas_call(
        weights_kernel,
        out_shape=jax.ShapeDtypeStruct((16, 8 * own, hidden_dev), BF16),
        in_specs=[vmem] * 2,
        out_specs=vmem,
        compiler_params=LIMIT,
        name="merge_weights",
    )(code.astype(np.int32)[:, None], line)
    plane = lax.all_to_all(line, ("x", "y"), 0, 0)

    later, panels_later, hidden_first, inputs_later, _ = lax.optimization_barrier(
        (both[own:], panels, local_hidden[: 2 * panel], sub_inputs, line[0, :16, :128])
    )
    pick_first = one_hot(hidden_first, hidden_dev)
    chosen = dot32(later, pick_first).astype(BF16)
    block01 = panels_later[0][:, panel : 2 * panel]
    other = lax.ppermute(jnp.concatenate([chosen[:, half:], block01], axis=0), "c", [(0, 1)])
    payload = jnp.where(core == 0, jnp.concatenate([chosen[:, :half], block01], axis=0), other)
    sent = [lax.ppermute(payload, "zh", [(0, k)]) for k in (1, 2, 3)]
    payload = jnp.where(z_hi == 0, payload, sent[0] + sent[1] + sent[2])

    chunks = rows_dev // half
    narrow = jnp.concatenate([panels_later.reshape(2 * panel_dev * chunks, half), payload], axis=0)
    pieces = ring_pieces(narrow, "zl", 4)
    device, source = [], []
    for q in range(2):
        for b in range(chunks):
            device += [r // panel_dev for r in range(4 * panel_dev)]
            source += [(q * panel_dev + r % panel_dev) * chunks + b for r in range(4 * panel_dev)]
    at = 2 * panel_dev * chunks
    device += [r // own for r in range(4 * own)] + [r // panel_dev for r in range(4 * panel_dev)]
    source += [at + r % own for r in range(4 * own)] + [at + own + r % panel_dev for r in range(4 * panel_dev)]
    extra = pl.pallas_call(
        extra_kernel,
        out_shape=jax.ShapeDtypeStruct((16, 16, len(device) // 16 * half), BF16),
        in_specs=[smem] + [vmem] * 6,
        out_specs=vmem,
        compiler_params=LIMIT,
        name="merge_extra",
    )(flag, np.array(device, np.int32)[:, None], np.array(source, np.int32)[:, None], *pieces)
    extra = lax.all_to_all(extra, ("x", "y"), 0, 0)

    picked = dot32(normed, one_hot(inputs_later, width))
    kept, given, slope = pl.pallas_call(
        forward_kernel,
        out_shape=(
            jax.ShapeDtypeStruct((images // 2, width + 2 * half), F32),
            jax.ShapeDtypeStruct((images // 2, width + 2 * half), F32),
            jax.ShapeDtypeStruct((images, hidden_dev), F32),
        ),
        in_specs=[smem] + [vmem] * 4,
        out_specs=(vmem,) * 3,
        scratch_shapes=[pltpu.VMEM((images, width), F32)],
        compiler_params=LIMIT,
        name="forward",
    )(flag, normed, plane, pick_first, picked[:, : 2 * panel])
    pair = kept + swap_core(given)
    pair_sent = pair.astype(BF16)
    peers = [lax.ppermute(pair_sent, "zh", [(i, (i + k) % 4) for i in range(4)]) for k in (2, 1, 3)]

    pick_own = one_hot(local_hidden, hidden_dev)
    down_t = plane[:, 4 * own :].reshape(width, hidden_dev)
    down_own = dot32(down_t, pick_own).astype(BF16)
    gain_own = dot_split(slope, pick_own) * picked
    head = final_gain[:, None] * head_cols.astype(F32)
    centred_head = head - jnp.mean(head, axis=0)
    head_parts = jnp.concatenate(split2(centred_head.T) + split2(head.T), axis=0)

    peers = [peer.astype(F32) for peer in peers]
    mine = lax.dynamic_slice_in_dim(residual_in, core * (images // 2), images // 2, 0).astype(F32)
    block = mine + ((pair + peers[0]) + (peers[1] + peers[2]))[:, :width]
    solved_gain = [values[:, width:] for values in (pair, peers[1], peers[0], peers[2])]
    gain = jnp.where(z_hi == 0, solved_gain[0], solved_gain[1])
    gain = jnp.where(z_hi == 2, solved_gain[2], jnp.where(z_hi == 3, solved_gain[3], gain))
    block = jnp.concatenate([block, gain], axis=1)
    block_pair = swap_core(block)

    down_mine = pl.pallas_call(
        solved_kernel,
        out_shape=jax.ShapeDtypeStruct((width, half), BF16),
        in_specs=[vmem],
        out_specs=vmem,
        compiler_params=LIMIT,
        name="solved",
    )(extra)
    down_theirs = swap_core(down_mine)
    inv_std, share, own_products, mix = pl.pallas_call(
        middle_kernel,
        out_shape=(
            jax.ShapeDtypeStruct((images, 1), F32),
            jax.ShapeDtypeStruct((images, logits), F32),
            jax.ShapeDtypeStruct((images + logits, rows_dev), F32),
            jax.ShapeDtypeStruct((2, 2 * images + logits, half), F32),
        ),
        in_specs=[smem] + [vmem] * 6,
        out_specs=(vmem,) * 4,
        compiler_params=LIMIT,
        name="middle",
    )(flag, block, block_pair, head_parts, down_own, down_mine, down_theirs)
    return pl.pallas_call(
        last_kernel,
        grid=(images // STEP,),
        out_shape=jax.ShapeDtypeStruct((images, logits, rows_dev), BF16),
        in_specs=[smem] + [vmem] * 7,
        out_specs=pl.BlockSpec((STEP, logits, rows_dev), lambda i: (i, 0, 0)),
        compiler_params=LIMIT,
        name="last",
    )(flag, gain_own, inv_std, share, own_products, mix, inverses, extra)


def solution(mesh):
    fine = Mesh(mesh.devices.reshape(4, 4, 4, 4, 2), ("x", "y", "zl", "zh", "c"))
    in_specs = (
        P(DP, None),
        P(DP, None),
        P(DP, TENSOR),
        P(TENSOR, DP),
        P(),
        P(),
        P(TENSOR),
        P(TENSOR),
        P(None, DP, TENSOR),
        P(),
    )
    out_specs = P(DP, None, TENSOR)

    return jax.shard_map(body, mesh=fine, in_specs=in_specs, out_specs=out_specs, check_vma=False)
```

time: 166 us -> 184 us (1.11)
  the two profiles are of different devices: /device:TPU:99 before, /device:TPU:32 now
where the time goes in v2:
time: 184 us; the launch traced here: 183 us
  waiting for transfers between devices  75.5 us (41%)
  starting transfers between devices  72.8 us (40%)
  local copies, waits for them, and re-layouts  14 us (8%)
  Pallas kernels  12.1 us (7%)
  matrix products  4.95 us (3%)
  other arithmetic  3.13 us (2%)
    all_to_all x1, waiting for transfers between devices, body(): plane = lax.all_to_all(line, ('x', 'y'), 0, 0)  33.2 us
    ppermute x3, starting transfers between devices, body(): lax.ppermute(pair_sent, 'zh', [(i, (i + k) % 4) for i in range(4)])  22.9 us
    all_to_all x1, waiting for transfers between devices, body(): extra = lax.all_to_all(extra, ('x', 'y'), 0, 0)  21 us
    ppermute x3, waiting for transfers between devices, body(): lax.ppermute(pair_sent, 'zh', [(i, (i + k) % 4) for i in range(4)])  17.8 us
    ppermute x3, starting transfers between devices, body(): sent = [lax.ppermute(payload, 'zh', [(0, k)]) for k in (1, 2, 3)]  12.1 us
    unnamed x38, local copies, waits for them, and re-layouts  11.1 us
    ppermute x3, starting transfers between devices, ring_pieces(): lax.ppermute(shard, axis, [(i, (i - k) % count) for i in range(count)])  11 us
    all_to_all x1, starting transfers between devices, gather_by_sends(): return lax.all_to_all(spread, axis, 0, 0)  8.34 us
  transfers between devices with their start and end apart: 16, of which 7 were waited for; matrix products, arithmetic and copies ran while one was open for 5% of the time, Pallas kernels for 2%

profile of v2, /device:TPU:32, one launch (start us, length us, event | category | flops | bytes accessed | tf_op | source)
XLA Modules:
  0.0 182.9 jit_solution(8615331308403688891)
XLA Ops:
  2.5 1.7 collective-permute-start.5
  5.7 8.3 %all-to-all-start = ((bf16[4,40,640]{2,1,0:T(8,128)(2,1)}), bf16[4,40,640]{2,1,0:T(8,128)(2,1)S(1)}, u32[]{:S(2)}, u32[]{:S(2)}) async-start(bf16[4,40,640]{2,1,0:T(8,128)(2,1)} %broadcast_in_dim.2), calls=%async_computation | async-start | bytes 409600 | tf_op jit(solution)/shard_map/all_to_all | solution.py:29
  14.1 7.8 %collective-permute-start.8 = (bf16[24,256]{1,0:T(8,128)(2,1)S(1)}, bf16[24,256]{1,0:T(8,128)(2,1)S(1)}, u32[]{:S(2)}, u32[]{:S(2)}) collective-permute-start(bf16[24,256]{1,0:T(8,128)(2,1)S(1)} %fusion.23), channel_id=1, source_target_pairs={{0,6},{1,7},{8,14},{9,15},{16,22},{17,23},{24,30},{25,31},{32,38},... | collective-permute-start | bytes 36872 | tf_op jit(solution)/shard_map/ppermute | solution.py:246
  23.2 3.0 %collective-permute-start.7 = (bf16[24,256]{1,0:T(8,128)(2,1)S(1)}, bf16[24,256]{1,0:T(8,128)(2,1)S(1)}, u32[]{:S(2)}, u32[]{:S(2)}) collective-permute-start(bf16[24,256]{1,0:T(8,128)(2,1)S(1)} %fusion.23), channel_id=1, source_target_pairs={{0,4},{1,5},{8,12},{9,13},{16,20},{17,21},{24,28},{25,29},{32,36},... | collective-permute-start | bytes 36872 | tf_op jit(solution)/shard_map/ppermute | solution.py:246
  27.7 2.0 %collective-permute-start.9 = (bf16[56,256]{1,0:T(8,128)(2,1)S(1)}, bf16[56,256]{1,0:T(8,128)(2,1)S(1)}, u32[]{:S(2)}, u32[]{:S(2)}) collective-permute-start(bf16[56,256]{1,0:T(8,128)(2,1)S(1)} %pad_maximum_fusion.3.p0), channel_id=1, source_target_pairs={{0,24},{8,0},{16,8},{24,16},{1,25},{9,1},{17,9},{25,17},{2,26},{10... | collective-permute-start | bytes 86024 | tf_op jit(solution)/shard_map/ppermute | solution.py:34
  29.6 4.8 %collective-permute-start.10 = (bf16[56,256]{1,0:T(8,128)(2,1)S(1)}, bf16[56,256]{1,0:T(8,128)(2,1)S(1)}, u32[]{:S(2)}, u32[]{:S(2)}) collective-permute-start(bf16[56,256]{1,0:T(8,128)(2,1)S(1)} %pad_maximum_fusion.3.p0), channel_id=1, source_target_pairs={{0,16},{8,24},{16,0},{24,8},{1,17},{9,25},{17,1},{25,9},{2,18},{10... | collective-permute-start | bytes 86024 | tf_op jit(solution)/shard_map/ppermute | solution.py:34
  34.4 4.3 %collective-permute-start.11 = (bf16[56,256]{1,0:T(8,128)(2,1)S(1)}, bf16[56,256]{1,0:T(8,128)(2,1)S(1)}, u32[]{:S(2)}, u32[]{:S(2)}) collective-permute-start(bf16[56,256]{1,0:T(8,128)(2,1)S(1)} %pad_maximum_fusion.3.p0), channel_id=1, source_target_pairs={{0,8},{8,16},{16,24},{24,0},{1,9},{9,17},{17,25},{25,1},{2,10},{10... | collective-permute-start | bytes 86024 | tf_op jit(solution)/shard_map/ppermute | solution.py:34
  44.3 7.2 %all-to-all-start.2 = ((bf16[16,16,3584]{2,1,0:T(8,128)(2,1)}), bf16[16,16,3584]{2,1,0:T(8,128)(2,1)S(1)}, u32[]{:S(2)}, u32[]{:S(2)}) async-start(bf16[16,16,3584]{2,1,0:T(8,128)(2,1)} %copy-done.4), calls=%async_computation.2 | async-start | bytes 3670016 | tf_op jit(solution)/shard_map/all_to_all | solution.py:268
  52.1 1.7 copy-done.3
  53.8 21.0 %all-to-all-done.2.extra_ref = bf16[16,16,3584]{2,1,0:T(8,128)(2,1)S(1)} async-done(((bf16[16,16,3584]{2,1,0:T(8,128)(2,1)}), bf16[16,16,3584]{2,1,0:T(8,128)(2,1)S(1)}, u32[]{:S(2)}, u32[]{:S(2)}) %all-to-all-start.2) | async-done | bytes 1835040 | tf_op jit(solution)/shard_map/all_to_all | solution.py:268
  76.0 3.7 %all-to-all-start.1 = ((bf16[16,160,640]{2,1,0:T(8,128)(2,1)}), bf16[16,160,640]{2,1,0:T(8,128)(2,1)S(1)}, u32[]{:S(2)}, u32[]{:S(2)}) async-start(bf16[16,160,640]{2,1,0:T(8,128)(2,1)} %copy-done.3), calls=%async_computation.1 | async-start | bytes 6553600 | tf_op jit(solution)/shard_map/all_to_all | solution.py:236
  83.5 1.5 copy-done.1
  85.8 1.9 %collective-permute-start.12 = (bf16[1280,256]{1,0:T(8,128)(2,1)}, bf16[1280,256]{1,0:T(8,128)(2,1)}, u32[]{:S(2)}, u32[]{:S(2)}) collective-permute-start(bf16[1280,256]{1,0:T(8,128)(2,1)} %solved.1.down0_ref), channel_id=1, source_target_pairs={{0,1},{1,0},{2,3},{3,2},{4,5},{5,4},{6,7},{7,6},{8,9},{9,8},{10,11... | collective-permute-start | bytes 1966088 | tf_op jit(solution)/shard_map/ppermute | solution.py:24
  87.7 33.2 %all-to-all-done.1.plane_ref = bf16[16,160,640]{2,1,0:T(8,128)(2,1)S(1)} async-done(((bf16[16,160,640]{2,1,0:T(8,128)(2,1)}), bf16[16,160,640]{2,1,0:T(8,128)(2,1)S(1)}, u32[]{:S(2)}, u32[]{:S(2)}) %all-to-all-start.1) | async-done | bytes 3276832 | tf_op jit(solution)/shard_map/all_to_all | solution.py:236
  123.9 1.6 forward.1
  125.4 1.9 %collective-permute-start = (f32[32,1792]{1,0:T(8,128)S(1)}, f32[32,1792]{1,0:T(8,128)S(1)}, u32[]{:S(2)}, u32[]{:S(2)}) collective-permute-start(f32[32,1792]{1,0:T(8,128)S(1)} %get-tuple-element.20), channel_id=1, source_target_pairs={{0,1},{1,0},{2,3},{3,2},{4,5},{5,4},{6,7},{7,6},{8,9},{9,8},{10,11... | collective-permute-start | bytes 688136 | tf_op jit(solution)/shard_map/ppermute | solution.py:24
  127.5 2.3 %convolution_convert_fusion.down_ref = bf16[1280,1024]{1,0:T(8,128)(2,1)S(1)} fusion(bf16[1280,640]{1,0:T(8,128)(2,1)S(1)} %bitcast.18, s32[1024]{0:T(1024)S(1)} %broadcast_subtract_fusion), kind=kOutput, calls=%fused_computation.2 | convolution fusion | flops 1679687680 | bytes 4263936 | tf_op jit(solution)/shard_map/dot_general | solution.py:92
  129.9 6.0 %collective-permute-start.2 = (bf16[32,1792]{1,0:T(8,128)(2,1)S(1)}, bf16[32,1792]{1,0:T(8,128)(2,1)S(1)}, u32[]{:S(2)}, u32[]{:S(2)}) collective-permute-start(bf16[32,1792]{1,0:T(8,128)(2,1)S(1)} %get-tuple-element.27), channel_id=1, source_target_pairs={{0,2},{2,4},{4,6},{6,0},{1,3},{3,5},{5,7},{7,1},{8,10},{10,12},{12... | collective-permute-start | bytes 344072 | tf_op jit(solution)/shard_map/ppermute | solution.py:286
  135.9 3.9 %collective-permute-start.3 = (bf16[32,1792]{1,0:T(8,128)(2,1)S(1)}, bf16[32,1792]{1,0:T(8,128)(2,1)S(1)}, u32[]{:S(2)}, u32[]{:S(2)}) collective-permute-start(bf16[32,1792]{1,0:T(8,128)(2,1)S(1)} %get-tuple-element.27), channel_id=1, source_target_pairs={{0,6},{2,0},{4,2},{6,4},{1,7},{3,1},{5,3},{7,5},{8,14},{10,8},{12,... | collective-permute-start | bytes 344072 | tf_op jit(solution)/shard_map/ppermute | solution.py:286
  139.8 13.0 %collective-permute-start.1 = (bf16[32,1792]{1,0:T(8,128)(2,1)S(1)}, bf16[32,1792]{1,0:T(8,128)(2,1)S(1)}, u32[]{:S(2)}, u32[]{:S(2)}) collective-permute-start(bf16[32,1792]{1,0:T(8,128)(2,1)S(1)} %get-tuple-element.27), channel_id=1, source_target_pairs={{0,4},{2,6},{4,0},{6,2},{1,5},{3,7},{5,1},{7,3},{8,12},{10,14},{12... | collective-permute-start | bytes 344072 | tf_op jit(solution)/shard_map/ppermute | solution.py:286
  154.4 16.9 %collective-permute-done.1 = bf16[32,1792]{1,0:T(8,128)(2,1)S(1)} collective-permute-done((bf16[32,1792]{1,0:T(8,128)(2,1)S(1)}, bf16[32,1792]{1,0:T(8,128)(2,1)S(1)}, u32[]{:S(2)}, u32[]{:S(2)}) %collective-permute-start.1) | collective-permute-done | bytes 114720 | tf_op jit(solution)/shard_map/ppermute | solution.py:286
  171.4 1.9 %collective-permute-start.4 = (f32[32,1792]{1,0:T(8,128)S(1)}, f32[32,1792]{1,0:T(8,128)S(1)}, u32[]{:S(2)}, u32[]{:S(2)}) collective-permute-start(f32[32,1792]{1,0:T(8,128)S(1)} %pad_maximum_fusion.mine_ref), channel_id=1, source_target_pairs={{0,1},{1,0},{2,3},{3,2},{4,5},{5,4},{6,7},{7,6},{8,9},{9,8},{10,11... | collective-permute-start | bytes 688136 | tf_op jit(solution)/shard_map/ppermute | solution.py:24
  174.8 2.4 %middle.1 = (f32[64,1]{1,0:T(8,128)S(1)}, f32[64,16]{1,0:T(8,128)S(1)}, f32[80,1024]{1,0:T(8,128)S(1)}, f32[2,144,256]{2,1,0:T(8,128)S(1)}) custom-call(s32[3]{0:T(128)S(1)} %pad_add_fusion.flag_ref, f32[32,1792]{1,0:T(8,128)S(1)} %pad_maximum_fusion.mine_ref, f32[32,1792]{1,0:T(8,128)S(1)} %collective-permute-done.4.theirs_ref, ...), custom_call_target="tpu_custom_call" | custom-call | tf_op jit(solution)/shard_map/middle/pallas_call | solution.py:314
  177.2 5.7 %last.1 = bf16[64,16,1024]{2,1,0:T(8,128)(2,1)} custom-call(s32[3]{0:T(128)S(1)} %pad_add_fusion.flag_ref, f32[64,1024]{1,0:T(8,128)S(1)} %fusion.10.gain_ref, f32[64,1]{1,0:T(8,128)S(1)} %get-tuple-element.23.inv_ref, f32[64,16]{1,0:T(8,128)S(1)} %get-tuple-element.24.share_ref, f32[80,1024]{1,0:T(8,128)S(1)} %get-tuple-element.25.own_ref, ...), custom_call_target="tpu_custom_call" | custom-call | tf_op jit(solution)/shard_map/last/pallas_call | solution.py:327
  (85 shorter events, 24.8 us)
Async XLA Ops:
  2.5 11.6 %collective-permute-start.5 = (bf16[24,256]{1,0:T(8,128)(2,1)S(1)}, bf16[24,256]{1,0:T(8,128)(2,1)S(1)}, u32[]{:S(2)}, u32[]{:S(2)}) collective-permute-start(bf16[24,256]{1,0:T(8,128)(2,1)S(1)} %pad_maximum_fusion.4), channel_id=1, source_target_pairs={{0,1},{2,3},{4,5},{6,7},{8,9},{10,11},{12,13},{14,15},{16,17},{18,... | collective-permute-start | bytes 36872 | tf_op jit(solution)/shard_map/ppermute | solution.py:244
  5.7 38.5 %all-to-all-start = ((bf16[4,40,640]{2,1,0:T(8,128)(2,1)}), bf16[4,40,640]{2,1,0:T(8,128)(2,1)S(1)}, u32[]{:S(2)}, u32[]{:S(2)}) async-start(bf16[4,40,640]{2,1,0:T(8,128)(2,1)} %broadcast_in_dim.2), calls=%async_computation | async-start | bytes 409600 | tf_op jit(solution)/shard_map/all_to_all | solution.py:29
  14.1 12.9 %collective-permute-start.8 = (bf16[24,256]{1,0:T(8,128)(2,1)S(1)}, bf16[24,256]{1,0:T(8,128)(2,1)S(1)}, u32[]{:S(2)}, u32[]{:S(2)}) collective-permute-start(bf16[24,256]{1,0:T(8,128)(2,1)S(1)} %fusion.23), channel_id=1, source_target_pairs={{0,6},{1,7},{8,14},{9,15},{16,22},{17,23},{24,30},{25,31},{32,38},... | collective-permute-start | bytes 36872 | tf_op jit(solution)/shard_map/ppermute | solution.py:246
  21.9 5.1 %collective-permute-start.6 = (bf16[24,256]{1,0:T(8,128)(2,1)S(1)}, bf16[24,256]{1,0:T(8,128)(2,1)S(1)}, u32[]{:S(2)}, u32[]{:S(2)}) collective-permute-start(bf16[24,256]{1,0:T(8,128)(2,1)S(1)} %fusion.23), channel_id=1, source_target_pairs={{0,2},{1,3},{8,10},{9,11},{16,18},{17,19},{24,26},{25,27},{32,34},... | collective-permute-start | bytes 36872 | tf_op jit(solution)/shard_map/ppermute | solution.py:246
  23.2 4.4 %collective-permute-start.7 = (bf16[24,256]{1,0:T(8,128)(2,1)S(1)}, bf16[24,256]{1,0:T(8,128)(2,1)S(1)}, u32[]{:S(2)}, u32[]{:S(2)}) collective-permute-start(bf16[24,256]{1,0:T(8,128)(2,1)S(1)} %fusion.23), channel_id=1, source_target_pairs={{0,4},{1,5},{8,12},{9,13},{16,20},{17,21},{24,28},{25,29},{32,36},... | collective-permute-start | bytes 36872 | tf_op jit(solution)/shard_map/ppermute | solution.py:246
  27.7 11.1 %collective-permute-start.9 = (bf16[56,256]{1,0:T(8,128)(2,1)S(1)}, bf16[56,256]{1,0:T(8,128)(2,1)S(1)}, u32[]{:S(2)}, u32[]{:S(2)}) collective-permute-start(bf16[56,256]{1,0:T(8,128)(2,1)S(1)} %pad_maximum_fusion.3.p0), channel_id=1, source_target_pairs={{0,24},{8,0},{16,8},{24,16},{1,25},{9,1},{17,9},{25,17},{2,26},{10... | collective-permute-start | bytes 86024 | tf_op jit(solution)/shard_map/ppermute | solution.py:34
  29.6 9.2 %collective-permute-start.10 = (bf16[56,256]{1,0:T(8,128)(2,1)S(1)}, bf16[56,256]{1,0:T(8,128)(2,1)S(1)}, u32[]{:S(2)}, u32[]{:S(2)}) collective-permute-start(bf16[56,256]{1,0:T(8,128)(2,1)S(1)} %pad_maximum_fusion.3.p0), channel_id=1, source_target_pairs={{0,16},{8,24},{16,0},{24,8},{1,17},{9,25},{17,1},{25,9},{2,18},{10... | collective-permute-start | bytes 86024 | tf_op jit(solution)/shard_map/ppermute | solution.py:34
  34.4 5.8 %collective-permute-start.11 = (bf16[56,256]{1,0:T(8,128)(2,1)S(1)}, bf16[56,256]{1,0:T(8,128)(2,1)S(1)}, u32[]{:S(2)}, u32[]{:S(2)}) collective-permute-start(bf16[56,256]{1,0:T(8,128)(2,1)S(1)} %pad_maximum_fusion.3.p0), channel_id=1, source_target_pairs={{0,8},{8,16},{16,24},{24,0},{1,9},{9,17},{17,25},{25,1},{2,10},{10... | collective-permute-start | bytes 86024 | tf_op jit(solution)/shard_map/ppermute | solution.py:34
  44.3 7.2 %copy-start.12 = (s32[160,1]{1,0:T(8,128)S(1)}, s32[160,1]{1,0:T(8,128)}, u32[]{:S(2)}) copy-start(s32[160,1]{1,0:T(8,128)} %constant.36.clone.code_ref) | copy-start | bytes 1924
  44.3 30.5 %all-to-all-start.2 = ((bf16[16,16,3584]{2,1,0:T(8,128)(2,1)}), bf16[16,16,3584]{2,1,0:T(8,128)(2,1)S(1)}, u32[]{:S(2)}, u32[]{:S(2)}) async-start(bf16[16,16,3584]{2,1,0:T(8,128)(2,1)} %copy-done.4), calls=%async_computation.2 | async-start | bytes 3670016 | tf_op jit(solution)/shard_map/all_to_all | solution.py:268
  53.8 26.1 %copy-start.8 = (bf16[64,1280]{1,0:T(8,128)(2,1)S(1)}, bf16[64,1280]{1,0:T(8,128)(2,1)}, u32[]{:S(2)}) copy-start(bf16[64,1280]{1,0:T(8,128)(2,1)} %normed_ref.1) | copy-start | bytes 491524
  53.8 26.1 %copy-start.18 = (s32[1024]{0:T(1024)S(1)}, s32[1024]{0:T(1024)}, u32[]{:S(2)}) copy-start(s32[1024]{0:T(1024)} %param.19) | copy-start | bytes 12292
  76.0 44.9 %all-to-all-start.1 = ((bf16[16,160,640]{2,1,0:T(8,128)(2,1)}), bf16[16,160,640]{2,1,0:T(8,128)(2,1)S(1)}, u32[]{:S(2)}, u32[]{:S(2)}) async-start(bf16[16,160,640]{2,1,0:T(8,128)(2,1)} %copy-done.3), calls=%async_computation.1 | async-start | bytes 6553600 | tf_op jit(solution)/shard_map/all_to_all | solution.py:236
  79.8 2.4 %copy-start.15 = (bf16[1280,16]{0,1:T(8,128)(2,1)S(1)}, bf16[1280,16]{0,1:T(8,128)(2,1)}, u32[]{:S(2)}) copy-start(bf16[1280,16]{0,1:T(8,128)(2,1)} %param.18) | copy-start | bytes 122884
  85.8 87.6 %collective-permute-start.12 = (bf16[1280,256]{1,0:T(8,128)(2,1)}, bf16[1280,256]{1,0:T(8,128)(2,1)}, u32[]{:S(2)}, u32[]{:S(2)}) collective-permute-start(bf16[1280,256]{1,0:T(8,128)(2,1)} %solved.1.down0_ref), channel_id=1, source_target_pairs={{0,1},{1,0},{2,3},{3,2},{4,5},{5,4},{6,7},{7,6},{8,9},{9,8},{10,11... | collective-permute-start | bytes 1966088 | tf_op jit(solution)/shard_map/ppermute | solution.py:24
  125.4 4.4 %collective-permute-start = (f32[32,1792]{1,0:T(8,128)S(1)}, f32[32,1792]{1,0:T(8,128)S(1)}, u32[]{:S(2)}, u32[]{:S(2)}) collective-permute-start(f32[32,1792]{1,0:T(8,128)S(1)} %get-tuple-element.20), channel_id=1, source_target_pairs={{0,1},{1,0},{2,3},{3,2},{4,5},{5,4},{6,7},{7,6},{8,9},{9,8},{10,11... | collective-permute-start | bytes 688136 | tf_op jit(solution)/shard_map/ppermute | solution.py:24
  129.8 41.5 %copy-start.16 = (bf16[64,1280]{1,0:T(8,128)(2,1)S(1)}, bf16[64,1280]{1,0:T(8,128)(2,1)}, u32[]{:S(2)}) copy-start(bf16[64,1280]{1,0:T(8,128)(2,1)} %param.14) | copy-start | bytes 491524
  129.9 43.5 %copy-start.14 = (f32[64,1024]{1,0:T(8,128)S(1)}, f32[64,1024]{1,0:T(8,128)}, u32[]{:S(2)}) copy-start(f32[64,1024]{1,0:T(8,128)} %copy-done.13) | copy-start | bytes 786436
  129.9 23.6 %collective-permute-start.2 = (bf16[32,1792]{1,0:T(8,128)(2,1)S(1)}, bf16[32,1792]{1,0:T(8,128)(2,1)S(1)}, u32[]{:S(2)}, u32[]{:S(2)}) collective-permute-start(bf16[32,1792]{1,0:T(8,128)(2,1)S(1)} %get-tuple-element.27), channel_id=1, source_target_pairs={{0,2},{2,4},{4,6},{6,0},{1,3},{3,5},{5,7},{7,1},{8,10},{10,12},{12... | collective-permute-start | bytes 344072 | tf_op jit(solution)/shard_map/ppermute | solution.py:286
  135.9 18.5 %collective-permute-start.3 = (bf16[32,1792]{1,0:T(8,128)(2,1)S(1)}, bf16[32,1792]{1,0:T(8,128)(2,1)S(1)}, u32[]{:S(2)}, u32[]{:S(2)}) collective-permute-start(bf16[32,1792]{1,0:T(8,128)(2,1)S(1)} %get-tuple-element.27), channel_id=1, source_target_pairs={{0,6},{2,0},{4,2},{6,4},{1,7},{3,1},{5,3},{7,5},{8,14},{10,8},{12,... | collective-permute-start | bytes 344072 | tf_op jit(solution)/shard_map/ppermute | solution.py:286
  139.8 31.5 %collective-permute-start.1 = (bf16[32,1792]{1,0:T(8,128)(2,1)S(1)}, bf16[32,1792]{1,0:T(8,128)(2,1)S(1)}, u32[]{:S(2)}, u32[]{:S(2)}) collective-permute-start(bf16[32,1792]{1,0:T(8,128)(2,1)S(1)} %get-tuple-element.27), channel_id=1, source_target_pairs={{0,4},{2,6},{4,0},{6,2},{1,5},{3,7},{5,1},{7,3},{8,12},{10,14},{12... | collective-permute-start | bytes 344072 | tf_op jit(solution)/shard_map/ppermute | solution.py:286
  171.4 3.4 %collective-permute-start.4 = (f32[32,1792]{1,0:T(8,128)S(1)}, f32[32,1792]{1,0:T(8,128)S(1)}, u32[]{:S(2)}, u32[]{:S(2)}) collective-permute-start(f32[32,1792]{1,0:T(8,128)S(1)} %pad_maximum_fusion.mine_ref), channel_id=1, source_target_pairs={{0,1},{1,0},{2,3},{3,2},{4,5},{5,4},{6,7},{7,6},{8,9},{9,8},{10,11... | collective-permute-start | bytes 688136 | tf_op jit(solution)/shard_map/ppermute | solution.py:24
  173.4 3.8 %copy-start.2 = (bf16[16,16,3584]{2,1,0:T(8,128)(2,1)S(1)}, bf16[16,16,3584]{2,1,0:T(8,128)(2,1)}, u32[]{:S(2)}) copy-start(bf16[16,16,3584]{2,1,0:T(8,128)(2,1)} %copy-done) | copy-start | bytes 5505028
  173.4 3.8 %copy-start.7 = (bf16[2,256,256]{2,1,0:T(8,128)(2,1)S(1)}, bf16[2,256,256]{2,1,0:T(8,128)(2,1)}, u32[]{:S(2)}) copy-start(bf16[2,256,256]{2,1,0:T(8,128)(2,1)} %inverse_ref.1) | copy-start | bytes 786436
  (11 other events, 13.4 us)

commit v3 on v2

--- a/solution.py
+++ b/solution.py
@@ -10,8 +10,9 @@
 TENSOR = ("zh", "c")
 F32 = jnp.float32
 BF16 = jnp.bfloat16
-STEP = 16
-LIMIT = pltpu.CompilerParams(vmem_limit_bytes=16 * 1024 * 1024)
+STEP = 32
+LARGE = pltpu.CompilerParams(vmem_limit_bytes=60 * 1024 * 1024)
+LIMIT = pltpu.CompilerParams(vmem_limit_bytes=20 * 1024 * 1024)
 
 
 def gelu_parts(values):
@@ -35,20 +36,30 @@
     ]
 
 
-def weights_kernel(code_ref, line_ref, out_ref):
+def weights_kernel(line_ref, out_ref, merged, done):
     pieces, rows, _ = line_ref.shape
+    own = rows // 2
+    shape = (pieces * rows, rows)
+    row, source = (lax.broadcasted_iota(jnp.int32, shape, axis) for axis in (0, 1))
     total = None
     for k in range(pieces):
-        lane = lax.broadcasted_iota(jnp.int32, (code_ref.shape[0], rows), 1) + k * rows
-        part = dot32((lane == code_ref[...]).astype(BF16), line_ref[k])
+        target = source + k * own + jnp.where(source < own, 0, (pieces - 1) * own)
+        part = dot32((row == target).astype(BF16), line_ref[k])
         total = part if total is None else total + part
-    line = total.astype(BF16)
-    for place in range(out_ref.shape[0]):
-        out_ref[place] = line
-
-
-def extra_kernel(flag_ref, device_ref, row_ref, p0, p1, p2, p3, out_ref):
-    places, sub, _ = out_ref.shape
+    merged[...] = total.astype(BF16)
+    send_copies(merged, out_ref, done)
+
+
+def send_copies(merged, out_ref, done):
+    copies = [pltpu.make_async_copy(merged, out_ref.at[place], done.at[place]) for place in range(out_ref.shape[0])]
+    for copy in copies:
+        copy.start()
+    for copy in copies:
+        copy.wait()
+
+
+def extra_kernel(flag_ref, device_ref, row_ref, p0, p1, p2, p3, out_ref, merged, done):
+    sub = merged.shape[0]
     rows, half = p0.shape
     code = jnp.bitwise_and(device_ref[...] - flag_ref[2], 3) * rows + row_ref[...]
     total = None
@@ -57,16 +68,17 @@
         part = dot32((lane == code).astype(BF16), piece[...])
         total = part if total is None else total + part
     line = total.astype(BF16)
-    for place in range(places):
-        for b in range(line.shape[0] // sub):
-            out_ref[place, :, b * half : (b + 1) * half] = line[b * sub : (b + 1) * sub, :]
-
-
-def forward_kernel(flag_ref, normed_ref, plane_ref, pick_ref, picked_ref, kept_ref, given_ref, slope_ref, part):
+    for b in range(line.shape[0] // sub):
+        merged[:, b * half : (b + 1) * half] = line[b * sub : (b + 1) * sub, :]
+    send_copies(merged, out_ref, done)
+
+
+def forward_kernel(flag_ref, normed_ref, plane_ref, index_ref, picked_ref, kept_ref, given_ref, slope_ref, part):
     _, rows, hidden_dev = plane_ref.shape
     images, width = normed_ref.shape
     half_images = kept_ref.shape[0]
-    half = pick_ref.shape[1] // 2
+    solved = index_ref.shape[1]
+    half = solved // 2
     up_pre = dot32(normed_ref[...], plane_ref[:, : rows // 2, :].reshape(width, hidden_dev))
     activ, slope = gelu_parts(up_pre)
     slope_ref[...] = slope
@@ -75,12 +87,17 @@
     core = flag_ref[1]
     high = slope.astype(BF16)
     low = (slope - high.astype(F32)).astype(BF16)
-    gain = dot32(jnp.concatenate([high, low], axis=0), pick_ref[...])
-    gain = jnp.where(core == 0, (gain[:images] + gain[images:]) * picked_ref[...], 0.0)
+    pick = (lax.broadcasted_iota(jnp.int32, (hidden_dev, solved), 0) == index_ref[...]).astype(BF16)
+    gain = dot32(jnp.concatenate([high, low], axis=0), pick)
+    gain = jnp.where(core == 0, (gain[:images] + gain[images:]) * picked_ref[:, :solved], 0.0)
     for out, side, at in ((kept_ref, core, 0), (given_ref, 1 - core, half)):
-        out[:, :width] = part[pl.ds(pl.multiple_of(side * half_images, half_images), half_images), :]
-        out[:, width : width + half] = gain[:half_images, at : at + half]
-        out[:, width + half :] = gain[half_images:, at : at + half]
+        rows_here = pl.ds(pl.multiple_of(side * half_images, half_images), half_images)
+        for run in range(2):
+            base = run * (width // 2 + half)
+            out[:, base : base + width // 2] = part[rows_here, run * (width // 2) : (run + 1) * (width // 2)]
+            out[:, base + width // 2 : base + width // 2 + half] = gain[
+                run * half_images : (run + 1) * half_images, at : at + half
+            ]
 
 
 def split2(values):
@@ -126,10 +143,14 @@
     half = down0_ref.shape[1]
     logits = head_ref.shape[0] // 4
     first_core = flag_ref[1] == 0
-    mine, theirs = mine_ref[:, :width], theirs_ref[:, :width]
+    run = width // 2 + half
+    mine, theirs = (
+        jnp.concatenate([source[:, : width // 2], source[:, run : run + width // 2]], axis=1)
+        for source in (mine_ref, theirs_ref)
+    )
     for side, source in ((flag_ref[1], mine_ref), (1 - flag_ref[1], theirs_ref)):
-        mix_ref[side, :half_images, :] = source[:, width : width + half]
-        mix_ref[side, half_images:images, :] = source[:, width + half :]
+        mix_ref[side, :half_images, :] = source[:, width // 2 : run]
+        mix_ref[side, half_images:images, :] = source[:, run + width // 2 :]
     block = jnp.concatenate([jnp.where(first_core, mine, theirs), jnp.where(first_core, theirs, mine)], axis=0)
     centred = block - jnp.mean(block, axis=1, keepdims=True)
     inv_std = lax.rsqrt(jnp.mean(centred * centred, axis=1, keepdims=True) + 1e-06)
@@ -223,31 +244,28 @@
 
     both = jnp.concatenate([w_up, w_down.T], axis=0)
     line = gather_by_sends(both, "zl", 4)
-    row = np.arange(8 * own)
-    code = row % (4 * own) // own * (2 * own) + row // (4 * own) * own + row % own
     line = pl.pallas_call(
         weights_kernel,
         out_shape=jax.ShapeDtypeStruct((16, 8 * own, hidden_dev), BF16),
-        in_specs=[vmem] * 2,
-        out_specs=vmem,
-        compiler_params=LIMIT,
+        in_specs=[vmem],
+        out_specs=pl.BlockSpec(memory_space=pltpu.HBM),
+        scratch_shapes=[pltpu.VMEM((8 * own, hidden_dev), BF16), pltpu.SemaphoreType.DMA((16,))],
+        compiler_params=LARGE,
         name="merge_weights",
-    )(code.astype(np.int32)[:, None], line)
+    )(line)
     plane = lax.all_to_all(line, ("x", "y"), 0, 0)
 
-    later, panels_later, hidden_first, inputs_later, _ = lax.optimization_barrier(
-        (both[own:], panels, local_hidden[: 2 * panel], sub_inputs, line[0, :16, :128])
-    )
-    pick_first = one_hot(hidden_first, hidden_dev)
-    chosen = dot32(later, pick_first).astype(BF16)
-    block01 = panels_later[0][:, panel : 2 * panel]
-    other = lax.ppermute(jnp.concatenate([chosen[:, half:], block01], axis=0), "c", [(0, 1)])
-    payload = jnp.where(core == 0, jnp.concatenate([chosen[:, :half], block01], axis=0), other)
-    sent = [lax.ppermute(payload, "zh", [(0, k)]) for k in (1, 2, 3)]
-    payload = jnp.where(z_hi == 0, payload, sent[0] + sent[1] + sent[2])
+    pick_first = one_hot(local_hidden[: 2 * panel], hidden_dev)
+    chosen = dot32(both[own:], pick_first).astype(BF16)
+    block01 = panels[0][:, panel : 2 * panel]
+    chosen = [jnp.concatenate([chosen[:, at : at + half], block01], axis=0) for at in (0, half)]
+    payload = jnp.where(core == 0, chosen[0], lax.ppermute(chosen[1], "c", [(0, 1)]))
+    payload = jnp.where(z_hi == 1, lax.ppermute(payload, "zh", [(0, 1)]), payload)
+    payload = jnp.where(z_hi >= 2, lax.ppermute(payload, "zh", [(0, 3), (1, 2)]), payload)
 
     chunks = rows_dev // half
-    narrow = jnp.concatenate([panels_later.reshape(2 * panel_dev * chunks, half), payload], axis=0)
+    narrow = panels.reshape(2 * panel_dev * chunks, half)
+    narrow = jnp.concatenate([narrow, payload], axis=0)
     pieces = ring_pieces(narrow, "zl", 4)
     device, source = [], []
     for q in range(2):
@@ -261,13 +279,14 @@
         extra_kernel,
         out_shape=jax.ShapeDtypeStruct((16, 16, len(device) // 16 * half), BF16),
         in_specs=[smem] + [vmem] * 6,
-        out_specs=vmem,
-        compiler_params=LIMIT,
+        out_specs=pl.BlockSpec(memory_space=pltpu.HBM),
+        scratch_shapes=[pltpu.VMEM((16, len(device) // 16 * half), BF16), pltpu.SemaphoreType.DMA((16,))],
+        compiler_params=LARGE,
         name="merge_extra",
     )(flag, np.array(device, np.int32)[:, None], np.array(source, np.int32)[:, None], *pieces)
     extra = lax.all_to_all(extra, ("x", "y"), 0, 0)
 
-    picked = dot32(normed, one_hot(inputs_later, width))
+    picked = dot32(normed, one_hot(sub_inputs, width))
     kept, given, slope = pl.pallas_call(
         forward_kernel,
         out_shape=(
@@ -280,10 +299,18 @@
         scratch_shapes=[pltpu.VMEM((images, width), F32)],
         compiler_params=LIMIT,
         name="forward",
-    )(flag, normed, plane, pick_first, picked[:, : 2 * panel])
+    )(flag, normed, plane, local_hidden[None, : 2 * panel], picked)
     pair = kept + swap_core(given)
-    pair_sent = pair.astype(BF16)
-    peers = [lax.ppermute(pair_sent, "zh", [(i, (i + k) % 4) for i in range(4)]) for k in (2, 1, 3)]
+    run = width // 2 + half
+    is_block = lax.broadcasted_iota(jnp.int32, (images // 2, run), 1) < width // 2
+    routes = ([(i, i ^ 1) for i in range(4)], [(i, 3 - i) for i in range(4)])
+    runs = [pair[:, :run], pair[:, run:]]
+    near = [lax.ppermute(part.astype(BF16), "zh", route) for part, route in zip(runs, routes)]
+    runs = [
+        jnp.where(is_block, part + got.astype(F32), jnp.where(z_hi == first, got.astype(F32), part))
+        for part, got, first in zip(runs, near, (1, 3))
+    ]
+    far = [lax.ppermute(part.astype(BF16), "zh", route) for part, route in zip(runs, routes[::-1])]
 
     pick_own = one_hot(local_hidden, hidden_dev)
     down_t = plane[:, 4 * own :].reshape(width, hidden_dev)
@@ -293,13 +320,15 @@
     centred_head = head - jnp.mean(head, axis=0)
     head_parts = jnp.concatenate(split2(centred_head.T) + split2(head.T), axis=0)
 
-    peers = [peer.astype(F32) for peer in peers]
     mine = lax.dynamic_slice_in_dim(residual_in, core * (images // 2), images // 2, 0).astype(F32)
-    block = mine + ((pair + peers[0]) + (peers[1] + peers[2]))[:, :width]
-    solved_gain = [values[:, width:] for values in (pair, peers[1], peers[0], peers[2])]
-    gain = jnp.where(z_hi == 0, solved_gain[0], solved_gain[1])
-    gain = jnp.where(z_hi == 2, solved_gain[2], jnp.where(z_hi == 3, solved_gain[3], gain))
-    block = jnp.concatenate([block, gain], axis=1)
+    mine = jnp.pad(mine.reshape(images // 2, 2, width // 2), ((0, 0), (0, 0), (0, half)))
+    block = jnp.concatenate(
+        [
+            jnp.where(is_block, mine[:, k] + (runs[k] + far[k].astype(F32)), jnp.where(late, far[k].astype(F32), runs[k]))
+            for k, late in enumerate((z_hi >= 2, (z_hi == 1) | (z_hi == 2)))
+        ],
+        axis=1,
+    )
     block_pair = swap_core(block)
 
     down_mine = pl.pallas_call(

time: 184 us -> 178 us (0.967)
  the two profiles are of different devices: /device:TPU:32 before, /device:TPU:1 now
where the time goes in v3:
time: 178 us; the launch traced here: 177 us
  starting transfers between devices  74.9 us (42%)
  waiting for transfers between devices  67.9 us (38%)
  Pallas kernels  15.1 us (8%)
  matrix products  6.58 us (4%)
  local copies, waits for them, and re-layouts  6.09 us (3%)
  other arithmetic  5.71 us (3%)
    all_to_all x1, waiting for transfers between devices, body(): plane = lax.all_to_all(line, ('x', 'y'), 0, 0)  24.5 us
    ppermute x4, starting transfers between devices, body(): lax.ppermute(part.astype(BF16), 'zh', route)  22.3 us
    all_to_all x1, waiting for transfers between devices, body(): extra = lax.all_to_all(extra, ('x', 'y'), 0, 0)  18.8 us
    ppermute x3, starting transfers between devices, swap_core(): return lax.ppermute(values, 'c', [(0, 1), (1, 0)])  17.5 us
    ppermute x4, waiting for transfers between devices, body(): lax.ppermute(part.astype(BF16), 'zh', route)  12.4 us
    ppermute x3, starting transfers between devices, ring_pieces(): lax.ppermute(shard, axis, [(i, (i - k) % count) for i in range(count)])  9.5 us
    ppermute x1, waiting for transfers between devices, body(): lax.ppermute(chosen[1], 'c', [(0, 1)])  7.48 us
    all_to_all x1, starting transfers between devices, body(): extra = lax.all_to_all(extra, ('x', 'y'), 0, 0)  6.77 us
  transfers between devices with their start and end apart: 16, of which 10 were waited for; matrix products, arithmetic and copies ran while one was open for 7% of the time, Pallas kernels for 5%

profile of v3, /device:TPU:1, one launch (start us, length us, event | category | flops | bytes accessed | tf_op | source)
XLA Modules:
  0.0 176.7 jit_solution(4734329614780520917)
XLA Ops:
  3.9 7.5 %collective-permute-done.6 = bf16[24,256]{1,0:T(8,128)(2,1)S(1)} collective-permute-done((bf16[24,256]{1,0:T(8,128)(2,1)S(1)}, bf16[24,256]{1,0:T(8,128)(2,1)S(1)}, u32[]{:S(2)}, u32[]{:S(2)}) %collective-permute-start.6) | collective-permute-done | bytes 12320 | tf_op jit(solution)/shard_map/ppermute | solution.py:262
  11.3 3.9 %collective-permute-start.7 = (bf16[24,256]{1,0:T(8,128)(2,1)S(1)}, bf16[24,256]{1,0:T(8,128)(2,1)S(1)}, u32[]{:S(2)}, u32[]{:S(2)}) collective-permute-start(bf16[24,256]{1,0:T(8,128)(2,1)S(1)} %fusion.27), channel_id=1, source_target_pairs={{0,2},{1,3},{8,10},{9,11},{16,18},{17,19},{24,26},{25,27},{32,34},... | collective-permute-start | bytes 36872 | tf_op jit(solution)/shard_map/ppermute | solution.py:263
  16.8 5.6 %all-to-all-start = ((bf16[4,40,640]{2,1,0:T(8,128)(2,1)}), bf16[4,40,640]{2,1,0:T(8,128)(2,1)S(1)}, u32[]{:S(2)}, u32[]{:S(2)}) async-start(bf16[4,40,640]{2,1,0:T(8,128)(2,1)} %broadcast_in_dim.4), calls=%async_computation | async-start | bytes 409600 | tf_op jit(solution)/shard_map/all_to_all | solution.py:30
  25.3 5.3 %collective-permute-start.9 = (bf16[56,256]{1,0:T(8,128)(2,1)S(1)}, bf16[56,256]{1,0:T(8,128)(2,1)S(1)}, u32[]{:S(2)}, u32[]{:S(2)}) collective-permute-start(bf16[56,256]{1,0:T(8,128)(2,1)S(1)} %pad_maximum_fusion.3.p0), channel_id=1, source_target_pairs={{0,24},{8,0},{16,8},{24,16},{1,25},{9,1},{17,9},{25,17},{2,26},{10... | collective-permute-start | bytes 86024 | tf_op jit(solution)/shard_map/ppermute | solution.py:35
  32.6 2.2 %collective-permute-start.11 = (bf16[56,256]{1,0:T(8,128)(2,1)S(1)}, bf16[56,256]{1,0:T(8,128)(2,1)S(1)}, u32[]{:S(2)}, u32[]{:S(2)}) collective-permute-start(bf16[56,256]{1,0:T(8,128)(2,1)S(1)} %pad_maximum_fusion.3.p0), channel_id=1, source_target_pairs={{0,8},{8,16},{16,24},{24,0},{1,9},{9,17},{17,25},{25,1},{2,10},{10... | collective-permute-start | bytes 86024 | tf_op jit(solution)/shard_map/ppermute | solution.py:35
  36.2 2.8 %collective-permute-done.11.p3 = bf16[56,256]{1,0:T(8,128)(2,1)S(1)} collective-permute-done((bf16[56,256]{1,0:T(8,128)(2,1)S(1)}, bf16[56,256]{1,0:T(8,128)(2,1)S(1)}, u32[]{:S(2)}, u32[]{:S(2)}) %collective-permute-start.11) | collective-permute-done | bytes 28704 | tf_op jit(solution)/shard_map/ppermute | solution.py:35
  39.6 2.7 %merge_extra.1 = bf16[16,16,3584]{2,1,0:T(8,128)(2,1)} custom-call(s32[3]{0:T(128)} %pad_add_fusion.flag_ref, s32[224,1]{1,0:T(8,128)} %constant.38.clone.device_ref, s32[224,1]{1,0:T(8,128)} %constant.39.clone.row_ref, bf16[56,256]{1,0:T(8,128)(2,1)} %copy-done.12, bf16[56,256]{1,0:T(8,128)(2,1)} %copy-done.14, bf16[56,256]{1,0:T(8,128)(2,1)} %copy-done.15, ...), custom_call_target="tpu_custom_call" | custom-call | tf_op jit(solution)/shard_map/merge_extra/pallas_call | solution.py:278
  42.3 6.8 %all-to-all-start.2 = ((bf16[16,16,3584]{2,1,0:T(8,128)(2,1)}), bf16[16,16,3584]{2,1,0:T(8,128)(2,1)S(1)}, u32[]{:S(2)}, u32[]{:S(2)}) async-start(bf16[16,16,3584]{2,1,0:T(8,128)(2,1)} %merge_extra.1), calls=%async_computation.2 | async-start | bytes 3670016 | tf_op jit(solution)/shard_map/all_to_all | solution.py:287
  49.1 3.1 %merge_weights.1 = bf16[16,160,640]{2,1,0:T(8,128)(2,1)} custom-call(bf16[4,40,640]{2,1,0:T(8,128)(2,1)} %copy-done.11), custom_call_target="tpu_custom_call" | custom-call | tf_op jit(solution)/shard_map/merge_weights/pallas_call | solution.py:247
  52.2 18.8 %all-to-all-done.2.extra_ref = bf16[16,16,3584]{2,1,0:T(8,128)(2,1)S(1)} async-done(((bf16[16,16,3584]{2,1,0:T(8,128)(2,1)}), bf16[16,16,3584]{2,1,0:T(8,128)(2,1)S(1)}, u32[]{:S(2)}, u32[]{:S(2)}) %all-to-all-start.2) | async-done | bytes 1835040 | tf_op jit(solution)/shard_map/all_to_all | solution.py:287
  72.2 5.8 %all-to-all-start.1 = ((bf16[16,160,640]{2,1,0:T(8,128)(2,1)}), bf16[16,160,640]{2,1,0:T(8,128)(2,1)S(1)}, u32[]{:S(2)}, u32[]{:S(2)}) async-start(bf16[16,160,640]{2,1,0:T(8,128)(2,1)} %merge_weights.1), calls=%async_computation.1 | async-start | bytes 6553600 | tf_op jit(solution)/shard_map/all_to_all | solution.py:256
  81.5 2.6 %fusion.6.picked_ref = f32[64,1024]{1,0:T(8,128)} fusion(bf16[64,1280]{1,0:T(8,128)(2,1)} %normed_ref.1, s32[1024]{0:T(1024)S(1)} %copy-done.17), kind=kOutput, calls=%fused_computation.10 | convolution fusion | flops 169082880 | bytes 430080 | tf_op jit(solution)/shard_map/dot_general | solution.py:109
  85.0 5.3 %collective-permute-start.12 = (bf16[1280,256]{1,0:T(8,128)(2,1)}, bf16[1280,256]{1,0:T(8,128)(2,1)}, u32[]{:S(2)}, u32[]{:S(2)}) collective-permute-start(bf16[1280,256]{1,0:T(8,128)(2,1)} %solved.1.down0_ref), channel_id=1, source_target_pairs={{0,1},{1,0},{2,3},{3,2},{4,5},{5,4},{6,7},{7,6},{8,9},{9,8},{10,11... | collective-permute-start | bytes 1966088 | tf_op jit(solution)/shard_map/ppermute | solution.py:25
  90.3 24.5 %all-to-all-done.1.plane_ref = bf16[16,160,640]{2,1,0:T(8,128)(2,1)S(1)} async-done(((bf16[16,160,640]{2,1,0:T(8,128)(2,1)}), bf16[16,160,640]{2,1,0:T(8,128)(2,1)S(1)}, u32[]{:S(2)}, u32[]{:S(2)}) %all-to-all-start.1) | async-done | bytes 3276832 | tf_op jit(solution)/shard_map/all_to_all | solution.py:256
  118.3 9.2 %collective-permute-start = (f32[32,1792]{1,0:T(8,128)S(1)}, f32[32,1792]{1,0:T(8,128)S(1)}, u32[]{:S(2)}, u32[]{:S(2)}) collective-permute-start(f32[32,1792]{1,0:T(8,128)S(1)} %get-tuple-element.14), channel_id=1, source_target_pairs={{0,1},{1,0},{2,3},{3,2},{4,5},{5,4},{6,7},{7,6},{8,9},{9,8},{10,11... | collective-permute-start | bytes 688136 | tf_op jit(solution)/shard_map/ppermute | solution.py:25
  127.7 2.3 %convolution_convert_fusion.down_ref = bf16[1280,1024]{1,0:T(8,128)(2,1)S(1)} fusion(bf16[1280,640]{1,0:T(8,128)(2,1)S(1)} %bitcast.34, s32[1024]{0:T(1024)S(1)} %broadcast_subtract_fusion), kind=kOutput, calls=%fused_computation.2 | convolution fusion | flops 1679687680 | bytes 4263936 | tf_op jit(solution)/shard_map/dot_general | solution.py:109
  130.0 7.0 %collective-permute-start.1 = (bf16[32,896]{1,0:T(8,128)(2,1)S(1)}, bf16[32,896]{1,0:T(8,128)(2,1)S(1)}, u32[]{:S(2)}, u32[]{:S(2)}) collective-permute-start(bf16[32,896]{1,0:T(8,128)(2,1)S(1)} %get-tuple-element.23), channel_id=1, source_target_pairs={{0,2},{2,0},{4,6},{6,4},{1,3},{3,1},{5,7},{7,5},{8,10},{10,8},{12,... | collective-permute-start | bytes 172040 | tf_op jit(solution)/shard_map/ppermute | solution.py:308
  137.0 5.3 %collective-permute-start.3 = (bf16[32,896]{1,0:T(8,128)(2,1)S(1)}, bf16[32,896]{1,0:T(8,128)(2,1)S(1)}, u32[]{:S(2)}, u32[]{:S(2)}) collective-permute-start(bf16[32,896]{1,0:T(8,128)(2,1)S(1)} %get-tuple-element.24), channel_id=1, source_target_pairs={{0,6},{2,4},{4,2},{6,0},{1,7},{3,5},{5,3},{7,1},{8,14},{10,12},{12... | collective-permute-start | bytes 172040 | tf_op jit(solution)/shard_map/ppermute | solution.py:308
  142.6 4.8 %collective-permute-done.3 = bf16[32,896]{1,0:T(8,128)(2,1)S(1)} collective-permute-done((bf16[32,896]{1,0:T(8,128)(2,1)S(1)}, bf16[32,896]{1,0:T(8,128)(2,1)S(1)}, u32[]{:S(2)}, u32[]{:S(2)}) %collective-permute-start.3) | collective-permute-done | bytes 57376 | tf_op jit(solution)/shard_map/ppermute | solution.py:308
  147.5 8.2 %collective-permute-start.2 = (bf16[32,896]{1,0:T(8,128)(2,1)S(1)}, bf16[32,896]{1,0:T(8,128)(2,1)S(1)}, u32[]{:S(2)}, u32[]{:S(2)}) collective-permute-start(bf16[32,896]{1,0:T(8,128)(2,1)S(1)} %get-tuple-element.21), channel_id=1, source_target_pairs={{0,6},{2,4},{4,2},{6,0},{1,7},{3,5},{5,3},{7,1},{8,14},{10,12},{12... | collective-permute-start | bytes 172040 | tf_op jit(solution)/shard_map/ppermute | solution.py:313
  158.3 7.2 %collective-permute-done.4 = bf16[32,896]{1,0:T(8,128)(2,1)S(1)} collective-permute-done((bf16[32,896]{1,0:T(8,128)(2,1)S(1)}, bf16[32,896]{1,0:T(8,128)(2,1)S(1)}, u32[]{:S(2)}, u32[]{:S(2)}) %collective-permute-start.4) | collective-permute-done | bytes 57376 | tf_op jit(solution)/shard_map/ppermute | solution.py:313
  165.7 3.0 %collective-permute-start.5 = (f32[32,1792]{1,0:T(8,128)S(1)}, f32[32,1792]{1,0:T(8,128)S(1)}, u32[]{:S(2)}, u32[]{:S(2)}) collective-permute-start(f32[32,1792]{1,0:T(8,128)S(1)} %pad_maximum_fusion.mine_ref), channel_id=1, source_target_pairs={{0,1},{1,0},{2,3},{3,2},{4,5},{5,4},{6,7},{7,6},{8,9},{9,8},{10,11... | collective-permute-start | bytes 688136 | tf_op jit(solution)/shard_map/ppermute | solution.py:25
  169.8 2.4 %middle.1 = (f32[64,1]{1,0:T(8,128)S(1)}, f32[64,16]{1,0:T(8,128)S(1)}, f32[80,1024]{1,0:T(8,128)S(1)}, f32[2,144,256]{2,1,0:T(8,128)S(1)}) custom-call(s32[3]{0:T(128)S(1)} %copy-done.9, f32[32,1792]{1,0:T(8,128)S(1)} %pad_maximum_fusion.mine_ref, f32[32,1792]{1,0:T(8,128)S(1)} %collective-permute-done.5.theirs_ref, bf16[64,1280]{1,0:T(8,128)(2,1)S(1)} %copy-done.6, ...), custom_call_target="tpu_custom_call" | custom-call | tf_op jit(solution)/shard_map/middle/pallas_call | solution.py:343
  172.2 4.5 %last.1 = bf16[64,16,1024]{2,1,0:T(8,128)(2,1)} custom-call(s32[3]{0:T(128)S(1)} %copy-done.9, f32[64,1024]{1,0:T(8,128)S(1)} %fusion.10.gain_ref, f32[64,1]{1,0:T(8,128)S(1)} %get-tuple-element.15.inv_ref, f32[64,16]{1,0:T(8,128)S(1)} %get-tuple-element.16.share_ref, f32[80,1024]{1,0:T(8,128)S(1)} %get-tuple-element.17.own_ref, ...), custom_call_target="tpu_custom_call" | custom-call | tf_op jit(solution)/shard_map/last/pallas_call | solution.py:356
  (84 shorter events, 25.3 us)
Async XLA Ops:
  0.0 78.1 %copy-start = (bf16[64,1280]{1,0:T(8,128)(2,1)S(1)}, bf16[64,1280]{1,0:T(8,128)(2,1)}, u32[]{:S(2)}) copy-start(bf16[64,1280]{1,0:T(8,128)(2,1)} %param.13) | copy-start | bytes 491524
  2.5 8.8 %collective-permute-start.6 = (bf16[24,256]{1,0:T(8,128)(2,1)S(1)}, bf16[24,256]{1,0:T(8,128)(2,1)S(1)}, u32[]{:S(2)}, u32[]{:S(2)}) collective-permute-start(bf16[24,256]{1,0:T(8,128)(2,1)S(1)} %pad_maximum_fusion.4), channel_id=1, source_target_pairs={{0,1},{2,3},{4,5},{6,7},{8,9},{10,11},{12,13},{14,15},{16,17},{18,... | collective-permute-start | bytes 36872 | tf_op jit(solution)/shard_map/ppermute | solution.py:262
  11.3 11.0 %collective-permute-start.7 = (bf16[24,256]{1,0:T(8,128)(2,1)S(1)}, bf16[24,256]{1,0:T(8,128)(2,1)S(1)}, u32[]{:S(2)}, u32[]{:S(2)}) collective-permute-start(bf16[24,256]{1,0:T(8,128)(2,1)S(1)} %fusion.27), channel_id=1, source_target_pairs={{0,2},{1,3},{8,10},{9,11},{16,18},{17,19},{24,26},{25,27},{32,34},... | collective-permute-start | bytes 36872 | tf_op jit(solution)/shard_map/ppermute | solution.py:263
  16.8 25.5 %all-to-all-start = ((bf16[4,40,640]{2,1,0:T(8,128)(2,1)}), bf16[4,40,640]{2,1,0:T(8,128)(2,1)S(1)}, u32[]{:S(2)}, u32[]{:S(2)}) async-start(bf16[4,40,640]{2,1,0:T(8,128)(2,1)} %broadcast_in_dim.4), calls=%async_computation | async-start | bytes 409600 | tf_op jit(solution)/shard_map/all_to_all | solution.py:30
  22.4 2.9 %collective-permute-start.8 = (bf16[24,256]{1,0:T(8,128)(2,1)S(1)}, bf16[24,256]{1,0:T(8,128)(2,1)S(1)}, u32[]{:S(2)}, u32[]{:S(2)}) collective-permute-start(bf16[24,256]{1,0:T(8,128)(2,1)S(1)} %broadcast_select_fusion), channel_id=1, source_target_pairs={{0,6},{2,4},{1,7},{3,5},{8,14},{10,12},{9,15},{11,13},{16,22},{18,... | collective-permute-start | bytes 36872 | tf_op jit(solution)/shard_map/ppermute | solution.py:264
  25.3 13.7 %copy-start.12 = (bf16[56,256]{1,0:T(8,128)(2,1)}, bf16[56,256]{1,0:T(8,128)(2,1)S(1)}, u32[]{:S(2)}) copy-start(bf16[56,256]{1,0:T(8,128)(2,1)S(1)} %pad_maximum_fusion.3.p0) | copy-start | bytes 86020
  25.3 10.1 %collective-permute-start.9 = (bf16[56,256]{1,0:T(8,128)(2,1)S(1)}, bf16[56,256]{1,0:T(8,128)(2,1)S(1)}, u32[]{:S(2)}, u32[]{:S(2)}) collective-permute-start(bf16[56,256]{1,0:T(8,128)(2,1)S(1)} %pad_maximum_fusion.3.p0), channel_id=1, source_target_pairs={{0,24},{8,0},{16,8},{24,16},{1,25},{9,1},{17,9},{25,17},{2,26},{10... | collective-permute-start | bytes 86024 | tf_op jit(solution)/shard_map/ppermute | solution.py:35
  30.7 5.5 %collective-permute-start.10 = (bf16[56,256]{1,0:T(8,128)(2,1)S(1)}, bf16[56,256]{1,0:T(8,128)(2,1)S(1)}, u32[]{:S(2)}, u32[]{:S(2)}) collective-permute-start(bf16[56,256]{1,0:T(8,128)(2,1)S(1)} %pad_maximum_fusion.3.p0), channel_id=1, source_target_pairs={{0,16},{8,24},{16,0},{24,8},{1,17},{9,25},{17,1},{25,9},{2,18},{10... | collective-permute-start | bytes 86024 | tf_op jit(solution)/shard_map/ppermute | solution.py:35
  32.6 6.4 %collective-permute-start.11 = (bf16[56,256]{1,0:T(8,128)(2,1)S(1)}, bf16[56,256]{1,0:T(8,128)(2,1)S(1)}, u32[]{:S(2)}, u32[]{:S(2)}) collective-permute-start(bf16[56,256]{1,0:T(8,128)(2,1)S(1)} %pad_maximum_fusion.3.p0), channel_id=1, source_target_pairs={{0,8},{8,16},{16,24},{24,0},{1,9},{9,17},{17,25},{25,1},{2,10},{10... | collective-permute-start | bytes 86024 | tf_op jit(solution)/shard_map/ppermute | solution.py:35
  42.3 28.7 %all-to-all-start.2 = ((bf16[16,16,3584]{2,1,0:T(8,128)(2,1)}), bf16[16,16,3584]{2,1,0:T(8,128)(2,1)S(1)}, u32[]{:S(2)}, u32[]{:S(2)}) async-start(bf16[16,16,3584]{2,1,0:T(8,128)(2,1)} %merge_extra.1), calls=%async_computation.2 | async-start | bytes 3670016 | tf_op jit(solution)/shard_map/all_to_all | solution.py:287
  52.2 26.0 %copy-start.13 = (f32[1280]{0:T(1024)S(1)}, f32[1280]{0:T(1024)}, u32[]{:S(2)}) copy-start(f32[1280]{0:T(1024)} %param.16) | copy-start | bytes 15364
  52.2 29.3 %copy-start.17 = (s32[1024]{0:T(1024)S(1)}, s32[1024]{0:T(1024)}, u32[]{:S(2)}) copy-start(s32[1024]{0:T(1024)} %param.18) | copy-start | bytes 12292
  72.2 42.6 %all-to-all-start.1 = ((bf16[16,160,640]{2,1,0:T(8,128)(2,1)}), bf16[16,160,640]{2,1,0:T(8,128)(2,1)S(1)}, u32[]{:S(2)}, u32[]{:S(2)}) async-start(bf16[16,160,640]{2,1,0:T(8,128)(2,1)} %merge_weights.1), calls=%async_computation.1 | async-start | bytes 6553600 | tf_op jit(solution)/shard_map/all_to_all | solution.py:256
  79.2 35.6 %copy-start.9 = (s32[3]{0:T(128)S(1)}, s32[3]{0:T(128)}, u32[]{:S(2)}) copy-start(s32[3]{0:T(128)} %pad_add_fusion.flag_ref) | copy-start | bytes 40
  85.0 83.8 %collective-permute-start.12 = (bf16[1280,256]{1,0:T(8,128)(2,1)}, bf16[1280,256]{1,0:T(8,128)(2,1)}, u32[]{:S(2)}, u32[]{:S(2)}) collective-permute-start(bf16[1280,256]{1,0:T(8,128)(2,1)} %solved.1.down0_ref), channel_id=1, source_target_pairs={{0,1},{1,0},{2,3},{3,2},{4,5},{5,4},{6,7},{7,6},{8,9},{9,8},{10,11... | collective-permute-start | bytes 1966088 | tf_op jit(solution)/shard_map/ppermute | solution.py:25
  118.3 11.7 %collective-permute-start = (f32[32,1792]{1,0:T(8,128)S(1)}, f32[32,1792]{1,0:T(8,128)S(1)}, u32[]{:S(2)}, u32[]{:S(2)}) collective-permute-start(f32[32,1792]{1,0:T(8,128)S(1)} %get-tuple-element.14), channel_id=1, source_target_pairs={{0,1},{1,0},{2,3},{3,2},{4,5},{5,4},{6,7},{7,6},{8,9},{9,8},{10,11... | collective-permute-start | bytes 688136 | tf_op jit(solution)/shard_map/ppermute | solution.py:25
  129.9 35.6 %copy-start.10 = (f32[32,2,896]{2,0,1:T(8,128)S(1)}, f32[32,2,896]{2,0,1:T(8,128)}, u32[]{:S(2)}) copy-start(f32[32,2,896]{2,0,1:T(8,128)} %pad_convert_fusion) | copy-start | bytes 688132
  129.9 38.7 %copy-start.5 = (f32[64,1024]{1,0:T(8,128)S(1)}, f32[64,1024]{1,0:T(8,128)}, u32[]{:S(2)}) copy-start(f32[64,1024]{1,0:T(8,128)} %fusion.6.picked_ref) | copy-start | bytes 786436
  130.0 39.8 %copy-start.6 = (bf16[64,1280]{1,0:T(8,128)(2,1)S(1)}, bf16[64,1280]{1,0:T(8,128)(2,1)}, u32[]{:S(2)}) copy-start(bf16[64,1280]{1,0:T(8,128)(2,1)} %pad_maximum_fusion.1.head_ref) | copy-start | bytes 491524
  130.0 12.6 %collective-permute-start.1 = (bf16[32,896]{1,0:T(8,128)(2,1)S(1)}, bf16[32,896]{1,0:T(8,128)(2,1)S(1)}, u32[]{:S(2)}, u32[]{:S(2)}) collective-permute-start(bf16[32,896]{1,0:T(8,128)(2,1)S(1)} %get-tuple-element.23), channel_id=1, source_target_pairs={{0,2},{2,0},{4,6},{6,4},{1,3},{3,1},{5,7},{7,5},{8,10},{10,8},{12,... | collective-permute-start | bytes 172040 | tf_op jit(solution)/shard_map/ppermute | solution.py:308
  137.0 10.5 %collective-permute-start.3 = (bf16[32,896]{1,0:T(8,128)(2,1)S(1)}, bf16[32,896]{1,0:T(8,128)(2,1)S(1)}, u32[]{:S(2)}, u32[]{:S(2)}) collective-permute-start(bf16[32,896]{1,0:T(8,128)(2,1)S(1)} %get-tuple-element.24), channel_id=1, source_target_pairs={{0,6},{2,4},{4,2},{6,0},{1,7},{3,5},{5,3},{7,1},{8,14},{10,12},{12... | collective-permute-start | bytes 172040 | tf_op jit(solution)/shard_map/ppermute | solution.py:308
  147.5 10.8 %collective-permute-start.2 = (bf16[32,896]{1,0:T(8,128)(2,1)S(1)}, bf16[32,896]{1,0:T(8,128)(2,1)S(1)}, u32[]{:S(2)}, u32[]{:S(2)}) collective-permute-start(bf16[32,896]{1,0:T(8,128)(2,1)S(1)} %get-tuple-element.21), channel_id=1, source_target_pairs={{0,6},{2,4},{4,2},{6,0},{1,7},{3,5},{5,3},{7,1},{8,14},{10,12},{12... | collective-permute-start | bytes 172040 | tf_op jit(solution)/shard_map/ppermute | solution.py:313
  155.7 9.8 %collective-permute-start.4 = (bf16[32,896]{1,0:T(8,128)(2,1)S(1)}, bf16[32,896]{1,0:T(8,128)(2,1)S(1)}, u32[]{:S(2)}, u32[]{:S(2)}) collective-permute-start(bf16[32,896]{1,0:T(8,128)(2,1)S(1)} %get-tuple-element.22), channel_id=1, source_target_pairs={{0,2},{2,0},{4,6},{6,4},{1,3},{3,1},{5,7},{7,5},{8,10},{10,8},{12,... | collective-permute-start | bytes 172040 | tf_op jit(solution)/shard_map/ppermute | solution.py:313
  165.7 4.1 %collective-permute-start.5 = (f32[32,1792]{1,0:T(8,128)S(1)}, f32[32,1792]{1,0:T(8,128)S(1)}, u32[]{:S(2)}, u32[]{:S(2)}) collective-permute-start(f32[32,1792]{1,0:T(8,128)S(1)} %pad_maximum_fusion.mine_ref), channel_id=1, source_target_pairs={{0,1},{1,0},{2,3},{3,2},{4,5},{5,4},{6,7},{7,6},{8,9},{9,8},{10,11... | collective-permute-start | bytes 688136 | tf_op jit(solution)/shard_map/ppermute | solution.py:25
  (10 other events, 35.9 us)

commit v4 on v3

--- a/solution.py
+++ b/solution.py
@@ -10,7 +10,7 @@
 TENSOR = ("zh", "c")
 F32 = jnp.float32
 BF16 = jnp.bfloat16
-STEP = 32
+STEP = 16
 LARGE = pltpu.CompilerParams(vmem_limit_bytes=60 * 1024 * 1024)
 LIMIT = pltpu.CompilerParams(vmem_limit_bytes=20 * 1024 * 1024)
 
@@ -185,46 +185,52 @@
     write(down1_ref, put_theirs)
 
 
-def last_kernel(flag_ref, gain_ref, inv_ref, share_ref, own_ref, mix_ref, inverse_ref, extra_ref, out_ref):
-    images = gain_ref.shape[0]
+def last_kernel(
+    flag_ref, gain_ref, inv_ref, share_ref, own_ref, mix_ref, inverse_ref, extra_ref, out_ref, result, done
+):
+    images, rows_dev = gain_ref.shape
     logits = share_ref.shape[1]
     panel = inverse_ref.shape[1]
-    first_image = pl.multiple_of(pl.program_id(0) * STEP, STEP)
-    here = pl.ds(first_image, STEP)
-    inv_std = inv_ref[here, :]
     diagonal = lax.broadcasted_iota(jnp.int32, (1, logits, logits), 1) == lax.broadcasted_iota(
         jnp.int32, (1, logits, logits), 2
     )
-    share = jnp.sum(jnp.where(diagonal, share_ref[here, :][:, None, :], 0.0), axis=2, keepdims=True)
-
-    def jacobian(gain, along, head):
-        scale = gain * inv_std
-        values = scale[:, None, :] * (head[None] - share * along[:, None, :])
-        return values.reshape(STEP * logits, values.shape[2])
-
-    def solved_side(side):
-        along = mix_ref[side, pl.ds(images + first_image, STEP), :]
-        return jacobian(mix_ref[side, here, :], along, mix_ref[side, 2 * images : 2 * images + logits, :])
+    panel_01 = extra_ref[:, :, extra_ref.shape[2] - panel :].reshape(panel, panel)
+    panel_0 = extra_ref[:, :, :rows_dev].reshape(panel, rows_dev)
+    panel_1 = extra_ref[:, :, rows_dev : 2 * rows_dev].reshape(panel, rows_dev)
 
     def inverted(values, inverse):
         high = values.astype(BF16)
         low = (values - high.astype(F32)).astype(BF16)
         return (dot_t(high, inverse) + dot_t(low, inverse)).astype(BF16)
 
-    first = inverted(solved_side(0), inverse_ref[0])
-    rows_dev = gain_ref.shape[1]
-    panel_01 = extra_ref[:, :, extra_ref.shape[2] - panel :].reshape(panel, panel)
-    second = inverted(solved_side(1) - dot32(first, panel_01), inverse_ref[1])
-    own = jacobian(gain_ref[here, :], own_ref[here, :], own_ref[images : images + logits, :])
-    panel_0 = extra_ref[:, :, :rows_dev].reshape(panel, rows_dev)
-    panel_1 = extra_ref[:, :, rows_dev : 2 * rows_dev].reshape(panel, rows_dev)
-    below = (own - (dot32(first, panel_0) + dot32(second, panel_1))).astype(BF16)
-    out_ref[...] = below.reshape(out_ref.shape)
-
-    @pl.when(flag_ref[0] == 1)
-    def _():
-        out_ref[:, :, :panel] = first.reshape(STEP, logits, panel)
-        out_ref[:, :, panel : 2 * panel] = second.reshape(STEP, logits, panel)
+    copies = []
+    for step in range(images // STEP):
+        here = slice(step * STEP, (step + 1) * STEP)
+        inv_std = inv_ref[here, :]
+        share = jnp.sum(jnp.where(diagonal, share_ref[here, :][:, None, :], 0.0), axis=2, keepdims=True)
+
+        def jacobian(gain, along, head):
+            scale = gain * inv_std
+            values = scale[:, None, :] * (head[None] - share * along[:, None, :])
+            return values.reshape(STEP * logits, values.shape[2])
+
+        def solved_side(side):
+            along = mix_ref[side, images + step * STEP : images + (step + 1) * STEP, :]
+            return jacobian(mix_ref[side, here, :], along, mix_ref[side, 2 * images : 2 * images + logits, :])
+
+        first = inverted(solved_side(0), inverse_ref[0])
+        second = inverted(solved_side(1) - dot32(first, panel_01), inverse_ref[1])
+        own = jacobian(gain_ref[here, :], own_ref[here, :], own_ref[images : images + logits, :])
+        below = (own - (dot32(first, panel_0) + dot32(second, panel_1))).astype(BF16)
+        holder = flag_ref[0] == 1
+        top = below[:, : 2 * panel]
+        top = jnp.where(holder, jnp.concatenate([first, second], axis=1), top)
+        result[here, :, : 2 * panel] = top.reshape(STEP, logits, 2 * panel)
+        result[here, :, 2 * panel :] = below[:, 2 * panel :].reshape(STEP, logits, rows_dev - 2 * panel)
+        copies.append(pltpu.make_async_copy(result.at[here], out_ref.at[here], done.at[step]))
+        copies[-1].start()
+    for copy in copies:
+        copy.wait()
 
 
 def body(normed, residual_in, w_up, w_down, final_gain, head_cols, sub_inputs, sub_hidden, panels, inverses):
@@ -355,10 +361,13 @@
     )(flag, block, block_pair, head_parts, down_own, down_mine, down_theirs)
     return pl.pallas_call(
         last_kernel,
-        grid=(images // STEP,),
         out_shape=jax.ShapeDtypeStruct((images, logits, rows_dev), BF16),
         in_specs=[smem] + [vmem] * 7,
-        out_specs=pl.BlockSpec((STEP, logits, rows_dev), lambda i: (i, 0, 0)),
+        out_specs=pl.BlockSpec(memory_space=pltpu.HBM),
+        scratch_shapes=[
+            pltpu.VMEM((images, logits, rows_dev), BF16),
+            pltpu.SemaphoreType.DMA((images // STEP,)),
+        ],
         compiler_params=LIMIT,
         name="last",
     )(flag, gain_own, inv_std, share, own_products, mix, inverses, extra)

time: 178 us -> 178 us (level)
  no operation moved by 1% of the time
where the time goes in v4:
time: 178 us; the launch traced here: 177 us
  starting transfers between devices  74.9 us (42%)
  waiting for transfers between devices  67.9 us (38%)
  Pallas kernels  15.4 us (9%)
  matrix products  6.58 us (4%)
  local copies, waits for them, and re-layouts  6.09 us (3%)
  other arithmetic  5.71 us (3%)
    all_to_all x1, waiting for transfers between devices, body(): plane = lax.all_to_all(line, ('x', 'y'), 0, 0)  24.5 us
    ppermute x4, starting transfers between devices, body(): lax.ppermute(part.astype(BF16), 'zh', route)  22.3 us
    all_to_all x1, waiting for transfers between devices, body(): extra = lax.all_to_all(extra, ('x', 'y'), 0, 0)  18.8 us
    ppermute x3, starting transfers between devices, swap_core(): return lax.ppermute(values, 'c', [(0, 1), (1, 0)])  17.5 us
    ppermute x4, waiting for transfers between devices, body(): lax.ppermute(part.astype(BF16), 'zh', route)  12.4 us
    ppermute x3, starting transfers between devices, ring_pieces(): lax.ppermute(shard, axis, [(i, (i - k) % count) for i in range(count)])  9.5 us
    ppermute x1, waiting for transfers between devices, body(): lax.ppermute(chosen[1], 'c', [(0, 1)])  7.48 us
    all_to_all x1, starting transfers between devices, body(): extra = lax.all_to_all(extra, ('x', 'y'), 0, 0)  6.77 us
  transfers between devices with their start and end apart: 16, of which 10 were waited for; matrix products, arithmetic and copies ran while one was open for 7% of the time, Pallas kernels for 5%

profile of v4, /device:TPU:1, one launch (start us, length us, event | category | flops | bytes accessed | tf_op | source)
XLA Modules:
  0.0 177.0 jit_solution(12149994986837572761)
XLA Ops:
  3.9 7.5 %collective-permute-done.6 = bf16[24,256]{1,0:T(8,128)(2,1)S(1)} collective-permute-done((bf16[24,256]{1,0:T(8,128)(2,1)S(1)}, bf16[24,256]{1,0:T(8,128)(2,1)S(1)}, u32[]{:S(2)}, u32[]{:S(2)}) %collective-permute-start.6) | collective-permute-done | bytes 12320 | tf_op jit(solution)/shard_map/ppermute | solution.py:268
  11.3 3.9 %collective-permute-start.7 = (bf16[24,256]{1,0:T(8,128)(2,1)S(1)}, bf16[24,256]{1,0:T(8,128)(2,1)S(1)}, u32[]{:S(2)}, u32[]{:S(2)}) collective-permute-start(bf16[24,256]{1,0:T(8,128)(2,1)S(1)} %fusion.27), channel_id=1, source_target_pairs={{0,2},{1,3},{8,10},{9,11},{16,18},{17,19},{24,26},{25,27},{32,34},... | collective-permute-start | bytes 36872 | tf_op jit(solution)/shard_map/ppermute | solution.py:269
  16.8 5.6 %all-to-all-start = ((bf16[4,40,640]{2,1,0:T(8,128)(2,1)}), bf16[4,40,640]{2,1,0:T(8,128)(2,1)S(1)}, u32[]{:S(2)}, u32[]{:S(2)}) async-start(bf16[4,40,640]{2,1,0:T(8,128)(2,1)} %broadcast_in_dim.4), calls=%async_computation | async-start | bytes 409600 | tf_op jit(solution)/shard_map/all_to_all | solution.py:30
  25.3 5.3 %collective-permute-start.9 = (bf16[56,256]{1,0:T(8,128)(2,1)S(1)}, bf16[56,256]{1,0:T(8,128)(2,1)S(1)}, u32[]{:S(2)}, u32[]{:S(2)}) collective-permute-start(bf16[56,256]{1,0:T(8,128)(2,1)S(1)} %pad_maximum_fusion.3.p0), channel_id=1, source_target_pairs={{0,24},{8,0},{16,8},{24,16},{1,25},{9,1},{17,9},{25,17},{2,26},{10... | collective-permute-start | bytes 86024 | tf_op jit(solution)/shard_map/ppermute | solution.py:35
  32.6 2.2 %collective-permute-start.11 = (bf16[56,256]{1,0:T(8,128)(2,1)S(1)}, bf16[56,256]{1,0:T(8,128)(2,1)S(1)}, u32[]{:S(2)}, u32[]{:S(2)}) collective-permute-start(bf16[56,256]{1,0:T(8,128)(2,1)S(1)} %pad_maximum_fusion.3.p0), channel_id=1, source_target_pairs={{0,8},{8,16},{16,24},{24,0},{1,9},{9,17},{17,25},{25,1},{2,10},{10... | collective-permute-start | bytes 86024 | tf_op jit(solution)/shard_map/ppermute | solution.py:35
  36.2 2.8 %collective-permute-done.11.p3 = bf16[56,256]{1,0:T(8,128)(2,1)S(1)} collective-permute-done((bf16[56,256]{1,0:T(8,128)(2,1)S(1)}, bf16[56,256]{1,0:T(8,128)(2,1)S(1)}, u32[]{:S(2)}, u32[]{:S(2)}) %collective-permute-start.11) | collective-permute-done | bytes 28704 | tf_op jit(solution)/shard_map/ppermute | solution.py:35
  39.6 2.7 %merge_extra.1 = bf16[16,16,3584]{2,1,0:T(8,128)(2,1)} custom-call(s32[3]{0:T(128)} %pad_add_fusion.flag_ref, s32[224,1]{1,0:T(8,128)} %constant.38.clone.device_ref, s32[224,1]{1,0:T(8,128)} %constant.39.clone.row_ref, bf16[56,256]{1,0:T(8,128)(2,1)} %copy-done.12, bf16[56,256]{1,0:T(8,128)(2,1)} %copy-done.14, bf16[56,256]{1,0:T(8,128)(2,1)} %copy-done.15, ...), custom_call_target="tpu_custom_call" | custom-call | tf_op jit(solution)/shard_map/merge_extra/pallas_call | solution.py:284
  42.3 6.8 %all-to-all-start.2 = ((bf16[16,16,3584]{2,1,0:T(8,128)(2,1)}), bf16[16,16,3584]{2,1,0:T(8,128)(2,1)S(1)}, u32[]{:S(2)}, u32[]{:S(2)}) async-start(bf16[16,16,3584]{2,1,0:T(8,128)(2,1)} %merge_extra.1), calls=%async_computation.2 | async-start | bytes 3670016 | tf_op jit(solution)/shard_map/all_to_all | solution.py:293
  49.1 3.1 %merge_weights.1 = bf16[16,160,640]{2,1,0:T(8,128)(2,1)} custom-call(bf16[4,40,640]{2,1,0:T(8,128)(2,1)} %copy-done.11), custom_call_target="tpu_custom_call" | custom-call | tf_op jit(solution)/shard_map/merge_weights/pallas_call | solution.py:253
  52.2 18.8 %all-to-all-done.2.extra_ref = bf16[16,16,3584]{2,1,0:T(8,128)(2,1)S(1)} async-done(((bf16[16,16,3584]{2,1,0:T(8,128)(2,1)}), bf16[16,16,3584]{2,1,0:T(8,128)(2,1)S(1)}, u32[]{:S(2)}, u32[]{:S(2)}) %all-to-all-start.2) | async-done | bytes 1835040 | tf_op jit(solution)/shard_map/all_to_all | solution.py:293
  72.2 5.8 %all-to-all-start.1 = ((bf16[16,160,640]{2,1,0:T(8,128)(2,1)}), bf16[16,160,640]{2,1,0:T(8,128)(2,1)S(1)}, u32[]{:S(2)}, u32[]{:S(2)}) async-start(bf16[16,160,640]{2,1,0:T(8,128)(2,1)} %merge_weights.1), calls=%async_computation.1 | async-start | bytes 6553600 | tf_op jit(solution)/shard_map/all_to_all | solution.py:262
  81.5 2.6 %fusion.6.picked_ref = f32[64,1024]{1,0:T(8,128)} fusion(bf16[64,1280]{1,0:T(8,128)(2,1)} %normed_ref.1, s32[1024]{0:T(1024)S(1)} %copy-done.17), kind=kOutput, calls=%fused_computation.10 | convolution fusion | flops 169082880 | bytes 430080 | tf_op jit(solution)/shard_map/dot_general | solution.py:109
  85.0 5.3 %collective-permute-start.12 = (bf16[1280,256]{1,0:T(8,128)(2,1)}, bf16[1280,256]{1,0:T(8,128)(2,1)}, u32[]{:S(2)}, u32[]{:S(2)}) collective-permute-start(bf16[1280,256]{1,0:T(8,128)(2,1)} %solved.1.down0_ref), channel_id=1, source_target_pairs={{0,1},{1,0},{2,3},{3,2},{4,5},{5,4},{6,7},{7,6},{8,9},{9,8},{10,11... | collective-permute-start | bytes 1966088 | tf_op jit(solution)/shard_map/ppermute | solution.py:25
  90.3 24.5 %all-to-all-done.1.plane_ref = bf16[16,160,640]{2,1,0:T(8,128)(2,1)S(1)} async-done(((bf16[16,160,640]{2,1,0:T(8,128)(2,1)}), bf16[16,160,640]{2,1,0:T(8,128)(2,1)S(1)}, u32[]{:S(2)}, u32[]{:S(2)}) %all-to-all-start.1) | async-done | bytes 3276832 | tf_op jit(solution)/shard_map/all_to_all | solution.py:262
  118.3 9.2 %collective-permute-start = (f32[32,1792]{1,0:T(8,128)S(1)}, f32[32,1792]{1,0:T(8,128)S(1)}, u32[]{:S(2)}, u32[]{:S(2)}) collective-permute-start(f32[32,1792]{1,0:T(8,128)S(1)} %get-tuple-element.14), channel_id=1, source_target_pairs={{0,1},{1,0},{2,3},{3,2},{4,5},{5,4},{6,7},{7,6},{8,9},{9,8},{10,11... | collective-permute-start | bytes 688136 | tf_op jit(solution)/shard_map/ppermute | solution.py:25
  127.7 2.3 %convolution_convert_fusion.down_ref = bf16[1280,1024]{1,0:T(8,128)(2,1)S(1)} fusion(bf16[1280,640]{1,0:T(8,128)(2,1)S(1)} %bitcast.34, s32[1024]{0:T(1024)S(1)} %broadcast_subtract_fusion), kind=kOutput, calls=%fused_computation.2 | convolution fusion | flops 1679687680 | bytes 4263936 | tf_op jit(solution)/shard_map/dot_general | solution.py:109
  130.0 7.0 %collective-permute-start.1 = (bf16[32,896]{1,0:T(8,128)(2,1)S(1)}, bf16[32,896]{1,0:T(8,128)(2,1)S(1)}, u32[]{:S(2)}, u32[]{:S(2)}) collective-permute-start(bf16[32,896]{1,0:T(8,128)(2,1)S(1)} %get-tuple-element.23), channel_id=1, source_target_pairs={{0,2},{2,0},{4,6},{6,4},{1,3},{3,1},{5,7},{7,5},{8,10},{10,8},{12,... | collective-permute-start | bytes 172040 | tf_op jit(solution)/shard_map/ppermute | solution.py:314
  137.0 5.3 %collective-permute-start.3 = (bf16[32,896]{1,0:T(8,128)(2,1)S(1)}, bf16[32,896]{1,0:T(8,128)(2,1)S(1)}, u32[]{:S(2)}, u32[]{:S(2)}) collective-permute-start(bf16[32,896]{1,0:T(8,128)(2,1)S(1)} %get-tuple-element.24), channel_id=1, source_target_pairs={{0,6},{2,4},{4,2},{6,0},{1,7},{3,5},{5,3},{7,1},{8,14},{10,12},{12... | collective-permute-start | bytes 172040 | tf_op jit(solution)/shard_map/ppermute | solution.py:314
  142.6 4.8 %collective-permute-done.3 = bf16[32,896]{1,0:T(8,128)(2,1)S(1)} collective-permute-done((bf16[32,896]{1,0:T(8,128)(2,1)S(1)}, bf16[32,896]{1,0:T(8,128)(2,1)S(1)}, u32[]{:S(2)}, u32[]{:S(2)}) %collective-permute-start.3) | collective-permute-done | bytes 57376 | tf_op jit(solution)/shard_map/ppermute | solution.py:314
  147.5 8.2 %collective-permute-start.2 = (bf16[32,896]{1,0:T(8,128)(2,1)S(1)}, bf16[32,896]{1,0:T(8,128)(2,1)S(1)}, u32[]{:S(2)}, u32[]{:S(2)}) collective-permute-start(bf16[32,896]{1,0:T(8,128)(2,1)S(1)} %get-tuple-element.21), channel_id=1, source_target_pairs={{0,6},{2,4},{4,2},{6,0},{1,7},{3,5},{5,3},{7,1},{8,14},{10,12},{12... | collective-permute-start | bytes 172040 | tf_op jit(solution)/shard_map/ppermute | solution.py:319
  158.3 7.2 %collective-permute-done.4 = bf16[32,896]{1,0:T(8,128)(2,1)S(1)} collective-permute-done((bf16[32,896]{1,0:T(8,128)(2,1)S(1)}, bf16[32,896]{1,0:T(8,128)(2,1)S(1)}, u32[]{:S(2)}, u32[]{:S(2)}) %collective-permute-start.4) | collective-permute-done | bytes 57376 | tf_op jit(solution)/shard_map/ppermute | solution.py:319
  165.7 3.0 %collective-permute-start.5 = (f32[32,1792]{1,0:T(8,128)S(1)}, f32[32,1792]{1,0:T(8,128)S(1)}, u32[]{:S(2)}, u32[]{:S(2)}) collective-permute-start(f32[32,1792]{1,0:T(8,128)S(1)} %pad_maximum_fusion.mine_ref), channel_id=1, source_target_pairs={{0,1},{1,0},{2,3},{3,2},{4,5},{5,4},{6,7},{7,6},{8,9},{9,8},{10,11... | collective-permute-start | bytes 688136 | tf_op jit(solution)/shard_map/ppermute | solution.py:25
  169.8 2.4 %middle.1 = (f32[64,1]{1,0:T(8,128)S(1)}, f32[64,16]{1,0:T(8,128)S(1)}, f32[80,1024]{1,0:T(8,128)S(1)}, f32[2,144,256]{2,1,0:T(8,128)S(1)}) custom-call(s32[3]{0:T(128)S(1)} %copy-done.9, f32[32,1792]{1,0:T(8,128)S(1)} %pad_maximum_fusion.mine_ref, f32[32,1792]{1,0:T(8,128)S(1)} %collective-permute-done.5.theirs_ref, bf16[64,1280]{1,0:T(8,128)(2,1)S(1)} %copy-done.6, ...), custom_call_target="tpu_custom_call" | custom-call | tf_op jit(solution)/shard_map/middle/pallas_call | solution.py:349
  172.2 4.8 %last.1 = bf16[64,16,1024]{2,1,0:T(8,128)(2,1)} custom-call(s32[3]{0:T(128)S(1)} %copy-done.9, f32[64,1024]{1,0:T(8,128)S(1)} %fusion.10.gain_ref, f32[64,1]{1,0:T(8,128)S(1)} %get-tuple-element.15.inv_ref, f32[64,16]{1,0:T(8,128)S(1)} %get-tuple-element.16.share_ref, f32[80,1024]{1,0:T(8,128)S(1)} %get-tuple-element.17.own_ref, ...), custom_call_target="tpu_custom_call" | custom-call | tf_op jit(solution)/shard_map/last/pallas_call | solution.py:362
  (84 shorter events, 25.3 us)
Async XLA Ops:
  0.0 78.1 %copy-start = (bf16[64,1280]{1,0:T(8,128)(2,1)S(1)}, bf16[64,1280]{1,0:T(8,128)(2,1)}, u32[]{:S(2)}) copy-start(bf16[64,1280]{1,0:T(8,128)(2,1)} %param.13) | copy-start | bytes 491524
  2.5 8.8 %collective-permute-start.6 = (bf16[24,256]{1,0:T(8,128)(2,1)S(1)}, bf16[24,256]{1,0:T(8,128)(2,1)S(1)}, u32[]{:S(2)}, u32[]{:S(2)}) collective-permute-start(bf16[24,256]{1,0:T(8,128)(2,1)S(1)} %pad_maximum_fusion.4), channel_id=1, source_target_pairs={{0,1},{2,3},{4,5},{6,7},{8,9},{10,11},{12,13},{14,15},{16,17},{18,... | collective-permute-start | bytes 36872 | tf_op jit(solution)/shard_map/ppermute | solution.py:268
  11.3 11.0 %collective-permute-start.7 = (bf16[24,256]{1,0:T(8,128)(2,1)S(1)}, bf16[24,256]{1,0:T(8,128)(2,1)S(1)}, u32[]{:S(2)}, u32[]{:S(2)}) collective-permute-start(bf16[24,256]{1,0:T(8,128)(2,1)S(1)} %fusion.27), channel_id=1, source_target_pairs={{0,2},{1,3},{8,10},{9,11},{16,18},{17,19},{24,26},{25,27},{32,34},... | collective-permute-start | bytes 36872 | tf_op jit(solution)/shard_map/ppermute | solution.py:269
  16.8 25.5 %all-to-all-start = ((bf16[4,40,640]{2,1,0:T(8,128)(2,1)}), bf16[4,40,640]{2,1,0:T(8,128)(2,1)S(1)}, u32[]{:S(2)}, u32[]{:S(2)}) async-start(bf16[4,40,640]{2,1,0:T(8,128)(2,1)} %broadcast_in_dim.4), calls=%async_computation | async-start | bytes 409600 | tf_op jit(solution)/shard_map/all_to_all | solution.py:30
  22.4 2.9 %collective-permute-start.8 = (bf16[24,256]{1,0:T(8,128)(2,1)S(1)}, bf16[24,256]{1,0:T(8,128)(2,1)S(1)}, u32[]{:S(2)}, u32[]{:S(2)}) collective-permute-start(bf16[24,256]{1,0:T(8,128)(2,1)S(1)} %broadcast_select_fusion), channel_id=1, source_target_pairs={{0,6},{2,4},{1,7},{3,5},{8,14},{10,12},{9,15},{11,13},{16,22},{18,... | collective-permute-start | bytes 36872 | tf_op jit(solution)/shard_map/ppermute | solution.py:270
  25.3 13.7 %copy-start.12 = (bf16[56,256]{1,0:T(8,128)(2,1)}, bf16[56,256]{1,0:T(8,128)(2,1)S(1)}, u32[]{:S(2)}) copy-start(bf16[56,256]{1,0:T(8,128)(2,1)S(1)} %pad_maximum_fusion.3.p0) | copy-start | bytes 86020
  25.3 10.1 %collective-permute-start.9 = (bf16[56,256]{1,0:T(8,128)(2,1)S(1)}, bf16[56,256]{1,0:T(8,128)(2,1)S(1)}, u32[]{:S(2)}, u32[]{:S(2)}) collective-permute-start(bf16[56,256]{1,0:T(8,128)(2,1)S(1)} %pad_maximum_fusion.3.p0), channel_id=1, source_target_pairs={{0,24},{8,0},{16,8},{24,16},{1,25},{9,1},{17,9},{25,17},{2,26},{10... | collective-permute-start | bytes 86024 | tf_op jit(solution)/shard_map/ppermute | solution.py:35
  30.7 5.5 %collective-permute-start.10 = (bf16[56,256]{1,0:T(8,128)(2,1)S(1)}, bf16[56,256]{1,0:T(8,128)(2,1)S(1)}, u32[]{:S(2)}, u32[]{:S(2)}) collective-permute-start(bf16[56,256]{1,0:T(8,128)(2,1)S(1)} %pad_maximum_fusion.3.p0), channel_id=1, source_target_pairs={{0,16},{8,24},{16,0},{24,8},{1,17},{9,25},{17,1},{25,9},{2,18},{10... | collective-permute-start | bytes 86024 | tf_op jit(solution)/shard_map/ppermute | solution.py:35
  32.6 6.4 %collective-permute-start.11 = (bf16[56,256]{1,0:T(8,128)(2,1)S(1)}, bf16[56,256]{1,0:T(8,128)(2,1)S(1)}, u32[]{:S(2)}, u32[]{:S(2)}) collective-permute-start(bf16[56,256]{1,0:T(8,128)(2,1)S(1)} %pad_maximum_fusion.3.p0), channel_id=1, source_target_pairs={{0,8},{8,16},{16,24},{24,0},{1,9},{9,17},{17,25},{25,1},{2,10},{10... | collective-permute-start | bytes 86024 | tf_op jit(solution)/shard_map/ppermute | solution.py:35
  42.3 28.7 %all-to-all-start.2 = ((bf16[16,16,3584]{2,1,0:T(8,128)(2,1)}), bf16[16,16,3584]{2,1,0:T(8,128)(2,1)S(1)}, u32[]{:S(2)}, u32[]{:S(2)}) async-start(bf16[16,16,3584]{2,1,0:T(8,128)(2,1)} %merge_extra.1), calls=%async_computation.2 | async-start | bytes 3670016 | tf_op jit(solution)/shard_map/all_to_all | solution.py:293
  52.2 26.0 %copy-start.13 = (f32[1280]{0:T(1024)S(1)}, f32[1280]{0:T(1024)}, u32[]{:S(2)}) copy-start(f32[1280]{0:T(1024)} %param.16) | copy-start | bytes 15364
  52.2 29.3 %copy-start.17 = (s32[1024]{0:T(1024)S(1)}, s32[1024]{0:T(1024)}, u32[]{:S(2)}) copy-start(s32[1024]{0:T(1024)} %param.18) | copy-start | bytes 12292
  72.2 42.6 %all-to-all-start.1 = ((bf16[16,160,640]{2,1,0:T(8,128)(2,1)}), bf16[16,160,640]{2,1,0:T(8,128)(2,1)S(1)}, u32[]{:S(2)}, u32[]{:S(2)}) async-start(bf16[16,160,640]{2,1,0:T(8,128)(2,1)} %merge_weights.1), calls=%async_computation.1 | async-start | bytes 6553600 | tf_op jit(solution)/shard_map/all_to_all | solution.py:262
  79.2 35.6 %copy-start.9 = (s32[3]{0:T(128)S(1)}, s32[3]{0:T(128)}, u32[]{:S(2)}) copy-start(s32[3]{0:T(128)} %pad_add_fusion.flag_ref) | copy-start | bytes 40
  85.0 83.8 %collective-permute-start.12 = (bf16[1280,256]{1,0:T(8,128)(2,1)}, bf16[1280,256]{1,0:T(8,128)(2,1)}, u32[]{:S(2)}, u32[]{:S(2)}) collective-permute-start(bf16[1280,256]{1,0:T(8,128)(2,1)} %solved.1.down0_ref), channel_id=1, source_target_pairs={{0,1},{1,0},{2,3},{3,2},{4,5},{5,4},{6,7},{7,6},{8,9},{9,8},{10,11... | collective-permute-start | bytes 1966088 | tf_op jit(solution)/shard_map/ppermute | solution.py:25
  118.3 11.7 %collective-permute-start = (f32[32,1792]{1,0:T(8,128)S(1)}, f32[32,1792]{1,0:T(8,128)S(1)}, u32[]{:S(2)}, u32[]{:S(2)}) collective-permute-start(f32[32,1792]{1,0:T(8,128)S(1)} %get-tuple-element.14), channel_id=1, source_target_pairs={{0,1},{1,0},{2,3},{3,2},{4,5},{5,4},{6,7},{7,6},{8,9},{9,8},{10,11... | collective-permute-start | bytes 688136 | tf_op jit(solution)/shard_map/ppermute | solution.py:25
  129.9 35.6 %copy-start.10 = (f32[32,2,896]{2,0,1:T(8,128)S(1)}, f32[32,2,896]{2,0,1:T(8,128)}, u32[]{:S(2)}) copy-start(f32[32,2,896]{2,0,1:T(8,128)} %pad_convert_fusion) | copy-start | bytes 688132
  129.9 38.7 %copy-start.5 = (f32[64,1024]{1,0:T(8,128)S(1)}, f32[64,1024]{1,0:T(8,128)}, u32[]{:S(2)}) copy-start(f32[64,1024]{1,0:T(8,128)} %fusion.6.picked_ref) | copy-start | bytes 786436
  130.0 39.8 %copy-start.6 = (bf16[64,1280]{1,0:T(8,128)(2,1)S(1)}, bf16[64,1280]{1,0:T(8,128)(2,1)}, u32[]{:S(2)}) copy-start(bf16[64,1280]{1,0:T(8,128)(2,1)} %pad_maximum_fusion.1.head_ref) | copy-start | bytes 491524
  130.0 12.6 %collective-permute-start.1 = (bf16[32,896]{1,0:T(8,128)(2,1)S(1)}, bf16[32,896]{1,0:T(8,128)(2,1)S(1)}, u32[]{:S(2)}, u32[]{:S(2)}) collective-permute-start(bf16[32,896]{1,0:T(8,128)(2,1)S(1)} %get-tuple-element.23), channel_id=1, source_target_pairs={{0,2},{2,0},{4,6},{6,4},{1,3},{3,1},{5,7},{7,5},{8,10},{10,8},{12,... | collective-permute-start | bytes 172040 | tf_op jit(solution)/shard_map/ppermute | solution.py:314
  137.0 10.5 %collective-permute-start.3 = (bf16[32,896]{1,0:T(8,128)(2,1)S(1)}, bf16[32,896]{1,0:T(8,128)(2,1)S(1)}, u32[]{:S(2)}, u32[]{:S(2)}) collective-permute-start(bf16[32,896]{1,0:T(8,128)(2,1)S(1)} %get-tuple-element.24), channel_id=1, source_target_pairs={{0,6},{2,4},{4,2},{6,0},{1,7},{3,5},{5,3},{7,1},{8,14},{10,12},{12... | collective-permute-start | bytes 172040 | tf_op jit(solution)/shard_map/ppermute | solution.py:314
  147.5 10.8 %collective-permute-start.2 = (bf16[32,896]{1,0:T(8,128)(2,1)S(1)}, bf16[32,896]{1,0:T(8,128)(2,1)S(1)}, u32[]{:S(2)}, u32[]{:S(2)}) collective-permute-start(bf16[32,896]{1,0:T(8,128)(2,1)S(1)} %get-tuple-element.21), channel_id=1, source_target_pairs={{0,6},{2,4},{4,2},{6,0},{1,7},{3,5},{5,3},{7,1},{8,14},{10,12},{12... | collective-permute-start | bytes 172040 | tf_op jit(solution)/shard_map/ppermute | solution.py:319
  155.7 9.8 %collective-permute-start.4 = (bf16[32,896]{1,0:T(8,128)(2,1)S(1)}, bf16[32,896]{1,0:T(8,128)(2,1)S(1)}, u32[]{:S(2)}, u32[]{:S(2)}) collective-permute-start(bf16[32,896]{1,0:T(8,128)(2,1)S(1)} %get-tuple-element.22), channel_id=1, source_target_pairs={{0,2},{2,0},{4,6},{6,4},{1,3},{3,1},{5,7},{7,5},{8,10},{10,8},{12,... | collective-permute-start | bytes 172040 | tf_op jit(solution)/shard_map/ppermute | solution.py:319
  165.7 4.1 %collective-permute-start.5 = (f32[32,1792]{1,0:T(8,128)S(1)}, f32[32,1792]{1,0:T(8,128)S(1)}, u32[]{:S(2)}, u32[]{:S(2)}) collective-permute-start(f32[32,1792]{1,0:T(8,128)S(1)} %pad_maximum_fusion.mine_ref), channel_id=1, source_target_pairs={{0,1},{1,0},{2,3},{3,2},{4,5},{5,4},{6,7},{7,6},{8,9},{9,8},{10,11... | collective-permute-start | bytes 688136 | tf_op jit(solution)/shard_map/ppermute | solution.py:25
  (10 other events, 35.9 us)

commit v5 on v3

--- a/solution.py
+++ b/solution.py
@@ -36,7 +36,7 @@
     ]
 
 
-def weights_kernel(line_ref, out_ref, merged, done):
+def weights_kernel(line_ref, out_ref):
     pieces, rows, _ = line_ref.shape
     own = rows // 2
     shape = (pieces * rows, rows)
@@ -46,8 +46,9 @@
         target = source + k * own + jnp.where(source < own, 0, (pieces - 1) * own)
         part = dot32((row == target).astype(BF16), line_ref[k])
         total = part if total is None else total + part
-    merged[...] = total.astype(BF16)
-    send_copies(merged, out_ref, done)
+    line = total.astype(BF16)
+    for place in range(out_ref.shape[0]):
+        out_ref[place] = line
 
 
 def send_copies(merged, out_ref, done):
@@ -92,12 +93,9 @@
     gain = jnp.where(core == 0, (gain[:images] + gain[images:]) * picked_ref[:, :solved], 0.0)
     for out, side, at in ((kept_ref, core, 0), (given_ref, 1 - core, half)):
         rows_here = pl.ds(pl.multiple_of(side * half_images, half_images), half_images)
-        for run in range(2):
-            base = run * (width // 2 + half)
-            out[:, base : base + width // 2] = part[rows_here, run * (width // 2) : (run + 1) * (width // 2)]
-            out[:, base + width // 2 : base + width // 2 + half] = gain[
-                run * half_images : (run + 1) * half_images, at : at + half
-            ]
+        out[:, :width] = part[rows_here, :]
+        out[:, width : width + half] = gain[:half_images, at : at + half]
+        out[:, width + half :] = gain[half_images:, at : at + half]
 
 
 def split2(values):
@@ -140,17 +138,9 @@
     half_images = mine_ref.shape[0]
     width = head_ref.shape[1]
     images = 2 * half_images
-    half = down0_ref.shape[1]
     logits = head_ref.shape[0] // 4
     first_core = flag_ref[1] == 0
-    run = width // 2 + half
-    mine, theirs = (
-        jnp.concatenate([source[:, : width // 2], source[:, run : run + width // 2]], axis=1)
-        for source in (mine_ref, theirs_ref)
-    )
-    for side, source in ((flag_ref[1], mine_ref), (1 - flag_ref[1], theirs_ref)):
-        mix_ref[side, :half_images, :] = source[:, width // 2 : run]
-        mix_ref[side, half_images:images, :] = source[:, run + width // 2 :]
+    mine, theirs = mine_ref[...], theirs_ref[...]
     block = jnp.concatenate([jnp.where(first_core, mine, theirs), jnp.where(first_core, theirs, mine)], axis=0)
     centred = block - jnp.mean(block, axis=1, keepdims=True)
     inv_std = lax.rsqrt(jnp.mean(centred * centred, axis=1, keepdims=True) + 1e-06)
@@ -175,17 +165,17 @@
         own_ref[rows, :] = values
 
     def put_mine(rows, values):
-        mix_ref[flag_ref[1], images + rows.start : images + rows.stop, :] = values
+        mix_ref[flag_ref[1], rows, :] = values
 
     def put_theirs(rows, values):
-        mix_ref[1 - flag_ref[1], images + rows.start : images + rows.stop, :] = values
+        mix_ref[1 - flag_ref[1], rows, :] = values
 
     write(down_ref, put_own)
     write(down0_ref, put_mine)
     write(down1_ref, put_theirs)
 
 
-def last_kernel(flag_ref, gain_ref, inv_ref, share_ref, own_ref, mix_ref, inverse_ref, extra_ref, out_ref):
+def last_kernel(flag_ref, gain_ref, inv_ref, share_ref, own_ref, mix_ref, mine_ref, theirs_ref, inverse_ref, extra_ref, out_ref):
     images = gain_ref.shape[0]
     logits = share_ref.shape[1]
     panel = inverse_ref.shape[1]
@@ -199,17 +189,16 @@
 
     def jacobian(gain, along, head):
         scale = gain * inv_std
-        values = scale[:, None, :] * (head[None] - share * along[:, None, :])
+        values = scale[:, None, :] * head[None] - share * (scale * along)[:, None, :]
         return values.reshape(STEP * logits, values.shape[2])
 
     def solved_side(side):
-        along = mix_ref[side, pl.ds(images + first_image, STEP), :]
-        return jacobian(mix_ref[side, here, :], along, mix_ref[side, 2 * images : 2 * images + logits, :])
+        lanes = pl.ds(pl.multiple_of(pl.program_id(0) * panel, panel), panel)
+        gain = jnp.where(flag_ref[1] == side, mine_ref[:, lanes], theirs_ref[:, lanes])
+        return jacobian(gain, mix_ref[side, here, :], mix_ref[side, images : images + logits, :])
 
     def inverted(values, inverse):
-        high = values.astype(BF16)
-        low = (values - high.astype(F32)).astype(BF16)
-        return (dot_t(high, inverse) + dot_t(low, inverse)).astype(BF16)
+        return dot_t(values.astype(BF16), inverse).astype(BF16)
 
     first = inverted(solved_side(0), inverse_ref[0])
     rows_dev = gain_ref.shape[1]
@@ -248,9 +237,8 @@
         weights_kernel,
         out_shape=jax.ShapeDtypeStruct((16, 8 * own, hidden_dev), BF16),
         in_specs=[vmem],
-        out_specs=pl.BlockSpec(memory_space=pltpu.HBM),
-        scratch_shapes=[pltpu.VMEM((8 * own, hidden_dev), BF16), pltpu.SemaphoreType.DMA((16,))],
-        compiler_params=LARGE,
+        out_specs=vmem,
+        compiler_params=LIMIT,
         name="merge_weights",
     )(line)
     plane = lax.all_to_all(line, ("x", "y"), 0, 0)
@@ -286,6 +274,11 @@
     )(flag, np.array(device, np.int32)[:, None], np.array(source, np.int32)[:, None], *pieces)
     extra = lax.all_to_all(extra, ("x", "y"), 0, 0)
 
+    mine = jnp.where(core == 0, residual_in[: images // 2], residual_in[images // 2 :]).astype(F32)
+    third = jnp.where(z_hi == 3, 1.0, 0.0) + jnp.zeros((images // 2, 2 * half), F32)
+    inner = jnp.where((z_hi == 1) | (z_hi == 2), 1.0, 0.0) + jnp.zeros((images // 2, 2 * half), F32)
+    mine, third, inner = lax.optimization_barrier((mine, third, inner))
+
     picked = dot32(normed, one_hot(sub_inputs, width))
     kept, given, slope = pl.pallas_call(
         forward_kernel,
@@ -301,16 +294,14 @@
         name="forward",
     )(flag, normed, plane, local_hidden[None, : 2 * panel], picked)
     pair = kept + swap_core(given)
-    run = width // 2 + half
-    is_block = lax.broadcasted_iota(jnp.int32, (images // 2, run), 1) < width // 2
-    routes = ([(i, i ^ 1) for i in range(4)], [(i, 3 - i) for i in range(4)])
-    runs = [pair[:, :run], pair[:, run:]]
-    near = [lax.ppermute(part.astype(BF16), "zh", route) for part, route in zip(runs, routes)]
-    runs = [
-        jnp.where(is_block, part + got.astype(F32), jnp.where(z_hi == first, got.astype(F32), part))
-        for part, got, first in zip(runs, near, (1, 3))
-    ]
-    far = [lax.ppermute(part.astype(BF16), "zh", route) for part, route in zip(runs, routes[::-1])]
+    gain, pair = pair[:, width:], pair[:, :width]
+    near = lax.ppermute(pair.astype(BF16), "zh", [(i, i ^ 1) for i in range(4)]).astype(F32)
+    got = lax.ppermute(gain.astype(BF16), "zh", [(0, 3)]).astype(F32)
+    pair = pair + near
+    gain = jnp.where(third > 0.5, got, gain)
+    far = lax.ppermute(pair.astype(BF16), "zh", [(i, 3 - i) for i in range(4)]).astype(F32)
+    got = lax.ppermute(gain.astype(BF16), "zh", [(0, 1), (3, 2)]).astype(F32)
+    gain = jnp.where(inner > 0.5, got, gain)
 
     pick_own = one_hot(local_hidden, hidden_dev)
     down_t = plane[:, 4 * own :].reshape(width, hidden_dev)
@@ -320,16 +311,9 @@
     centred_head = head - jnp.mean(head, axis=0)
     head_parts = jnp.concatenate(split2(centred_head.T) + split2(head.T), axis=0)
 
-    mine = lax.dynamic_slice_in_dim(residual_in, core * (images // 2), images // 2, 0).astype(F32)
-    mine = jnp.pad(mine.reshape(images // 2, 2, width // 2), ((0, 0), (0, 0), (0, half)))
-    block = jnp.concatenate(
-        [
-            jnp.where(is_block, mine[:, k] + (runs[k] + far[k].astype(F32)), jnp.where(late, far[k].astype(F32), runs[k]))
-            for k, late in enumerate((z_hi >= 2, (z_hi == 1) | (z_hi == 2)))
-        ],
-        axis=1,
-    )
+    block = mine + (pair + far)
     block_pair = swap_core(block)
+    gain_pair = swap_core(gain)
 
     down_mine = pl.pallas_call(
         solved_kernel,
@@ -346,7 +330,7 @@
             jax.ShapeDtypeStruct((images, 1), F32),
             jax.ShapeDtypeStruct((images, logits), F32),
             jax.ShapeDtypeStruct((images + logits, rows_dev), F32),
-            jax.ShapeDtypeStruct((2, 2 * images + logits, half), F32),
+            jax.ShapeDtypeStruct((2, images + logits, half), F32),
         ),
         in_specs=[smem] + [vmem] * 6,
         out_specs=(vmem,) * 4,
@@ -357,11 +341,11 @@
         last_kernel,
         grid=(images // STEP,),
         out_shape=jax.ShapeDtypeStruct((images, logits, rows_dev), BF16),
-        in_specs=[smem] + [vmem] * 7,
+        in_specs=[smem] + [vmem] * 9,
         out_specs=pl.BlockSpec((STEP, logits, rows_dev), lambda i: (i, 0, 0)),
         compiler_params=LIMIT,
         name="last",
-    )(flag, gain_own, inv_std, share, own_products, mix, inverses, extra)
+    )(flag, gain_own, inv_std, share, own_products, mix, gain, gain_pair, inverses, extra)
 
 
 def solution(mesh):

time: 178 us -> 175 us (0.983)
  Pallas kernels: 15.1 us -> 12.2 us
  local copies, waits for them, and re-layouts: 6.09 us -> 8.6 us
    ppermute x3 -> x4, starting transfers between devices: 17.5 us -> 20.8 us  [swap_core(): return lax.ppermute(values, 'c', [(0, 1), (1, 0)])]
    ppermute x4, starting transfers between devices: 22.3 us -> 19.5 us  [the longest x1 8.39 us: body(): got = lax.ppermute(gain.astype(BF16), 'zh', [(0, 3)]).astype(F32)]
    pallas_call x1, Pallas kernels: 3.09 us -> 0.54 us  [body(): pl.pallas_call(weights_kernel, out_shape=jax.ShapeDtypeStruct((16, 8 * ow...]
    ppermute x4, waiting for transfers between devices: 12.4 us -> 10.1 us  [the longest x1 5.47 us: body(): lax.ppermute(pair.astype(BF16), 'zh', [(i, i ^ 1) for i in range(4)])]
    unnamed x36 -> x44, local copies, waits for them, and re-layouts: 3.76 us -> 5.05 us
  transfers between devices with their start and end apart: 16 -> 17, of which waited for: 10 -> 9; matrix products, arithmetic and copies ran while one was open for 7% -> 6% of each run, Pallas kernels for 5% -> 5%
where the time goes in v5:
time: 175 us; the launch traced here: 174 us
  starting transfers between devices  75.4 us (43%)
  waiting for transfers between devices  67.6 us (39%)
  Pallas kernels  12.2 us (7%)
  local copies, waits for them, and re-layouts  8.6 us (5%)
  matrix products  5.86 us (3%)
  other arithmetic  3.97 us (2%)
    all_to_all x1, waiting for transfers between devices, body(): plane = lax.all_to_all(line, ('x', 'y'), 0, 0)  25.7 us
    ppermute x4, starting transfers between devices, swap_core(): return lax.ppermute(values, 'c', [(0, 1), (1, 0)])  20.8 us
    all_to_all x1, waiting for transfers between devices, body(): extra = lax.all_to_all(extra, ('x', 'y'), 0, 0)  19.7 us
    ppermute x3, starting transfers between devices, ring_pieces(): lax.ppermute(shard, axis, [(i, (i - k) % count) for i in range(count)])  9.5 us
    ppermute x1, starting transfers between devices, body(): got = lax.ppermute(gain.astype(BF16), 'zh', [(0, 3)]).astype(F32)  8.39 us
    ppermute x1, waiting for transfers between devices, body(): lax.ppermute(chosen[1], 'c', [(0, 1)])  7.48 us
    ppermute x1, starting transfers between devices, body(): got = lax.ppermute(gain.astype(BF16), 'zh', [(0, 1), (3, 2)]).astype(F32)  7.27 us
    all_to_all x1, starting transfers between devices, body(): extra = lax.all_to_all(extra, ('x', 'y'), 0, 0)  6.76 us
  transfers between devices with their start and end apart: 17, of which 9 were waited for; matrix products, arithmetic and copies ran while one was open for 6% of the time, Pallas kernels for 5%

profile of v5, /device:TPU:1, one launch (start us, length us, event | category | flops | bytes accessed | tf_op | source)
XLA Modules:
  0.0 174.1 jit_solution(13995331526667625578)
XLA Ops:
  4.4 7.5 %collective-permute-done.4 = bf16[24,256]{1,0:T(8,128)(2,1)S(1)} collective-permute-done((bf16[24,256]{1,0:T(8,128)(2,1)S(1)}, bf16[24,256]{1,0:T(8,128)(2,1)S(1)}, u32[]{:S(2)}, u32[]{:S(2)}) %collective-permute-start.4) | collective-permute-done | bytes 12320 | tf_op jit(solution)/shard_map/ppermute | solution.py:250
  11.9 3.9 %collective-permute-start.5 = (bf16[24,256]{1,0:T(8,128)(2,1)S(1)}, bf16[24,256]{1,0:T(8,128)(2,1)S(1)}, u32[]{:S(2)}, u32[]{:S(2)}) collective-permute-start(bf16[24,256]{1,0:T(8,128)(2,1)S(1)} %fusion.20), channel_id=1, source_target_pairs={{0,2},{1,3},{8,10},{9,11},{16,18},{17,19},{24,26},{25,27},{32,34},... | collective-permute-start | bytes 36872 | tf_op jit(solution)/shard_map/ppermute | solution.py:251
  17.3 5.6 %all-to-all-start = ((bf16[4,40,640]{2,1,0:T(8,128)(2,1)}), bf16[4,40,640]{2,1,0:T(8,128)(2,1)S(1)}, u32[]{:S(2)}, u32[]{:S(2)}) async-start(bf16[4,40,640]{2,1,0:T(8,128)(2,1)} %broadcast_in_dim.4), calls=%async_computation | async-start | bytes 409600 | tf_op jit(solution)/shard_map/all_to_all | solution.py:30
  22.9 2.1 %collective-permute-start.6 = (bf16[24,256]{1,0:T(8,128)(2,1)S(1)}, bf16[24,256]{1,0:T(8,128)(2,1)S(1)}, u32[]{:S(2)}, u32[]{:S(2)}) collective-permute-start(bf16[24,256]{1,0:T(8,128)(2,1)S(1)} %broadcast_select_fusion), channel_id=1, source_target_pairs={{0,6},{2,4},{1,7},{3,5},{8,14},{10,12},{9,15},{11,13},{16,22},{18,... | collective-permute-start | bytes 36872 | tf_op jit(solution)/shard_map/ppermute | solution.py:252
  25.9 5.3 %collective-permute-start.7 = (bf16[56,256]{1,0:T(8,128)(2,1)S(1)}, bf16[56,256]{1,0:T(8,128)(2,1)S(1)}, u32[]{:S(2)}, u32[]{:S(2)}) collective-permute-start(bf16[56,256]{1,0:T(8,128)(2,1)S(1)} %pad_maximum_fusion.2.p0), channel_id=1, source_target_pairs={{0,24},{8,0},{16,8},{24,16},{1,25},{9,1},{17,9},{25,17},{2,26},{10... | collective-permute-start | bytes 86024 | tf_op jit(solution)/shard_map/ppermute | solution.py:35
  31.2 1.9 %collective-permute-start.8 = (bf16[56,256]{1,0:T(8,128)(2,1)S(1)}, bf16[56,256]{1,0:T(8,128)(2,1)S(1)}, u32[]{:S(2)}, u32[]{:S(2)}) collective-permute-start(bf16[56,256]{1,0:T(8,128)(2,1)S(1)} %pad_maximum_fusion.2.p0), channel_id=1, source_target_pairs={{0,16},{8,24},{16,0},{24,8},{1,17},{9,25},{17,1},{25,9},{2,18},{10... | collective-permute-start | bytes 86024 | tf_op jit(solution)/shard_map/ppermute | solution.py:35
  33.1 2.2 %collective-permute-start.9 = (bf16[56,256]{1,0:T(8,128)(2,1)S(1)}, bf16[56,256]{1,0:T(8,128)(2,1)S(1)}, u32[]{:S(2)}, u32[]{:S(2)}) collective-permute-start(bf16[56,256]{1,0:T(8,128)(2,1)S(1)} %pad_maximum_fusion.2.p0), channel_id=1, source_target_pairs={{0,8},{8,16},{16,24},{24,0},{1,9},{9,17},{17,25},{25,1},{2,10},{10... | collective-permute-start | bytes 86024 | tf_op jit(solution)/shard_map/ppermute | solution.py:35
  36.7 2.8 %collective-permute-done.9.p3 = bf16[56,256]{1,0:T(8,128)(2,1)S(1)} collective-permute-done((bf16[56,256]{1,0:T(8,128)(2,1)S(1)}, bf16[56,256]{1,0:T(8,128)(2,1)S(1)}, u32[]{:S(2)}, u32[]{:S(2)}) %collective-permute-start.9) | collective-permute-done | bytes 28704 | tf_op jit(solution)/shard_map/ppermute | solution.py:35
  40.2 2.7 %merge_extra.1 = bf16[16,16,3584]{2,1,0:T(8,128)(2,1)} custom-call(s32[3]{0:T(128)} %pad_add_fusion.flag_ref, s32[224,1]{1,0:T(8,128)} %constant.34.clone.device_ref, s32[224,1]{1,0:T(8,128)} %constant.35.clone.row_ref, bf16[56,256]{1,0:T(8,128)(2,1)} %copy-done.14, bf16[56,256]{1,0:T(8,128)(2,1)} %copy-done.16, bf16[56,256]{1,0:T(8,128)(2,1)} %copy-done.17, ...), custom_call_target="tpu_custom_call" | custom-call | tf_op jit(solution)/shard_map/merge_extra/pallas_call | solution.py:266
  42.8 6.8 %all-to-all-start.2 = ((bf16[16,16,3584]{2,1,0:T(8,128)(2,1)}), bf16[16,16,3584]{2,1,0:T(8,128)(2,1)S(1)}, u32[]{:S(2)}, u32[]{:S(2)}) async-start(bf16[16,16,3584]{2,1,0:T(8,128)(2,1)} %merge_extra.1), calls=%async_computation.2 | async-start | bytes 3670016 | tf_op jit(solution)/shard_map/all_to_all | solution.py:275
  51.8 19.7 %all-to-all-done.2.extra_ref = bf16[16,16,3584]{2,1,0:T(8,128)(2,1)S(1)} async-done(((bf16[16,16,3584]{2,1,0:T(8,128)(2,1)}), bf16[16,16,3584]{2,1,0:T(8,128)(2,1)S(1)}, u32[]{:S(2)}, u32[]{:S(2)}) %all-to-all-start.2) | async-done | bytes 1835040 | tf_op jit(solution)/shard_map/all_to_all | solution.py:275
  72.8 6.0 %all-to-all-start.1 = ((bf16[16,160,640]{2,1,0:T(8,128)(2,1)}), bf16[16,160,640]{2,1,0:T(8,128)(2,1)S(1)}, u32[]{:S(2)}, u32[]{:S(2)}) async-start(bf16[16,160,640]{2,1,0:T(8,128)(2,1)} %copy-done.3), calls=%async_computation.1 | async-start | bytes 6553600 | tf_op jit(solution)/shard_map/all_to_all | solution.py:244
  84.4 5.3 %collective-permute-start.10 = (bf16[1280,256]{1,0:T(8,128)(2,1)}, bf16[1280,256]{1,0:T(8,128)(2,1)}, u32[]{:S(2)}, u32[]{:S(2)}) collective-permute-start(bf16[1280,256]{1,0:T(8,128)(2,1)} %solved.1.down0_ref), channel_id=1, source_target_pairs={{0,1},{1,0},{2,3},{3,2},{4,5},{5,4},{6,7},{7,6},{8,9},{9,8},{10,11... | collective-permute-start | bytes 1966088 | tf_op jit(solution)/shard_map/ppermute | solution.py:25
  89.8 25.7 %all-to-all-done.1.plane_ref = bf16[16,160,640]{2,1,0:T(8,128)(2,1)S(1)} async-done(((bf16[16,160,640]{2,1,0:T(8,128)(2,1)}), bf16[16,160,640]{2,1,0:T(8,128)(2,1)S(1)}, u32[]{:S(2)}, u32[]{:S(2)}) %all-to-all-start.1) | async-done | bytes 3276832 | tf_op jit(solution)/shard_map/all_to_all | solution.py:244
  118.0 9.2 %collective-permute-start = (f32[32,1792]{1,0:T(8,128)S(1)}, f32[32,1792]{1,0:T(8,128)S(1)}, u32[]{:S(2)}, u32[]{:S(2)}) collective-permute-start(f32[32,1792]{1,0:T(8,128)S(1)} %get-tuple-element.18), channel_id=1, source_target_pairs={{0,1},{1,0},{2,3},{3,2},{4,5},{5,4},{6,7},{7,6},{8,9},{9,8},{10,11... | collective-permute-start | bytes 688136 | tf_op jit(solution)/shard_map/ppermute | solution.py:25
  127.4 2.3 %convolution_convert_fusion.down_ref = bf16[1280,1024]{1,0:T(8,128)(2,1)S(1)} fusion(bf16[1280,640]{1,0:T(8,128)(2,1)S(1)} %bitcast.22, s32[1024]{0:T(1024)S(1)} %copy-done.20), kind=kOutput, calls=%fused_computation.2 | convolution fusion | flops 1679687680 | bytes 4263936 | tf_op jit(solution)/shard_map/dot_general | solution.py:107
  129.8 8.4 %collective-permute-start.11 = (bf16[32,512]{1,0:T(8,128)(2,1)S(1)}, bf16[32,512]{1,0:T(8,128)(2,1)S(1)}, u32[]{:S(2)}, u32[]{:S(2)}) collective-permute-start(bf16[32,512]{1,0:T(8,128)(2,1)S(1)} %slice.77), channel_id=1, source_target_pairs={{0,6},{1,7},{8,14},{9,15},{16,22},{17,23},{24,30},{25,31},{32,38},... | collective-permute-start | bytes 98312 | tf_op jit(solution)/shard_map/ppermute | solution.py:299
  140.8 7.3 %collective-permute-start.12 = (bf16[32,512]{1,0:T(8,128)(2,1)S(1)}, bf16[32,512]{1,0:T(8,128)(2,1)S(1)}, u32[]{:S(2)}, u32[]{:S(2)}) collective-permute-start(bf16[32,512]{1,0:T(8,128)(2,1)S(1)} %fusion.21), channel_id=1, source_target_pairs={{0,2},{6,4},{1,3},{7,5},{8,10},{14,12},{9,11},{15,13},{16,18},{22,... | collective-permute-start | bytes 98312 | tf_op jit(solution)/shard_map/ppermute | solution.py:303
  148.1 5.5 %collective-permute-done.1 = bf16[32,1280]{1,0:T(8,128)(2,1)S(1)} collective-permute-done((bf16[32,1280]{1,0:T(8,128)(2,1)S(1)}, bf16[32,1280]{1,0:T(8,128)(2,1)S(1)}, u32[]{:S(2)}, u32[]{:S(2)}) %collective-permute-start.1) | collective-permute-done | bytes 81952 | tf_op jit(solution)/shard_map/ppermute | solution.py:298
  155.6 2.5 %collective-permute-start.13 = (f32[32,512]{1,0:T(8,128)S(1)}, f32[32,512]{1,0:T(8,128)S(1)}, u32[]{:S(2)}, u32[]{:S(2)}) collective-permute-start(f32[32,512]{1,0:T(8,128)S(1)} %convert_select_fusion.mine_ref), channel_id=1, source_target_pairs={{0,1},{1,0},{2,3},{3,2},{4,5},{5,4},{6,7},{7,6},{8,9},{9,8},{10,11... | collective-permute-start | bytes 196616 | tf_op jit(solution)/shard_map/ppermute | solution.py:25
  158.1 4.6 %collective-permute-done.2 = bf16[32,1280]{1,0:T(8,128)(2,1)S(1)} collective-permute-done((bf16[32,1280]{1,0:T(8,128)(2,1)S(1)}, bf16[32,1280]{1,0:T(8,128)(2,1)S(1)}, u32[]{:S(2)}, u32[]{:S(2)}) %collective-permute-start.2) | collective-permute-done | bytes 81952 | tf_op jit(solution)/shard_map/ppermute | solution.py:302
  162.8 3.8 %collective-permute-start.3 = (f32[32,1280]{1,0:T(8,128)S(1)}, f32[32,1280]{1,0:T(8,128)S(1)}, u32[]{:S(2)}, u32[]{:S(2)}) collective-permute-start(f32[32,1280]{1,0:T(8,128)S(1)} %add_add_fusion.mine_ref), channel_id=1, source_target_pairs={{0,1},{1,0},{2,3},{3,2},{4,5},{5,4},{6,7},{7,6},{8,9},{9,8},{10,11... | collective-permute-start | bytes 491528 | tf_op jit(solution)/shard_map/ppermute | solution.py:25
  167.5 2.4 %middle.1 = (f32[64,1]{1,0:T(8,128)S(1)}, f32[64,16]{1,0:T(8,128)S(1)}, f32[80,1024]{1,0:T(8,128)S(1)}, f32[2,80,256]{2,1,0:T(8,128)S(1)}) custom-call(s32[3]{0:T(128)S(1)} %copy-done.7, f32[32,1280]{1,0:T(8,128)S(1)} %add_add_fusion.mine_ref, f32[32,1280]{1,0:T(8,128)S(1)} %collective-permute-done.3.theirs_ref, bf16[64,1280]{1,0:T(8,128)(2,1)S(1)} %copy-done.4, ...), custom_call_target="tpu_custom_call" | custom-call | tf_op jit(solution)/shard_map/middle/pallas_call | solution.py:327
  170.0 4.1 %last.1 = bf16[64,16,1024]{2,1,0:T(8,128)(2,1)} custom-call(s32[3]{0:T(128)S(1)} %copy-done.7, f32[64,1024]{1,0:T(8,128)S(1)} %fusion.10.gain_ref, f32[64,1]{1,0:T(8,128)S(1)} %get-tuple-element.19.inv_ref, f32[64,16]{1,0:T(8,128)S(1)} %get-tuple-element.20.share_ref, f32[80,1024]{1,0:T(8,128)S(1)} %get-tuple-element.21.own_ref, ...), custom_call_target="tpu_custom_call" | custom-call | tf_op jit(solution)/shard_map/last/pallas_call | solution.py:340
  (95 shorter events, 26.0 us)
Async XLA Ops:
  3.1 8.8 %collective-permute-start.4 = (bf16[24,256]{1,0:T(8,128)(2,1)S(1)}, bf16[24,256]{1,0:T(8,128)(2,1)S(1)}, u32[]{:S(2)}, u32[]{:S(2)}) collective-permute-start(bf16[24,256]{1,0:T(8,128)(2,1)S(1)} %pad_maximum_fusion.3), channel_id=1, source_target_pairs={{0,1},{2,3},{4,5},{6,7},{8,9},{10,11},{12,13},{14,15},{16,17},{18,... | collective-permute-start | bytes 36872 | tf_op jit(solution)/shard_map/ppermute | solution.py:250
  11.9 11.0 %collective-permute-start.5 = (bf16[24,256]{1,0:T(8,128)(2,1)S(1)}, bf16[24,256]{1,0:T(8,128)(2,1)S(1)}, u32[]{:S(2)}, u32[]{:S(2)}) collective-permute-start(bf16[24,256]{1,0:T(8,128)(2,1)S(1)} %fusion.20), channel_id=1, source_target_pairs={{0,2},{1,3},{8,10},{9,11},{16,18},{17,19},{24,26},{25,27},{32,34},... | collective-permute-start | bytes 36872 | tf_op jit(solution)/shard_map/ppermute | solution.py:251
  17.3 25.5 %all-to-all-start = ((bf16[4,40,640]{2,1,0:T(8,128)(2,1)}), bf16[4,40,640]{2,1,0:T(8,128)(2,1)S(1)}, u32[]{:S(2)}, u32[]{:S(2)}) async-start(bf16[4,40,640]{2,1,0:T(8,128)(2,1)} %broadcast_in_dim.4), calls=%async_computation | async-start | bytes 409600 | tf_op jit(solution)/shard_map/all_to_all | solution.py:30
  22.9 2.9 %collective-permute-start.6 = (bf16[24,256]{1,0:T(8,128)(2,1)S(1)}, bf16[24,256]{1,0:T(8,128)(2,1)S(1)}, u32[]{:S(2)}, u32[]{:S(2)}) collective-permute-start(bf16[24,256]{1,0:T(8,128)(2,1)S(1)} %broadcast_select_fusion), channel_id=1, source_target_pairs={{0,6},{2,4},{1,7},{3,5},{8,14},{10,12},{9,15},{11,13},{16,22},{18,... | collective-permute-start | bytes 36872 | tf_op jit(solution)/shard_map/ppermute | solution.py:252
  25.9 10.2 %collective-permute-start.7 = (bf16[56,256]{1,0:T(8,128)(2,1)S(1)}, bf16[56,256]{1,0:T(8,128)(2,1)S(1)}, u32[]{:S(2)}, u32[]{:S(2)}) collective-permute-start(bf16[56,256]{1,0:T(8,128)(2,1)S(1)} %pad_maximum_fusion.2.p0), channel_id=1, source_target_pairs={{0,24},{8,0},{16,8},{24,16},{1,25},{9,1},{17,9},{25,17},{2,26},{10... | collective-permute-start | bytes 86024 | tf_op jit(solution)/shard_map/ppermute | solution.py:35
  31.2 5.5 %collective-permute-start.8 = (bf16[56,256]{1,0:T(8,128)(2,1)S(1)}, bf16[56,256]{1,0:T(8,128)(2,1)S(1)}, u32[]{:S(2)}, u32[]{:S(2)}) collective-permute-start(bf16[56,256]{1,0:T(8,128)(2,1)S(1)} %pad_maximum_fusion.2.p0), channel_id=1, source_target_pairs={{0,16},{8,24},{16,0},{24,8},{1,17},{9,25},{17,1},{25,9},{2,18},{10... | collective-permute-start | bytes 86024 | tf_op jit(solution)/shard_map/ppermute | solution.py:35
  33.1 6.4 %collective-permute-start.9 = (bf16[56,256]{1,0:T(8,128)(2,1)S(1)}, bf16[56,256]{1,0:T(8,128)(2,1)S(1)}, u32[]{:S(2)}, u32[]{:S(2)}) collective-permute-start(bf16[56,256]{1,0:T(8,128)(2,1)S(1)} %pad_maximum_fusion.2.p0), channel_id=1, source_target_pairs={{0,8},{8,16},{16,24},{24,0},{1,9},{9,17},{17,25},{25,1},{2,10},{10... | collective-permute-start | bytes 86024 | tf_op jit(solution)/shard_map/ppermute | solution.py:35
  42.8 28.7 %all-to-all-start.2 = ((bf16[16,16,3584]{2,1,0:T(8,128)(2,1)}), bf16[16,16,3584]{2,1,0:T(8,128)(2,1)S(1)}, u32[]{:S(2)}, u32[]{:S(2)}) async-start(bf16[16,16,3584]{2,1,0:T(8,128)(2,1)} %merge_extra.1), calls=%async_computation.2 | async-start | bytes 3670016 | tf_op jit(solution)/shard_map/all_to_all | solution.py:275
  51.8 27.0 %copy-start.11 = (bf16[64,1280]{1,0:T(8,128)(2,1)S(1)}, bf16[64,1280]{1,0:T(8,128)(2,1)}, u32[]{:S(2)}) copy-start(bf16[64,1280]{1,0:T(8,128)(2,1)} %param.13) | copy-start | bytes 491524
  51.8 28.9 %copy-start.12 = (bf16[1280,16]{0,1:T(8,128)(2,1)S(1)}, bf16[1280,16]{0,1:T(8,128)(2,1)}, u32[]{:S(2)}) copy-start(bf16[1280,16]{0,1:T(8,128)(2,1)} %param.17) | copy-start | bytes 122884
  51.8 28.9 %copy-start.15 = (f32[1280]{0:T(1024)S(1)}, f32[1280]{0:T(1024)}, u32[]{:S(2)}) copy-start(f32[1280]{0:T(1024)} %param.16) | copy-start | bytes 15364
  51.8 29.9 %copy-start.21 = (s32[1024]{0:T(1024)S(1)}, s32[1024]{0:T(1024)}, u32[]{:S(2)}) copy-start(s32[1024]{0:T(1024)} %param.18) | copy-start | bytes 12292
  72.8 42.7 %all-to-all-start.1 = ((bf16[16,160,640]{2,1,0:T(8,128)(2,1)}), bf16[16,160,640]{2,1,0:T(8,128)(2,1)S(1)}, u32[]{:S(2)}, u32[]{:S(2)}) async-start(bf16[16,160,640]{2,1,0:T(8,128)(2,1)} %copy-done.3), calls=%async_computation.1 | async-start | bytes 6553600 | tf_op jit(solution)/shard_map/all_to_all | solution.py:244
  79.5 36.0 %copy-start.7 = (s32[3]{0:T(128)S(1)}, s32[3]{0:T(128)}, u32[]{:S(2)}) copy-start(s32[3]{0:T(128)} %pad_add_fusion.flag_ref) | copy-start | bytes 40
  84.4 82.2 %collective-permute-start.10 = (bf16[1280,256]{1,0:T(8,128)(2,1)}, bf16[1280,256]{1,0:T(8,128)(2,1)}, u32[]{:S(2)}, u32[]{:S(2)}) collective-permute-start(bf16[1280,256]{1,0:T(8,128)(2,1)} %solved.1.down0_ref), channel_id=1, source_target_pairs={{0,1},{1,0},{2,3},{3,2},{4,5},{5,4},{6,7},{7,6},{8,9},{9,8},{10,11... | collective-permute-start | bytes 1966088 | tf_op jit(solution)/shard_map/ppermute | solution.py:25
  118.0 11.7 %collective-permute-start = (f32[32,1792]{1,0:T(8,128)S(1)}, f32[32,1792]{1,0:T(8,128)S(1)}, u32[]{:S(2)}, u32[]{:S(2)}) collective-permute-start(f32[32,1792]{1,0:T(8,128)S(1)} %get-tuple-element.18), channel_id=1, source_target_pairs={{0,1},{1,0},{2,3},{3,2},{4,5},{5,4},{6,7},{7,6},{8,9},{9,8},{10,11... | collective-permute-start | bytes 688136 | tf_op jit(solution)/shard_map/ppermute | solution.py:25
  129.7 33.0 %copy-start.8 = (f32[32,1280]{1,0:T(8,128)S(1)}, f32[32,1280]{1,0:T(8,128)}, u32[]{:S(2)}) copy-start(f32[32,1280]{1,0:T(8,128)} %select_convert_fusion) | copy-start | bytes 491524
  129.7 37.9 %copy-start.4 = (bf16[64,1280]{1,0:T(8,128)(2,1)S(1)}, bf16[64,1280]{1,0:T(8,128)(2,1)}, u32[]{:S(2)}) copy-start(bf16[64,1280]{1,0:T(8,128)(2,1)} %pad_maximum_fusion.head_ref) | copy-start | bytes 491524
  129.8 11.0 %collective-permute-start.11 = (bf16[32,512]{1,0:T(8,128)(2,1)S(1)}, bf16[32,512]{1,0:T(8,128)(2,1)S(1)}, u32[]{:S(2)}, u32[]{:S(2)}) collective-permute-start(bf16[32,512]{1,0:T(8,128)(2,1)S(1)} %slice.77), channel_id=1, source_target_pairs={{0,6},{1,7},{8,14},{9,15},{16,22},{17,23},{24,30},{25,31},{32,38},... | collective-permute-start | bytes 98312 | tf_op jit(solution)/shard_map/ppermute | solution.py:299
  138.9 14.7 %collective-permute-start.1 = (bf16[32,1280]{1,0:T(8,128)(2,1)S(1)}, bf16[32,1280]{1,0:T(8,128)(2,1)S(1)}, u32[]{:S(2)}, u32[]{:S(2)}) collective-permute-start(bf16[32,1280]{1,0:T(8,128)(2,1)S(1)} %slice.76), channel_id=1, source_target_pairs={{0,2},{2,0},{4,6},{6,4},{1,3},{3,1},{5,7},{7,5},{8,10},{10,8},{12,... | collective-permute-start | bytes 245768 | tf_op jit(solution)/shard_map/ppermute | solution.py:298
  140.8 14.7 %collective-permute-start.12 = (bf16[32,512]{1,0:T(8,128)(2,1)S(1)}, bf16[32,512]{1,0:T(8,128)(2,1)S(1)}, u32[]{:S(2)}, u32[]{:S(2)}) collective-permute-start(bf16[32,512]{1,0:T(8,128)(2,1)S(1)} %fusion.21), channel_id=1, source_target_pairs={{0,2},{6,4},{1,3},{7,5},{8,10},{14,12},{9,11},{15,13},{16,18},{22,... | collective-permute-start | bytes 98312 | tf_op jit(solution)/shard_map/ppermute | solution.py:303
  153.6 9.1 %collective-permute-start.2 = (bf16[32,1280]{1,0:T(8,128)(2,1)S(1)}, bf16[32,1280]{1,0:T(8,128)(2,1)S(1)}, u32[]{:S(2)}, u32[]{:S(2)}) collective-permute-start(bf16[32,1280]{1,0:T(8,128)(2,1)S(1)} %fusion.15), channel_id=1, source_target_pairs={{0,6},{2,4},{4,2},{6,0},{1,7},{3,5},{5,3},{7,1},{8,14},{10,12},{12... | collective-permute-start | bytes 245768 | tf_op jit(solution)/shard_map/ppermute | solution.py:302
  155.6 14.4 %collective-permute-start.13 = (f32[32,512]{1,0:T(8,128)S(1)}, f32[32,512]{1,0:T(8,128)S(1)}, u32[]{:S(2)}, u32[]{:S(2)}) collective-permute-start(f32[32,512]{1,0:T(8,128)S(1)} %convert_select_fusion.mine_ref), channel_id=1, source_target_pairs={{0,1},{1,0},{2,3},{3,2},{4,5},{5,4},{6,7},{7,6},{8,9},{9,8},{10,11... | collective-permute-start | bytes 196616 | tf_op jit(solution)/shard_map/ppermute | solution.py:25
  162.8 4.8 %collective-permute-start.3 = (f32[32,1280]{1,0:T(8,128)S(1)}, f32[32,1280]{1,0:T(8,128)S(1)}, u32[]{:S(2)}, u32[]{:S(2)}) collective-permute-start(f32[32,1280]{1,0:T(8,128)S(1)} %add_add_fusion.mine_ref), channel_id=1, source_target_pairs={{0,1},{1,0},{2,3},{3,2},{4,5},{5,4},{6,7},{7,6},{8,9},{9,8},{10,11... | collective-permute-start | bytes 491528 | tf_op jit(solution)/shard_map/ppermute | solution.py:25
  (15 other events, 100.4 us)

commit v6 on v5

--- a/solution.py
+++ b/solution.py
@@ -138,9 +138,13 @@
     half_images = mine_ref.shape[0]
     width = head_ref.shape[1]
     images = 2 * half_images
+    half = down0_ref.shape[1]
     logits = head_ref.shape[0] // 4
     first_core = flag_ref[1] == 0
-    mine, theirs = mine_ref[...], theirs_ref[...]
+    mine, theirs = mine_ref[:, :width], theirs_ref[:, :width]
+    for side, source in ((flag_ref[1], mine_ref), (1 - flag_ref[1], theirs_ref)):
+        mix_ref[side, :half_images, :] = source[:, width : width + half]
+        mix_ref[side, half_images:images, :] = source[:, width + half :]
     block = jnp.concatenate([jnp.where(first_core, mine, theirs), jnp.where(first_core, theirs, mine)], axis=0)
     centred = block - jnp.mean(block, axis=1, keepdims=True)
     inv_std = lax.rsqrt(jnp.mean(centred * centred, axis=1, keepdims=True) + 1e-06)
@@ -165,17 +169,17 @@
         own_ref[rows, :] = values
 
     def put_mine(rows, values):
-        mix_ref[flag_ref[1], rows, :] = values
+        mix_ref[flag_ref[1], images + rows.start : images + rows.stop, :] = values
 
     def put_theirs(rows, values):
-        mix_ref[1 - flag_ref[1], rows, :] = values
+        mix_ref[1 - flag_ref[1], images + rows.start : images + rows.stop, :] = values
 
     write(down_ref, put_own)
     write(down0_ref, put_mine)
     write(down1_ref, put_theirs)
 
 
-def last_kernel(flag_ref, gain_ref, inv_ref, share_ref, own_ref, mix_ref, mine_ref, theirs_ref, inverse_ref, extra_ref, out_ref):
+def last_kernel(flag_ref, gain_ref, inv_ref, share_ref, own_ref, mix_ref, inverse_ref, extra_ref, out_ref):
     images = gain_ref.shape[0]
     logits = share_ref.shape[1]
     panel = inverse_ref.shape[1]
@@ -193,9 +197,8 @@
         return values.reshape(STEP * logits, values.shape[2])
 
     def solved_side(side):
-        lanes = pl.ds(pl.multiple_of(pl.program_id(0) * panel, panel), panel)
-        gain = jnp.where(flag_ref[1] == side, mine_ref[:, lanes], theirs_ref[:, lanes])
-        return jacobian(gain, mix_ref[side, here, :], mix_ref[side, images : images + logits, :])
+        along = mix_ref[side, pl.ds(images + first_image, STEP), :]
+        return jacobian(mix_ref[side, here, :], along, mix_ref[side, 2 * images : 2 * images + logits, :])
 
     def inverted(values, inverse):
         return dot_t(values.astype(BF16), inverse).astype(BF16)
@@ -275,9 +278,7 @@
     extra = lax.all_to_all(extra, ("x", "y"), 0, 0)
 
     mine = jnp.where(core == 0, residual_in[: images // 2], residual_in[images // 2 :]).astype(F32)
-    third = jnp.where(z_hi == 3, 1.0, 0.0) + jnp.zeros((images // 2, 2 * half), F32)
-    inner = jnp.where((z_hi == 1) | (z_hi == 2), 1.0, 0.0) + jnp.zeros((images // 2, 2 * half), F32)
-    mine, third, inner = lax.optimization_barrier((mine, third, inner))
+    mine = jnp.pad(mine, ((0, 0), (0, 2 * half)))
 
     picked = dot32(normed, one_hot(sub_inputs, width))
     kept, given, slope = pl.pallas_call(
@@ -294,14 +295,10 @@
         name="forward",
     )(flag, normed, plane, local_hidden[None, : 2 * panel], picked)
     pair = kept + swap_core(given)
-    gain, pair = pair[:, width:], pair[:, :width]
+    is_block = lax.broadcasted_iota(jnp.int32, pair.shape, 1) < width
     near = lax.ppermute(pair.astype(BF16), "zh", [(i, i ^ 1) for i in range(4)]).astype(F32)
-    got = lax.ppermute(gain.astype(BF16), "zh", [(0, 3)]).astype(F32)
-    pair = pair + near
-    gain = jnp.where(third > 0.5, got, gain)
+    pair = jnp.where(is_block, pair + near, jnp.where(z_hi == 1, near, pair))
     far = lax.ppermute(pair.astype(BF16), "zh", [(i, 3 - i) for i in range(4)]).astype(F32)
-    got = lax.ppermute(gain.astype(BF16), "zh", [(0, 1), (3, 2)]).astype(F32)
-    gain = jnp.where(inner > 0.5, got, gain)
 
     pick_own = one_hot(local_hidden, hidden_dev)
     down_t = plane[:, 4 * own :].reshape(width, hidden_dev)
@@ -311,9 +308,8 @@
     centred_head = head - jnp.mean(head, axis=0)
     head_parts = jnp.concatenate(split2(centred_head.T) + split2(head.T), axis=0)
 
-    block = mine + (pair + far)
+    block = jnp.where(is_block, mine + (pair + far), jnp.where(z_hi >= 2, far, pair))
     block_pair = swap_core(block)
-    gain_pair = swap_core(gain)
 
     down_mine = pl.pallas_call(
         solved_kernel,
@@ -330,7 +326,7 @@
             jax.ShapeDtypeStruct((images, 1), F32),
             jax.ShapeDtypeStruct((images, logits), F32),
             jax.ShapeDtypeStruct((images + logits, rows_dev), F32),
-            jax.ShapeDtypeStruct((2, images + logits, half), F32),
+            jax.ShapeDtypeStruct((2, 2 * images + logits, half), F32),
         ),
         in_specs=[smem] + [vmem] * 6,
         out_specs=(vmem,) * 4,
@@ -341,11 +337,11 @@
         last_kernel,
         grid=(images // STEP,),
         out_shape=jax.ShapeDtypeStruct((images, logits, rows_dev), BF16),
-        in_specs=[smem] + [vmem] * 9,
+        in_specs=[smem] + [vmem] * 7,
         out_specs=pl.BlockSpec((STEP, logits, rows_dev), lambda i: (i, 0, 0)),
         compiler_params=LIMIT,
         name="last",
-    )(flag, gain_own, inv_std, share, own_products, mix, gain, gain_pair, inverses, extra)
+    )(flag, gain_own, inv_std, share, own_products, mix, inverses, extra)
 
 
 def solution(mesh):

time: 175 us -> 173 us (0.989)
  starting transfers between devices: 75.4 us -> 64.2 us
  waiting for transfers between devices: 67.6 us -> 76.7 us
  local copies, waits for them, and re-layouts: 8.6 us -> 6.77 us
    ppermute x2 -> x0, starting transfers between devices: 15.7 us -> none  [the longest x1 8.39 us: body(): got = lax.ppermute(gain.astype(BF16), 'zh', [(0, 3)]).astype(F32)]
    ppermute x1, starting transfers between devices: 1.92 us -> 7 us  [body(): lax.ppermute(pair.astype(BF16), 'zh', [(i, i ^ 1) for i in range(4)])]
    ppermute x1, waiting for transfers between devices: 5.47 us -> 10.5 us  [body(): lax.ppermute(pair.astype(BF16), 'zh', [(i, i ^ 1) for i in range(4)])]
    ppermute x1, waiting for transfers between devices: 4.62 us -> 8.82 us  [body(): lax.ppermute(pair.astype(BF16), 'zh', [(i, 3 - i) for i in range(4)])]
    ppermute x4 -> x3, starting transfers between devices: 20.8 us -> 17.2 us  [swap_core(): return lax.ppermute(values, 'c', [(0, 1), (1, 0)])]
    ppermute x1, starting transfers between devices: 1.92 us -> 4.92 us  [body(): lax.ppermute(pair.astype(BF16), 'zh', [(i, 3 - i) for i in range(4)])]
    unnamed x44 -> x38, local copies, waits for them, and re-layouts: 5.05 us -> 4.48 us
  transfers between devices with their start and end apart: 17 -> 14, of which waited for: 9 -> 9; matrix products, arithmetic and copies ran while one was open for 6% -> 6% of each run, Pallas kernels for 5% -> 3%
where the time goes in v6:
time: 173 us; the launch traced here: 172 us
  waiting for transfers between devices  76.7 us (44%)
  starting transfers between devices  64.2 us (37%)
  Pallas kernels  12.1 us (7%)
  local copies, waits for them, and re-layouts  6.77 us (4%)
  matrix products  5.88 us (3%)
  other arithmetic  5.46 us (3%)
    all_to_all x1, waiting for transfers between devices, body(): plane = lax.all_to_all(line, ('x', 'y'), 0, 0)  25.5 us
    all_to_all x1, waiting for transfers between devices, body(): extra = lax.all_to_all(extra, ('x', 'y'), 0, 0)  19.7 us
    ppermute x3, starting transfers between devices, swap_core(): return lax.ppermute(values, 'c', [(0, 1), (1, 0)])  17.2 us
    ppermute x1, waiting for transfers between devices, body(): lax.ppermute(pair.astype(BF16), 'zh', [(i, i ^ 1) for i in range(4)])  10.5 us
    ppermute x3, starting transfers between devices, ring_pieces(): lax.ppermute(shard, axis, [(i, (i - k) % count) for i in range(count)])  9.5 us
    ppermute x1, waiting for transfers between devices, body(): lax.ppermute(pair.astype(BF16), 'zh', [(i, 3 - i) for i in range(4)])  8.82 us
    ppermute x1, waiting for transfers between devices, body(): lax.ppermute(chosen[1], 'c', [(0, 1)])  7.48 us
    ppermute x1, starting transfers between devices, body(): lax.ppermute(pair.astype(BF16), 'zh', [(i, i ^ 1) for i in range(4)])  7 us
  transfers between devices with their start and end apart: 14, of which 9 were waited for; matrix products, arithmetic and copies ran while one was open for 6% of the time, Pallas kernels for 3%

profile of v6, /device:TPU:1, one launch (start us, length us, event | category | flops | bytes accessed | tf_op | source)
XLA Modules:
  0.0 171.5 jit_solution(11219925643539383440)
XLA Ops:
  3.8 7.5 %collective-permute-done.4 = bf16[24,256]{1,0:T(8,128)(2,1)S(1)} collective-permute-done((bf16[24,256]{1,0:T(8,128)(2,1)S(1)}, bf16[24,256]{1,0:T(8,128)(2,1)S(1)}, u32[]{:S(2)}, u32[]{:S(2)}) %collective-permute-start.4) | collective-permute-done | bytes 12320 | tf_op jit(solution)/shard_map/ppermute | solution.py:253
  11.3 3.9 %collective-permute-start.5 = (bf16[24,256]{1,0:T(8,128)(2,1)S(1)}, bf16[24,256]{1,0:T(8,128)(2,1)S(1)}, u32[]{:S(2)}, u32[]{:S(2)}) collective-permute-start(bf16[24,256]{1,0:T(8,128)(2,1)S(1)} %fusion.23), channel_id=1, source_target_pairs={{0,2},{1,3},{8,10},{9,11},{16,18},{17,19},{24,26},{25,27},{32,34},... | collective-permute-start | bytes 36872 | tf_op jit(solution)/shard_map/ppermute | solution.py:254
  16.7 5.6 %all-to-all-start = ((bf16[4,40,640]{2,1,0:T(8,128)(2,1)}), bf16[4,40,640]{2,1,0:T(8,128)(2,1)S(1)}, u32[]{:S(2)}, u32[]{:S(2)}) async-start(bf16[4,40,640]{2,1,0:T(8,128)(2,1)} %broadcast_in_dim.4), calls=%async_computation | async-start | bytes 409600 | tf_op jit(solution)/shard_map/all_to_all | solution.py:30
  22.4 2.1 %collective-permute-start.6 = (bf16[24,256]{1,0:T(8,128)(2,1)S(1)}, bf16[24,256]{1,0:T(8,128)(2,1)S(1)}, u32[]{:S(2)}, u32[]{:S(2)}) collective-permute-start(bf16[24,256]{1,0:T(8,128)(2,1)S(1)} %broadcast_select_fusion), channel_id=1, source_target_pairs={{0,6},{2,4},{1,7},{3,5},{8,14},{10,12},{9,15},{11,13},{16,22},{18,... | collective-permute-start | bytes 36872 | tf_op jit(solution)/shard_map/ppermute | solution.py:255
  25.3 5.3 %collective-permute-start.7 = (bf16[56,256]{1,0:T(8,128)(2,1)S(1)}, bf16[56,256]{1,0:T(8,128)(2,1)S(1)}, u32[]{:S(2)}, u32[]{:S(2)}) collective-permute-start(bf16[56,256]{1,0:T(8,128)(2,1)S(1)} %pad_maximum_fusion.2.p0), channel_id=1, source_target_pairs={{0,24},{8,0},{16,8},{24,16},{1,25},{9,1},{17,9},{25,17},{2,26},{10... | collective-permute-start | bytes 86024 | tf_op jit(solution)/shard_map/ppermute | solution.py:35
  30.6 1.9 %collective-permute-start.8 = (bf16[56,256]{1,0:T(8,128)(2,1)S(1)}, bf16[56,256]{1,0:T(8,128)(2,1)S(1)}, u32[]{:S(2)}, u32[]{:S(2)}) collective-permute-start(bf16[56,256]{1,0:T(8,128)(2,1)S(1)} %pad_maximum_fusion.2.p0), channel_id=1, source_target_pairs={{0,16},{8,24},{16,0},{24,8},{1,17},{9,25},{17,1},{25,9},{2,18},{10... | collective-permute-start | bytes 86024 | tf_op jit(solution)/shard_map/ppermute | solution.py:35
  32.6 2.2 %collective-permute-start.9 = (bf16[56,256]{1,0:T(8,128)(2,1)S(1)}, bf16[56,256]{1,0:T(8,128)(2,1)S(1)}, u32[]{:S(2)}, u32[]{:S(2)}) collective-permute-start(bf16[56,256]{1,0:T(8,128)(2,1)S(1)} %pad_maximum_fusion.2.p0), channel_id=1, source_target_pairs={{0,8},{8,16},{16,24},{24,0},{1,9},{9,17},{17,25},{25,1},{2,10},{10... | collective-permute-start | bytes 86024 | tf_op jit(solution)/shard_map/ppermute | solution.py:35
  36.1 2.8 %collective-permute-done.9.p3 = bf16[56,256]{1,0:T(8,128)(2,1)S(1)} collective-permute-done((bf16[56,256]{1,0:T(8,128)(2,1)S(1)}, bf16[56,256]{1,0:T(8,128)(2,1)S(1)}, u32[]{:S(2)}, u32[]{:S(2)}) %collective-permute-start.9) | collective-permute-done | bytes 28704 | tf_op jit(solution)/shard_map/ppermute | solution.py:35
  39.6 2.7 %merge_extra.1 = bf16[16,16,3584]{2,1,0:T(8,128)(2,1)} custom-call(s32[3]{0:T(128)} %pad_add_fusion.flag_ref, s32[224,1]{1,0:T(8,128)} %constant.33.clone.device_ref, s32[224,1]{1,0:T(8,128)} %constant.34.clone.row_ref, bf16[56,256]{1,0:T(8,128)(2,1)} %copy-done.11, bf16[56,256]{1,0:T(8,128)(2,1)} %copy-done.13, bf16[56,256]{1,0:T(8,128)(2,1)} %copy-done.14, ...), custom_call_target="tpu_custom_call" | custom-call | tf_op jit(solution)/shard_map/merge_extra/pallas_call | solution.py:269
  42.3 6.8 %all-to-all-start.2 = ((bf16[16,16,3584]{2,1,0:T(8,128)(2,1)}), bf16[16,16,3584]{2,1,0:T(8,128)(2,1)S(1)}, u32[]{:S(2)}, u32[]{:S(2)}) async-start(bf16[16,16,3584]{2,1,0:T(8,128)(2,1)} %merge_extra.1), calls=%async_computation.2 | async-start | bytes 3670016 | tf_op jit(solution)/shard_map/all_to_all | solution.py:278
  51.3 19.7 %all-to-all-done.2.extra_ref = bf16[16,16,3584]{2,1,0:T(8,128)(2,1)S(1)} async-done(((bf16[16,16,3584]{2,1,0:T(8,128)(2,1)}), bf16[16,16,3584]{2,1,0:T(8,128)(2,1)S(1)}, u32[]{:S(2)}, u32[]{:S(2)}) %all-to-all-start.2) | async-done | bytes 1835040 | tf_op jit(solution)/shard_map/all_to_all | solution.py:278
  72.2 6.0 %all-to-all-start.1 = ((bf16[16,160,640]{2,1,0:T(8,128)(2,1)}), bf16[16,160,640]{2,1,0:T(8,128)(2,1)S(1)}, u32[]{:S(2)}, u32[]{:S(2)}) async-start(bf16[16,160,640]{2,1,0:T(8,128)(2,1)} %copy-done.3), calls=%async_computation.1 | async-start | bytes 6553600 | tf_op jit(solution)/shard_map/all_to_all | solution.py:247
  79.7 1.9 %fusion.6.picked_ref = f32[64,1024]{1,0:T(8,128)S(1)} fusion(bf16[64,1280]{1,0:T(8,128)(2,1)} %normed_ref.1, s32[1024]{0:T(1024)} %param.18), kind=kOutput, calls=%fused_computation.10 | convolution fusion | flops 169082880 | bytes 430080 | tf_op jit(solution)/shard_map/dot_general | solution.py:107
  84.1 5.3 %collective-permute-start.10 = (bf16[1280,256]{1,0:T(8,128)(2,1)}, bf16[1280,256]{1,0:T(8,128)(2,1)}, u32[]{:S(2)}, u32[]{:S(2)}) collective-permute-start(bf16[1280,256]{1,0:T(8,128)(2,1)} %solved.1.down0_ref), channel_id=1, source_target_pairs={{0,1},{1,0},{2,3},{3,2},{4,5},{5,4},{6,7},{7,6},{8,9},{9,8},{10,11... | collective-permute-start | bytes 1966088 | tf_op jit(solution)/shard_map/ppermute | solution.py:25
  89.4 25.5 %all-to-all-done.1.plane_ref = bf16[16,160,640]{2,1,0:T(8,128)(2,1)S(1)} async-done(((bf16[16,160,640]{2,1,0:T(8,128)(2,1)}), bf16[16,160,640]{2,1,0:T(8,128)(2,1)S(1)}, u32[]{:S(2)}, u32[]{:S(2)}) %all-to-all-start.1) | async-done | bytes 3276832 | tf_op jit(solution)/shard_map/all_to_all | solution.py:247
  117.4 9.2 %collective-permute-start = (f32[32,1792]{1,0:T(8,128)S(1)}, f32[32,1792]{1,0:T(8,128)S(1)}, u32[]{:S(2)}, u32[]{:S(2)}) collective-permute-start(f32[32,1792]{1,0:T(8,128)S(1)} %get-tuple-element.14), channel_id=1, source_target_pairs={{0,1},{1,0},{2,3},{3,2},{4,5},{5,4},{6,7},{7,6},{8,9},{9,8},{10,11... | collective-permute-start | bytes 688136 | tf_op jit(solution)/shard_map/ppermute | solution.py:25
  126.8 2.3 %convolution_convert_fusion.down_ref = bf16[1280,1024]{1,0:T(8,128)(2,1)S(1)} fusion(bf16[1280,640]{1,0:T(8,128)(2,1)S(1)} %bitcast.22, s32[1024]{0:T(1024)S(1)} %copy-done.18), kind=kOutput, calls=%fused_computation.2 | convolution fusion | flops 1679687680 | bytes 4263936 | tf_op jit(solution)/shard_map/dot_general | solution.py:107
  129.2 7.0 %collective-permute-start.1 = (bf16[32,1792]{1,0:T(8,128)(2,1)S(1)}, bf16[32,1792]{1,0:T(8,128)(2,1)S(1)}, u32[]{:S(2)}, u32[]{:S(2)}) collective-permute-start(bf16[32,1792]{1,0:T(8,128)(2,1)S(1)} %get-tuple-element.19), channel_id=1, source_target_pairs={{0,2},{2,0},{4,6},{6,4},{1,3},{3,1},{5,7},{7,5},{8,10},{10,8},{12,... | collective-permute-start | bytes 344072 | tf_op jit(solution)/shard_map/ppermute | solution.py:299
  136.2 10.5 %collective-permute-done.1 = bf16[32,1792]{1,0:T(8,128)(2,1)S(1)} collective-permute-done((bf16[32,1792]{1,0:T(8,128)(2,1)S(1)}, bf16[32,1792]{1,0:T(8,128)(2,1)S(1)}, u32[]{:S(2)}, u32[]{:S(2)}) %collective-permute-start.1) | collective-permute-done | bytes 114720 | tf_op jit(solution)/shard_map/ppermute | solution.py:299
  146.8 4.9 %collective-permute-start.2 = (bf16[32,1792]{1,0:T(8,128)(2,1)S(1)}, bf16[32,1792]{1,0:T(8,128)(2,1)S(1)}, u32[]{:S(2)}, u32[]{:S(2)}) collective-permute-start(bf16[32,1792]{1,0:T(8,128)(2,1)S(1)} %fusion.18), channel_id=1, source_target_pairs={{0,6},{2,4},{4,2},{6,0},{1,7},{3,5},{5,3},{7,1},{8,14},{10,12},{12... | collective-permute-start | bytes 344072 | tf_op jit(solution)/shard_map/ppermute | solution.py:301
  152.3 8.8 %collective-permute-done.2 = bf16[32,1792]{1,0:T(8,128)(2,1)S(1)} collective-permute-done((bf16[32,1792]{1,0:T(8,128)(2,1)S(1)}, bf16[32,1792]{1,0:T(8,128)(2,1)S(1)}, u32[]{:S(2)}, u32[]{:S(2)}) %collective-permute-start.2) | collective-permute-done | bytes 114720 | tf_op jit(solution)/shard_map/ppermute | solution.py:301
  161.3 2.6 %collective-permute-start.3 = (f32[32,1792]{1,0:T(8,128)S(1)}, f32[32,1792]{1,0:T(8,128)S(1)}, u32[]{:S(2)}, u32[]{:S(2)}) collective-permute-start(f32[32,1792]{1,0:T(8,128)S(1)} %fusion.13.mine_ref), channel_id=1, source_target_pairs={{0,1},{1,0},{2,3},{3,2},{4,5},{5,4},{6,7},{7,6},{8,9},{9,8},{10,11... | collective-permute-start | bytes 688136 | tf_op jit(solution)/shard_map/ppermute | solution.py:25
  165.0 2.4 %middle.1 = (f32[64,1]{1,0:T(8,128)S(1)}, f32[64,16]{1,0:T(8,128)S(1)}, f32[80,1024]{1,0:T(8,128)S(1)}, f32[2,144,256]{2,1,0:T(8,128)S(1)}) custom-call(s32[3]{0:T(128)S(1)} %copy-done.7, f32[32,1792]{1,0:T(8,128)S(1)} %fusion.13.mine_ref, f32[32,1792]{1,0:T(8,128)S(1)} %collective-permute-done.3.theirs_ref, bf16[64,1280]{1,0:T(8,128)(2,1)S(1)} %copy-done.4, ...), custom_call_target="tpu_custom_call" | custom-call | tf_op jit(solution)/shard_map/middle/pallas_call | solution.py:323
  167.5 4.1 %last.1 = bf16[64,16,1024]{2,1,0:T(8,128)(2,1)} custom-call(s32[3]{0:T(128)S(1)} %copy-done.7, f32[64,1024]{1,0:T(8,128)S(1)} %fusion.10.gain_ref, f32[64,1]{1,0:T(8,128)S(1)} %get-tuple-element.15.inv_ref, f32[64,16]{1,0:T(8,128)S(1)} %get-tuple-element.16.share_ref, f32[80,1024]{1,0:T(8,128)S(1)} %get-tuple-element.17.own_ref, ...), custom_call_target="tpu_custom_call" | custom-call | tf_op jit(solution)/shard_map/last/pallas_call | solution.py:336
  (78 shorter events, 20.0 us)
Async XLA Ops:
  2.5 8.8 %collective-permute-start.4 = (bf16[24,256]{1,0:T(8,128)(2,1)S(1)}, bf16[24,256]{1,0:T(8,128)(2,1)S(1)}, u32[]{:S(2)}, u32[]{:S(2)}) collective-permute-start(bf16[24,256]{1,0:T(8,128)(2,1)S(1)} %pad_maximum_fusion.3), channel_id=1, source_target_pairs={{0,1},{2,3},{4,5},{6,7},{8,9},{10,11},{12,13},{14,15},{16,17},{18,... | collective-permute-start | bytes 36872 | tf_op jit(solution)/shard_map/ppermute | solution.py:253
  11.3 11.0 %collective-permute-start.5 = (bf16[24,256]{1,0:T(8,128)(2,1)S(1)}, bf16[24,256]{1,0:T(8,128)(2,1)S(1)}, u32[]{:S(2)}, u32[]{:S(2)}) collective-permute-start(bf16[24,256]{1,0:T(8,128)(2,1)S(1)} %fusion.23), channel_id=1, source_target_pairs={{0,2},{1,3},{8,10},{9,11},{16,18},{17,19},{24,26},{25,27},{32,34},... | collective-permute-start | bytes 36872 | tf_op jit(solution)/shard_map/ppermute | solution.py:254
  16.7 25.5 %all-to-all-start = ((bf16[4,40,640]{2,1,0:T(8,128)(2,1)}), bf16[4,40,640]{2,1,0:T(8,128)(2,1)S(1)}, u32[]{:S(2)}, u32[]{:S(2)}) async-start(bf16[4,40,640]{2,1,0:T(8,128)(2,1)} %broadcast_in_dim.4), calls=%async_computation | async-start | bytes 409600 | tf_op jit(solution)/shard_map/all_to_all | solution.py:30
  22.4 2.9 %collective-permute-start.6 = (bf16[24,256]{1,0:T(8,128)(2,1)S(1)}, bf16[24,256]{1,0:T(8,128)(2,1)S(1)}, u32[]{:S(2)}, u32[]{:S(2)}) collective-permute-start(bf16[24,256]{1,0:T(8,128)(2,1)S(1)} %broadcast_select_fusion), channel_id=1, source_target_pairs={{0,6},{2,4},{1,7},{3,5},{8,14},{10,12},{9,15},{11,13},{16,22},{18,... | collective-permute-start | bytes 36872 | tf_op jit(solution)/shard_map/ppermute | solution.py:255
  25.3 13.7 %copy-start.11 = (bf16[56,256]{1,0:T(8,128)(2,1)}, bf16[56,256]{1,0:T(8,128)(2,1)S(1)}, u32[]{:S(2)}) copy-start(bf16[56,256]{1,0:T(8,128)(2,1)S(1)} %pad_maximum_fusion.2.p0) | copy-start | bytes 86020
  25.3 10.2 %collective-permute-start.7 = (bf16[56,256]{1,0:T(8,128)(2,1)S(1)}, bf16[56,256]{1,0:T(8,128)(2,1)S(1)}, u32[]{:S(2)}, u32[]{:S(2)}) collective-permute-start(bf16[56,256]{1,0:T(8,128)(2,1)S(1)} %pad_maximum_fusion.2.p0), channel_id=1, source_target_pairs={{0,24},{8,0},{16,8},{24,16},{1,25},{9,1},{17,9},{25,17},{2,26},{10... | collective-permute-start | bytes 86024 | tf_op jit(solution)/shard_map/ppermute | solution.py:35
  30.6 5.5 %collective-permute-start.8 = (bf16[56,256]{1,0:T(8,128)(2,1)S(1)}, bf16[56,256]{1,0:T(8,128)(2,1)S(1)}, u32[]{:S(2)}, u32[]{:S(2)}) collective-permute-start(bf16[56,256]{1,0:T(8,128)(2,1)S(1)} %pad_maximum_fusion.2.p0), channel_id=1, source_target_pairs={{0,16},{8,24},{16,0},{24,8},{1,17},{9,25},{17,1},{25,9},{2,18},{10... | collective-permute-start | bytes 86024 | tf_op jit(solution)/shard_map/ppermute | solution.py:35
  32.6 6.4 %collective-permute-start.9 = (bf16[56,256]{1,0:T(8,128)(2,1)S(1)}, bf16[56,256]{1,0:T(8,128)(2,1)S(1)}, u32[]{:S(2)}, u32[]{:S(2)}) collective-permute-start(bf16[56,256]{1,0:T(8,128)(2,1)S(1)} %pad_maximum_fusion.2.p0), channel_id=1, source_target_pairs={{0,8},{8,16},{16,24},{24,0},{1,9},{9,17},{17,25},{25,1},{2,10},{10... | collective-permute-start | bytes 86024 | tf_op jit(solution)/shard_map/ppermute | solution.py:35
  42.3 28.7 %all-to-all-start.2 = ((bf16[16,16,3584]{2,1,0:T(8,128)(2,1)}), bf16[16,16,3584]{2,1,0:T(8,128)(2,1)S(1)}, u32[]{:S(2)}, u32[]{:S(2)}) async-start(bf16[16,16,3584]{2,1,0:T(8,128)(2,1)} %merge_extra.1), calls=%async_computation.2 | async-start | bytes 3670016 | tf_op jit(solution)/shard_map/all_to_all | solution.py:278
  51.3 27.6 %copy-start.9 = (bf16[1280,16]{0,1:T(8,128)(2,1)S(1)}, bf16[1280,16]{0,1:T(8,128)(2,1)}, u32[]{:S(2)}) copy-start(bf16[1280,16]{0,1:T(8,128)(2,1)} %param.17) | copy-start | bytes 122884
  51.3 27.6 %copy-start.12 = (f32[1280]{0:T(1024)S(1)}, f32[1280]{0:T(1024)}, u32[]{:S(2)}) copy-start(f32[1280]{0:T(1024)} %param.16) | copy-start | bytes 15364
  72.2 6.7 %copy-start.10 = (bf16[1280,16]{0,1:T(8,128)(2,1)S(1)}, bf16[1280,16]{0,1:T(8,128)(2,1)}, u32[]{:S(2)}) copy-start(bf16[1280,16]{0,1:T(8,128)(2,1)} %param.17) | copy-start | bytes 122884
  72.2 42.7 %all-to-all-start.1 = ((bf16[16,160,640]{2,1,0:T(8,128)(2,1)}), bf16[16,160,640]{2,1,0:T(8,128)(2,1)S(1)}, u32[]{:S(2)}, u32[]{:S(2)}) async-start(bf16[16,160,640]{2,1,0:T(8,128)(2,1)} %copy-done.3), calls=%async_computation.1 | async-start | bytes 6553600 | tf_op jit(solution)/shard_map/all_to_all | solution.py:247
  78.2 36.7 %copy-start.7 = (s32[3]{0:T(128)S(1)}, s32[3]{0:T(128)}, u32[]{:S(2)}) copy-start(s32[3]{0:T(128)} %pad_add_fusion.flag_ref) | copy-start | bytes 40
  84.1 79.9 %collective-permute-start.10 = (bf16[1280,256]{1,0:T(8,128)(2,1)}, bf16[1280,256]{1,0:T(8,128)(2,1)}, u32[]{:S(2)}, u32[]{:S(2)}) collective-permute-start(bf16[1280,256]{1,0:T(8,128)(2,1)} %solved.1.down0_ref), channel_id=1, source_target_pairs={{0,1},{1,0},{2,3},{3,2},{4,5},{5,4},{6,7},{7,6},{8,9},{9,8},{10,11... | collective-permute-start | bytes 1966088 | tf_op jit(solution)/shard_map/ppermute | solution.py:25
  115.9 11.0 %copy-start.18 = (s32[1024]{0:T(1024)S(1)}, s32[1024]{0:T(1024)}, u32[]{:S(2)}) copy-start(s32[1024]{0:T(1024)} %copy-done.17) | copy-start | bytes 12292
  117.4 11.7 %collective-permute-start = (f32[32,1792]{1,0:T(8,128)S(1)}, f32[32,1792]{1,0:T(8,128)S(1)}, u32[]{:S(2)}, u32[]{:S(2)}) collective-permute-start(f32[32,1792]{1,0:T(8,128)S(1)} %get-tuple-element.14), channel_id=1, source_target_pairs={{0,1},{1,0},{2,3},{3,2},{4,5},{5,4},{6,7},{7,6},{8,9},{9,8},{10,11... | collective-permute-start | bytes 688136 | tf_op jit(solution)/shard_map/ppermute | solution.py:25
  126.8 19.9 %copy-start.16 = (pred[1792]{0:T(1024)(128)(4,1)S(1)}, pred[1792]{0:T(1024)(128)(4,1)}, u32[]{:S(2)}) copy-start(pred[1792]{0:T(1024)(128)(4,1)} %iota_compare_fusion.13) | copy-start | bytes 5380
  129.1 32.1 %copy-start.8 = (bf16[32,1280]{1,0:T(8,128)(2,1)S(1)}, bf16[32,1280]{1,0:T(8,128)(2,1)}, u32[]{:S(2)}) copy-start(bf16[32,1280]{1,0:T(8,128)(2,1)} %slice_select_fusion) | copy-start | bytes 245764
  129.1 35.9 %copy-start.4 = (bf16[64,1280]{1,0:T(8,128)(2,1)S(1)}, bf16[64,1280]{1,0:T(8,128)(2,1)}, u32[]{:S(2)}) copy-start(bf16[64,1280]{1,0:T(8,128)(2,1)} %pad_maximum_fusion.head_ref) | copy-start | bytes 491524
  129.2 17.5 %collective-permute-start.1 = (bf16[32,1792]{1,0:T(8,128)(2,1)S(1)}, bf16[32,1792]{1,0:T(8,128)(2,1)S(1)}, u32[]{:S(2)}, u32[]{:S(2)}) collective-permute-start(bf16[32,1792]{1,0:T(8,128)(2,1)S(1)} %get-tuple-element.19), channel_id=1, source_target_pairs={{0,2},{2,0},{4,6},{6,4},{1,3},{3,1},{5,7},{7,5},{8,10},{10,8},{12,... | collective-permute-start | bytes 344072 | tf_op jit(solution)/shard_map/ppermute | solution.py:299
  146.8 14.4 %collective-permute-start.2 = (bf16[32,1792]{1,0:T(8,128)(2,1)S(1)}, bf16[32,1792]{1,0:T(8,128)(2,1)S(1)}, u32[]{:S(2)}, u32[]{:S(2)}) collective-permute-start(bf16[32,1792]{1,0:T(8,128)(2,1)S(1)} %fusion.18), channel_id=1, source_target_pairs={{0,6},{2,4},{4,2},{6,0},{1,7},{3,5},{5,3},{7,1},{8,14},{10,12},{12... | collective-permute-start | bytes 344072 | tf_op jit(solution)/shard_map/ppermute | solution.py:301
  161.2 6.2 %copy-start.2 = (bf16[16,16,3584]{2,1,0:T(8,128)(2,1)S(1)}, bf16[16,16,3584]{2,1,0:T(8,128)(2,1)}, u32[]{:S(2)}) copy-start(bf16[16,16,3584]{2,1,0:T(8,128)(2,1)} %copy-done) | copy-start | bytes 5505028
  161.3 3.7 %collective-permute-start.3 = (f32[32,1792]{1,0:T(8,128)S(1)}, f32[32,1792]{1,0:T(8,128)S(1)}, u32[]{:S(2)}, u32[]{:S(2)}) collective-permute-start(f32[32,1792]{1,0:T(8,128)S(1)} %fusion.13.mine_ref), channel_id=1, source_target_pairs={{0,1},{1,0},{2,3},{3,2},{4,5},{5,4},{6,7},{7,6},{8,9},{9,8},{10,11... | collective-permute-start | bytes 688136 | tf_op jit(solution)/shard_map/ppermute | solution.py:25
  (9 other events, 22.7 us)
